TPU v7x, 256 devices: a whole 4x4x8 slice. The times are simulated.
256 devices in a mesh: tm: 16 (over z, core), space: 16 (over x, y).
Axes of the slice: x: 4, y: 4, z: 8, core: 2. Of those that a mesh axis runs over, the one named last changes fastest.
Arguments:
- features: bfloat16 [64, 256, 128, 128], P('tm', 'space'), may hold values from -6 to 6
- kernel_first: bfloat16 [3, 3, 3, 128, 128], replicated, may hold values from -0.109375 to 0.109375
- bias_first: float32 [128], replicated, may hold values from -3 to 3
- kernel_down: bfloat16 [3, 3, 128, 256], replicated, may hold values from -0.1875 to 0.1875
- bias_down: float32 [256], replicated, may hold values from -3 to 3
- kernel_second: bfloat16 [3, 3, 3, 256, 256], replicated, may hold values from -0.078125 to 0.078125
- bias_second: float32 [256], replicated, may hold values from -3 to 3
Outputs:
- latent: bfloat16 [64, 128, 64, 256], P('tm', 'space')
All inputs are finite; a program needn't handle non-finite values.
Results may differ from a plain program's by a relative error of at most 0.0095.
Values may be sent and summed in bfloat16 or wider, within the bound.
No kernel may reach another device: no remote copies, remote signals or barrier semaphores. Data moves between devices by JAX's collectives and lax.ppermute only.
A program may use at most 64 MiB of HBM per device.

v0:
```python
import jax
import jax.numpy as jnp
from jax import lax
from jax.experimental import pallas as pl
from jax.experimental.pallas import tpu as pltpu
from jax.sharding import PartitionSpec as P

BF = jnp.bfloat16
F32 = jnp.float32
VMEM = pltpu.VMEM
LIMIT = 24 * 2**20


def silu(v):
    h = 0.5 * v
    return h + h * jnp.tanh(h)


def clear_edges(s_ref):
    for f in range(s_ref.shape[0]):
        for e in range(2):
            s_ref[f, e, 0:8] = jnp.zeros((8, s_ref.shape[-1]), F32)
            s_ref[f, e, s_ref.shape[2] - 8 :] = jnp.zeros((8, s_ref.shape[-1]), F32)


def prep_first(x, f, r, u_ref, x2_ref, s_ref, q_ref, residual=True):
    q_ref[f] = x.astype(F32)
    even = q_ref[f, pl.ds(0, 64, stride=2), :]
    odd = q_ref[f, pl.ds(1, 64, stride=2), :]
    d1 = silu(even)
    d2 = silu(odd)
    s_ref[f, 0, 8:72] = d1
    s_ref[f, 1, 8:72] = d2
    d3 = s_ref[f, 0, 9:73]
    d0 = s_ref[f, 1, 7:71]
    lanes = slice((f % 2) * 128, (f % 2) * 128 + 128)
    for k, v in enumerate((d0 - d2, d1 + d2, d2 - d1, d1 - d3)):
        u_ref[k, f // 2, r + 1, :, lanes] = v.astype(BF)
    if residual:
        x2_ref[f, r, :, 0:128] = even.astype(BF)
        x2_ref[f, r, :, 128:256] = odd.astype(BF)


def transformed(g0, g1, g2):
    half = 0.5 * (g0 + g2)
    return half + 0.5 * g1, half - 0.5 * g1


def first_rows(u_ref, w_ref, f_ref, o_ref, pairs, g0, rows, below, residual, bias):
    ms = []
    for k in range(4):
        lhs = jnp.concatenate(
            [u_ref[k, p, g0 + j : g0 + j + rows].reshape(rows * 64, 256) for j in range(3) for p, _ in pairs], axis=1
        )
        rhs = jnp.concatenate([w_ref[k, j, which] for j in range(3) for _, which in pairs], axis=0)
        ms.append(jnp.dot(lhs, rhs, preferred_element_type=F32))
    both = (ms[1] + ms[2] + ms[0], ms[1] - ms[2] - ms[3])
    for q in range(2):
        for e in range(2):
            lanes = slice(e * 128, e * 128 + 128)
            y = both[e][:, q * 128 : q * 128 + 128].reshape(rows, 64, 128)
            if residual is not None:
                y = y + residual[q, g0 : g0 + rows, :, lanes].astype(F32) + bias
            for n in range(rows):
                g = g0 + n
                at = (g % 2, (g + 1) // 2)
                row = y[n] * below if g >= 16 else y[n]
                f_ref[q, at[0], at[1], :, lanes] = row.astype(BF)
                if e == 1:
                    o_ref[q, n, 8:72] = row
                    f_ref[q, at[0], at[1], :, 256:384] = o_ref[q, n, 7:71].astype(BF)


def clear_shift(o_ref):
    for q in range(2):
        for n in range(o_ref.shape[1]):
            o_ref[q, n, 0:8] = jnp.zeros((8, 128), F32)


def down_conv(f_ref, kd_ref):
    rhs = jnp.concatenate([kd_ref[j, c] for j in range(3) for c in (1, 2, 0)], axis=0)
    out = []
    for q in range(2):
        lhs = jnp.concatenate(
            [
                f_ref[q, 1, 0:9].reshape(576, 384),
                f_ref[q, 0, 0:9].reshape(576, 384),
                f_ref[q, 1, 1:10].reshape(576, 384),
            ],
            axis=1,
        )
        out.append(jnp.dot(lhs, rhs, preferred_element_type=F32))
    return out


PAIR01 = ((0, 1),)
PAIR23 = ((0, 0), (1, 1))
PAIR45 = ((1, 0),)


def kernel_own(
    x_hbm, kf_hbm, ks_hbm, bf_ref, u_ref, x2_ref, w_ref, ks_ref, f45_ref, f23_ref, x_ref, kf_ref, s_ref, q_ref, o_ref, sem
):
    xs = [pltpu.make_async_copy(x_hbm.at[:, n * 4 : n * 4 + 4], x_ref.at[:, n * 4 : n * 4 + 4], sem.at[n]) for n in range(4)]
    first = pltpu.make_async_copy(kf_hbm, kf_ref, sem.at[4])
    second = pltpu.make_async_copy(ks_hbm, ks_ref, sem.at[5])
    xs[0].start()
    first.start()
    for c in xs[1:]:
        c.start()
    second.start()
    clear_edges(s_ref)
    clear_shift(o_ref)
    for k in range(4):
        for p in range(2):
            u_ref[k, p, 0] = jnp.zeros((64, 256), BF)
    for q in range(2):
        f45_ref[q, 1, 0] = jnp.zeros((64, 384), BF)
        f23_ref[q, 1, 0] = jnp.zeros((64, 384), BF)

    def row(r, carry):
        for f in range(4):
            prep_first(x_ref[f, r], f, r, u_ref, x2_ref, s_ref, q_ref)
        return carry

    for n in range(4):
        xs[n].wait()
        lax.fori_loop(n * 4, n * 4 + 4, row, 0)

    first.wait()

    def wrow(j, carry):
        zero = jnp.zeros((128, 128), BF)
        for i in range(3):
            g0, g1, g2 = (kf_ref[i, j, c] for c in range(3))
            a, b = transformed(g0.astype(F32), g1.astype(F32), g2.astype(F32))
            for k, g in enumerate((g0, a.astype(BF), b.astype(BF), g2)):
                if i == 0:
                    w_ref[k, j, 0, 0:128, 0:128] = g
                    w_ref[k, j, 0, 128:256, 128:256] = g
                    w_ref[k, j, 0, 0:128, 128:256] = zero
                    w_ref[k, j, 1, 128:256, 0:128] = zero
                elif i == 1:
                    w_ref[k, j, 0, 128:256, 0:128] = g
                    w_ref[k, j, 1, 0:128, 128:256] = g
                else:
                    w_ref[k, j, 1, 0:128, 0:128] = g
                    w_ref[k, j, 1, 128:256, 128:256] = g
        return carry

    lax.fori_loop(0, 3, wrow, 0)
    for g0, rows in ((0, 8), (8, 7)):
        first_rows(u_ref, w_ref, f45_ref, o_ref, PAIR45, g0, rows, None, None, None)
    for g0, rows in ((0, 8), (8, 7)):
        first_rows(u_ref, w_ref, f23_ref, o_ref, PAIR23, g0, rows, None, x2_ref.at[2:4], bf_ref[...])
    second.wait()


def kernel_ahead(ok_ref, u_in, x2_in, f_in, halo_ref, w_ref, kd_ref, u_ref, x2_ref, f_ref, part_ref, s_ref, q_ref, o_ref):
    clear_edges(s_ref)
    clear_shift(o_ref)
    for n in range(3):
        for f in range(4):
            prep_first(halo_ref[f, n], f, 16 + n, u_ref, x2_ref, s_ref, q_ref, n < 2)
    below = ok_ref[1].astype(F32)
    first_rows(u_ref, w_ref, f_ref, o_ref, PAIR45, 15, 3, below, None, None)
    out = down_conv(f_ref, kd_ref)
    for q in range(2):
        part_ref[q] = out[q].reshape(9, 64, 256).astype(BF)


def kernel_late(
    ok_ref, u_ref, x2_ref, f_in, w_ref, kd_ref, bf_ref, bd_ref, f_ref, red_ref, act_ref, edge_ref, o_ref
):
    clear_shift(o_ref)
    below = ok_ref[1].astype(F32)
    first_rows(u_ref, w_ref, f_ref, o_ref, PAIR23, 15, 3, below, x2_ref.at[2:4], bf_ref[...])
    out = down_conv(f_ref, kd_ref)
    for q in range(2):
        r16 = (out[q] + bd_ref[...]).astype(BF).reshape(9, 64, 256)
        red_ref[q] = r16
        act_ref[q] = silu(r16.astype(F32)).astype(BF)
        act_ref[q, 8] = (silu(r16[8].astype(F32)) * below).astype(BF)
        edge_ref[q, 0] = act_ref[q, 7]
        edge_ref[q, 1] = act_ref[q, 8]


def kernel_early(ok_ref, u_ref, x2_ref, w_ref, kd_ref, bf_ref, bd_ref, z_ref, red23_ref, red_ref, dn_ref, f_ref, o_ref):
    clear_shift(o_ref)
    below = ok_ref[1].astype(F32)
    for q in range(2):
        f_ref[q, 1, 0] = jnp.zeros((64, 384), BF)
    for g0 in (0, 9):
        first_rows(u_ref, w_ref, f_ref, o_ref, PAIR01, g0, 9, below, x2_ref.at[0:2], bf_ref[...])
    out = down_conv(f_ref, kd_ref)
    for q in range(2):
        red_ref[q] = (out[q] + bd_ref[...] + z_ref[q].reshape(576, 256).astype(F32)).astype(BF).reshape(9, 64, 256)
        for n in range(2):
            dn_ref[q, n] = red_ref[q, 7 + n]
            dn_ref[2 + q, n] = red23_ref[q, 7 + n]


def prep_mid(act, f, to, u_ref, s_ref, q_ref):
    q_ref[f, 0] = act[:, 0:128]
    q_ref[f, 1] = act[:, 128:256]
    d1 = jnp.concatenate([q_ref[f, h, pl.ds(0, 32, stride=2), :] for h in range(2)], axis=1)
    d2 = jnp.concatenate([q_ref[f, h, pl.ds(1, 32, stride=2), :] for h in range(2)], axis=1)
    s_ref[f, 0, 8:40] = d1
    s_ref[f, 1, 8:40] = d2
    d3 = s_ref[f, 0, 9:41]
    d0 = s_ref[f, 1, 7:39]
    for k, v in enumerate((d0 - d2, d1 + d2, d2 - d1, d1 - d3)):
        u_ref[(k, *to)] = v.astype(BF)


def kernel_mid(ok_ref, red01_ref, red23_ref, ks_ref, u_ref, g_ref, s_ref, q_ref):
    clear_edges(s_ref)

    def row(r, carry):
        scale = jnp.where(r == 8, ok_ref[1], 1).astype(F32)
        for f in range(4):
            v = (red01_ref, red23_ref)[f // 2][f % 2, r].astype(F32)
            prep_mid(silu(v) * scale, f, (f, r + 1), u_ref, s_ref, q_ref)
        return carry

    lax.fori_loop(1, 9, row, 0)

    def grow(i, carry):
        for j in range(3):
            a, b = transformed(*(ks_ref[i, j, c].astype(F32) for c in range(3)))
            g_ref[0, i, j] = a.astype(BF)
            g_ref[1, i, j] = b.astype(BF)
        return carry

    lax.fori_loop(0, 3, grow, 0)


def second_conv(slab, ks_ref, g_ref, red, bias, t_ref, out_ref):
    ms = []
    for k in range(4):
        lhs = jnp.concatenate([slab(k, i, j) for i in range(3) for j in range(3)], axis=1)
        if k == 0 or k == 3:
            rhs = jnp.concatenate([ks_ref[i, j, 2 * (k // 3)] for i in range(3) for j in range(3)], axis=0)
        else:
            rhs = g_ref[k - 1].reshape(2304, 256)
        ms.append(jnp.dot(lhs, rhs, preferred_element_type=F32))
    y0 = (ms[1] + ms[2] + ms[0]).reshape(16, 32, 256)
    y1 = (ms[1] - ms[2] - ms[3]).reshape(16, 32, 256)
    for n in range(16):
        for h in range(2):
            lanes = slice(h * 128, h * 128 + 128)
            t_ref[n, h, pl.ds(0, 32, stride=2), :] = y0[n, :, lanes]
            t_ref[n, h, pl.ds(1, 32, stride=2), :] = y1[n, :, lanes]
            v = t_ref[n, h] + red(n // 8, n % 8, lanes) + bias[:, lanes]
            out_ref[n // 8, n % 8, :, lanes] = v.astype(BF)


def kernel_mid_late(
    ok_ref, u_in, halo_ref, red01_ref, ks_ref, g_ref, red_ref, bs_ref, lat_ref, u_ref, s_ref, q_ref, t_ref, out_ref, sem
):
    clear_edges(s_ref)
    inner = ok_ref[0] > 0
    for f in range(4):
        own = (red01_ref, red_ref)[f // 2][f % 2, 0].astype(F32)
        above = jnp.where(inner, halo_ref[f, 1].astype(F32), own)
        prep_mid(silu(halo_ref[f, 0].astype(F32)), f, (f, 0), u_ref, s_ref, q_ref)
        prep_mid(silu(above), f, (f, 1), u_ref, s_ref, q_ref)

    def red(f, r, lanes):
        v = red_ref[f, r, :, lanes].astype(F32)
        return jnp.where(inner, halo_ref[2 + f, 1, :, lanes].astype(F32), v) if r == 0 else v

    def slab(k, i, j):
        return u_ref[k, i : i + 2, j : j + 8].reshape(512, 256)

    second_conv(slab, ks_ref, g_ref, red, bs_ref[...], t_ref, out_ref)
    copy = pltpu.make_async_copy(out_ref, lat_ref.at[2:4], sem)
    copy.start()
    copy.wait()


def kernel_mid_early(
    ok_ref, lat_in, u_ref, zact_ref, zedge_ref, halo_ref, ks_ref, g_ref, red_ref, bs_ref, lat_ref, v_ref, s_ref, q_ref, t_ref, out_ref, sem
):
    clear_edges(s_ref)
    inner = ok_ref[0] > 0

    def row(r, carry):
        for f in range(2):
            prep_mid(zact_ref[f, r].astype(F32), f, (f, r + 1), v_ref, s_ref, q_ref)
        return carry

    lax.fori_loop(1, 9, row, 0)
    for f in range(2):
        above = jnp.where(inner, zedge_ref[f, 1].astype(F32), zact_ref[f, 0].astype(F32))
        prep_mid(zedge_ref[f, 0].astype(F32), f, (f, 0), v_ref, s_ref, q_ref)
        prep_mid(above, f, (f, 1), v_ref, s_ref, q_ref)

    def red(f, r, lanes):
        v = red_ref[f, r, :, lanes].astype(F32)
        return jnp.where(inner, halo_ref[f, 1, :, lanes].astype(F32), v) if r == 0 else v

    def slab(k, i, j):
        if i == 0:
            return v_ref[k, :, j : j + 8].reshape(512, 256)
        if i == 2:
            return u_ref[k, 0:2, j : j + 8].reshape(512, 256)
        return jnp.concatenate(
            [v_ref[k, 1, j : j + 8].reshape(256, 256), u_ref[k, 0, j : j + 8].reshape(256, 256)], axis=0
        )

    second_conv(slab, ks_ref, g_ref, red, bs_ref[...], t_ref, out_ref)
    copy = pltpu.make_async_copy(out_ref, lat_ref.at[0:2], sem)
    copy.start()
    copy.wait()


V = pl.BlockSpec(memory_space=pltpu.VMEM)
ANY = pl.BlockSpec(memory_space=pl.ANY)
HBM = pl.BlockSpec(memory_space=pltpu.HBM)
SM = pl.BlockSpec(memory_space=pltpu.SMEM)


def sds(*shape):
    return jax.ShapeDtypeStruct(shape, BF)


def res(*shape):
    return VMEM(shape, BF)


def keep(*xs):
    return [pltpu.with_memory_space_constraint(x, pltpu.VMEM) for x in xs]


def call(body, name, ins, outs, scratch, flops, in_specs=None, out_specs=None, aliases=None):
    return pl.pallas_call(
        body,
        out_shape=outs,
        in_specs=in_specs or [V] * len(ins),
        out_specs=out_specs or [V] * len(outs),
        scratch_shapes=scratch,
        input_output_aliases=aliases or {},
        compiler_params=pltpu.CompilerParams(vmem_limit_bytes=LIMIT),
        cost_estimate=pl.CostEstimate(flops=flops, bytes_accessed=4 << 20, transcendentals=0),
        name=name,
    )(*ins)


def on_device(features, kf, bf, kd, bd, ks, bs):
    tm, sp = lax.axis_size("tm"), lax.axis_size("space")
    down = [(i, i + 1) for i in range(sp - 1)]
    up = [(i + 1, i) for i in range(sp - 1)]
    later = [(i, i + 1) for i in range(tm - 1)]
    cross = [(t * sp + s, (t + 1) * sp + s + 1) for t in range(tm - 1) for s in range(sp - 1)]
    at = lax.axis_index("space")
    ok = jnp.stack([(at > 0).astype(jnp.int32), (at < sp - 1).astype(jnp.int32)])
    bf2, bd2, bs2 = bf.reshape(1, 128), bd.reshape(1, 256), bs.reshape(1, 256)

    halo = lax.ppermute(features[:, 0:3], "space", up)
    wide = [VMEM((4, 2, 80, 128), F32), VMEM((4, 128, 128), F32)]
    shift = lambda n: VMEM((2, n, 72, 128), F32)
    fshape = (2, 2, 10, 64, 384)
    u, x2, w, ksv, f45, f23 = call(
        kernel_own, "own", (*[pltpu.with_memory_space_constraint(v, pltpu.HBM) for v in (features, kf, ks)], bf2),
        [res(4, 2, 20, 64, 256), res(4, 18, 64, 256), res(4, 3, 2, 256, 256), res(3, 3, 3, 256, 256), res(*fshape), res(*fshape)],
        [VMEM((4, 16, 128, 128), BF), VMEM((3, 3, 3, 128, 128), BF), *wide, shift(8), pltpu.SemaphoreType.DMA((6,))],
        6_000_000_000, in_specs=[HBM, HBM, HBM, V],
    )
    u, x2, _, part = call(
        kernel_ahead, "ahead", (ok, *keep(u, x2, f45), halo, *keep(w), kd),
        [res(4, 2, 20, 64, 256), res(4, 18, 64, 256), res(*fshape), sds(2, 9, 64, 256)],
        [*wide, shift(3)], 2_000_000_000, in_specs=[SM] + [V] * 6, aliases={1: 0, 2: 1, 3: 2},
    )
    zpart = lax.ppermute(part, "tm", later)
    _, red23, act23, edge23 = call(
        kernel_late, "late", (ok, *keep(u, x2, f23, w), kd, bf2, bd2),
        [res(*fshape), res(2, 9, 64, 256), sds(2, 9, 64, 256), sds(2, 2, 64, 256)],
        [shift(3)], 2_500_000_000, in_specs=[SM] + [V] * 7, aliases={3: 0},
    )
    zact = lax.ppermute(act23, "tm", later)
    zedge = lax.ppermute(edge23, ("tm", "space"), cross)
    red01, dn = call(
        kernel_early, "early", (ok, *keep(u, x2, w), kd, bf2, bd2, zpart, *keep(red23)),
        [res(2, 9, 64, 256), sds(4, 2, 64, 256)],
        [VMEM(fshape, BF), shift(9)], 3_000_000_000, in_specs=[SM] + [V] * 8,
    )
    halo_mid = lax.ppermute(dn, "space", down)
    half = lambda n: [VMEM((n, 2, 48, 256), F32), VMEM((n, 2, 64, 128), F32)]
    tail = [VMEM((16, 2, 64, 128), F32), VMEM((2, 8, 64, 256), BF), pltpu.SemaphoreType.DMA]
    u2, g = call(
        kernel_mid, "mid", (ok, *keep(red01, red23, ksv)),
        [res(4, 4, 10, 32, 256), res(2, 3, 3, 256, 256)], half(4), 1_500_000_000, in_specs=[SM] + [V] * 3,
    )
    lat, u2 = call(
        kernel_mid_late, "mid_late", (ok, *keep(u2), halo_mid, *keep(red01, ksv, g, red23), bs2),
        [sds(4, 8, 64, 256), res(4, 4, 10, 32, 256)],
        half(4) + tail, 3_000_000_000, in_specs=[SM] + [V] * 7, out_specs=[ANY, V], aliases={1: 1},
    )
    (lat,) = call(
        kernel_mid_early, "mid_early", (ok, lat, *keep(u2), zact, zedge, halo_mid, *keep(ksv, g, red01), bs2),
        [sds(4, 8, 64, 256)],
        [VMEM((4, 2, 10, 32, 256), BF)] + half(2) + tail,
        3_000_000_000, in_specs=[SM, ANY] + [V] * 8, out_specs=[ANY], aliases={1: 0},
    )
    return lat


def solution(mesh):
    in_specs = (P("tm", "space", None, None), P(), P(), P(), P(), P(), P())
    out_specs = P("tm", "space", None, None)
    return jax.shard_map(on_device, mesh=mesh, in_specs=in_specs, out_specs=out_specs, check_vma=False)
```

profile of v0, /device:TPU:103, one launch (start us, length us, event | category | flops | bytes accessed | tf_op | source)
XLA Modules:
  0.0 56.2 jit_solution(15776957806200936650)
XLA Ops:
  0.0 1.0 %slice.3 = bf16[4,3,128,128]{3,2,1,0:T(8,128)(2,1)S(1)} slice(bf16[4,16,128,128]{3,2,1,0:T(8,128)(2,1)} %x_hbm.1), slice={[0:4], [0:3], [0:128], [0:128]} | slice | bytes 786432 | tf_op jit(solution)/shard_map/slice | solution.py:360
  1.0 4.9 %collective-permute-start = (bf16[4,3,128,128]{3,2,1,0:T(8,128)(2,1)S(1)}, bf16[4,3,128,128]{3,2,1,0:T(8,128)(2,1)S(1)}, u32[]{:S(2)}, u32[]{:S(2)}) collective-permute-start(bf16[4,3,128,128]{3,2,1,0:T(8,128)(2,1)S(1)} %slice.3), channel_id=1, source_target_pairs={{1,0},{2,1},{3,2},{4,3},{5,4},{6,5},{7,6},{8,7},{9,8},{10,9},{11,1... | collective-permute-start | bytes 1179656 | tf_op jit(solution)/shard_map/ppermute | solution.py:360
  5.9 0.1 add_convert_fusion.ok_ref
  6.0 0.0 copy-start.2
  6.0 0.7 %copy-done.2 = f32[128]{0:T(128)S(1)} copy-done((f32[128]{0:T(128)S(1)}, f32[128]{0:T(128)}, u32[]{:S(2)}) %copy-start.2) | copy-done | bytes 536
  6.7 0.0 copy-start
  6.7 8.9 %own.1 = (bf16[4,2,20,64,256]{4,3,2,1,0:T(8,128)(2,1)S(1)}, bf16[4,18,64,256]{3,2,1,0:T(8,128)(2,1)S(1)}, bf16[4,3,2,256,256]{4,3,2,1,0:T(8,128)(2,1)S(1)}, bf16...) custom-call(bf16[4,16,128,128]{3,2,1,0:T(8,128)(2,1)} %x_hbm.1, ...), custom_call_target="tpu_custom_call" | custom-call | flops 6000000000 | bytes 4194304 | tf_op jit(solution)/shard_map/own/pallas_call | solution.py:337
  15.6 0.0 collective-permute-done.halo_ref
  15.6 0.0 copy-done
  15.6 0.0 copy-start.1
  15.6 2.1 %ahead.1 = (bf16[4,2,20,64,256]{4,3,2,1,0:T(8,128)(2,1)S(1)}, bf16[4,18,64,256]{3,2,1,0:T(8,128)(2,1)S(1)}, bf16[2,2,10,64,384]{4,3,2,1,0:T(8,128)(2,1)S(1)}, bf16[2,9,64,256]{3,2,1,0:T(8,128)(2,1)S(1)}) custom-call(s32[2]{0:T(128)S(1)} %add_convert_fusion.ok_ref, ...), custom_call_target="tpu_custom_call", output_to_operand_aliasing={{0}: (1, {}), {1}: (2, {}), {2}: (3, {})} | custom-call | flops 2000000000 | bytes 4194304 | tf_op jit(solution)/shard_map/ahead/pallas_call | solution.py:337
  17.7 5.6 %collective-permute-start.1 = (bf16[2,9,64,256]{3,2,1,0:T(8,128)(2,1)S(1)}, bf16[2,9,64,256]{3,2,1,0:T(8,128)(2,1)S(1)}, u32[]{:S(2)}, u32[]{:S(2)}) collective-permute-start(bf16[2,9,64,256]{3,2,1,0:T(8,128)(2,1)S(1)} %get-tuple-element.29), channel_id=1, source_target_pairs={{0,16},{16,32},{32,48},{48,64},{64,80},{80,96},{96,112},{112,128},... | collective-permute-start | bytes 1769480 | tf_op jit(solution)/shard_map/ppermute | solution.py:375
  23.3 0.0 copy-done.1
  23.3 2.3 %late.1 = (bf16[2,2,10,64,384]{4,3,2,1,0:T(8,128)(2,1)S(1)}, bf16[2,9,64,256]{3,2,1,0:T(8,128)(2,1)S(1)}, bf16[2,9,64,256]{3,2,1,0:T(8,128)(2,1)S(1)}, bf16[2,2,64,256]{3,2,1,0:T(8,128)(2,1)S(1)}) custom-call(s32[2]{0:T(128)S(1)} %add_convert_fusion.ok_ref, ...), custom_call_target="tpu_custom_call", output_to_operand_aliasing={{0}: (3, {})} | custom-call | flops 2500000000 | bytes 4194304 | tf_op jit(solution)/shard_map/late/pallas_call | solution.py:337
  25.6 1.9 %collective-permute-start.3 = (bf16[2,9,64,256]{3,2,1,0:T(8,128)(2,1)S(1)}, bf16[2,9,64,256]{3,2,1,0:T(8,128)(2,1)S(1)}, u32[]{:S(2)}, u32[]{:S(2)}) collective-permute-start(bf16[2,9,64,256]{3,2,1,0:T(8,128)(2,1)S(1)} %get-tuple-element.39), channel_id=1, source_target_pairs={{0,16},{16,32},{32,48},{48,64},{64,80},{80,96},{96,112},{112,128},... | collective-permute-start | bytes 1769480 | tf_op jit(solution)/shard_map/ppermute | solution.py:381
  27.5 2.6 %collective-permute-done.1.z_ref = bf16[2,9,64,256]{3,2,1,0:T(8,128)(2,1)S(1)} collective-permute-done((bf16[2,9,64,256]{3,2,1,0:T(8,128)(2,1)S(1)}, bf16[2,9,64,256]{3,2,1,0:T(8,128)(2,1)S(1)}, u32[]{:S(2)}, u32[]{:S(2)}) %collective-permute-start.1) | collective-permute-done | bytes 589856 | tf_op jit(solution)/shard_map/ppermute | solution.py:375
  30.1 3.5 %early.1 = (bf16[2,9,64,256]{3,2,1,0:T(8,128)(2,1)S(1)}, bf16[4,2,64,256]{3,2,1,0:T(8,128)(2,1)S(1)}) custom-call(s32[2]{0:T(128)S(1)} %add_convert_fusion.ok_ref, bf16[4,2,20,64,256]{4,3,2,1,0:T(8,128)(2,1)S(1)} %get-tuple-element.27.u_ref, bf16[4,18,64,256]{3,2,1,0:T(8,128)(2,1)S(1)} %get-tuple-element.28.x2_ref, ...), custom_call_target="tpu_custom_call" | custom-call | flops 3000000000 | bytes 4194304 | tf_op jit(solution)/shard_map/early/pallas_call | solution.py:337
  33.6 1.9 %collective-permute-start.2 = (bf16[4,2,64,256]{3,2,1,0:T(8,128)(2,1)S(1)}, bf16[4,2,64,256]{3,2,1,0:T(8,128)(2,1)S(1)}, u32[]{:S(2)}, u32[]{:S(2)}) collective-permute-start(bf16[4,2,64,256]{3,2,1,0:T(8,128)(2,1)S(1)} %get-tuple-element.35), channel_id=1, source_target_pairs={{0,1},{1,2},{2,3},{3,4},{4,5},{5,6},{6,7},{7,8},{8,9},{9,10},{10,1... | collective-permute-start | bytes 786440 | tf_op jit(solution)/shard_map/ppermute | solution.py:388
  35.6 6.2 %collective-permute-start.4 = (bf16[2,2,64,256]{3,2,1,0:T(8,128)(2,1)S(1)}, bf16[2,2,64,256]{3,2,1,0:T(8,128)(2,1)S(1)}, u32[]{:S(2)}, u32[]{:S(2)}) collective-permute-start(bf16[2,2,64,256]{3,2,1,0:T(8,128)(2,1)S(1)} %get-tuple-element.40), channel_id=1, source_target_pairs={{0,17},{1,18},{2,19},{3,20},{4,21},{5,22},{6,23},{7,24},{8,25},{9,... | collective-permute-start | bytes 393224 | tf_op jit(solution)/shard_map/ppermute | solution.py:382
  41.8 0.0 copy-start.3
  41.8 2.5 %mid.1 = (bf16[4,4,10,32,256]{4,3,2,1,0:T(8,128)(2,1)S(1)}, bf16[2,3,3,256,256]{4,3,2,1,0:T(8,128)(2,1)S(1)}) custom-call(s32[2]{0:T(128)S(1)} %add_convert_fusion.ok_ref, bf16[2,9,64,256]{3,2,1,0:T(8,128)(2,1)S(1)} %get-tuple-element.32.red01_ref.red_ref, bf16[2,9,64,256]{3,2,1,0:T(8,128)(2,1)S(1)} %get-tuple-element.31.red23_ref.red_ref, ...), custom_call_target="tpu_custom_call" | custom-call | flops 1500000000 | bytes 4194304 | tf_op jit(solution)/shard_map/mid/pallas_call | solution.py:337
  44.3 2.9 %collective-permute-done.2.halo_ref = bf16[4,2,64,256]{3,2,1,0:T(8,128)(2,1)S(1)} collective-permute-done((bf16[4,2,64,256]{3,2,1,0:T(8,128)(2,1)S(1)}, bf16[4,2,64,256]{3,2,1,0:T(8,128)(2,1)S(1)}, u32[]{:S(2)}, u32[]{:S(2)}) %collective-permute-start.2) | collective-permute-done | bytes 262176 | tf_op jit(solution)/shard_map/ppermute | solution.py:388
  47.2 0.0 copy-done.3
  47.2 4.2 %mid_late.1 = (bf16[4,8,64,256]{3,2,1,0:T(8,128)(2,1)}, bf16[4,4,10,32,256]{4,3,2,1,0:T(8,128)(2,1)S(1)}) custom-call(s32[2]{0:T(128)S(1)} %add_convert_fusion.ok_ref, bf16[4,4,10,32,256]{4,3,2,1,0:T(8,128)(2,1)S(1)} %get-tuple-element.34.u_in, bf16[4,2,64,256]{3,2,1,0:T(8,128)(2,1)S(1)} %collective-permute-done.2.halo_ref, ...), custom_call_target="tpu_custom_call", output_to_operand_aliasing={{1}: (1, {})} | custom-call | flops 3000000000 | bytes 4194304 | tf_op jit(solution)/shard_map/mid_late/pallas_call | solution.py:337
  51.4 0.0 collective-permute-done.4.zedge_ref
  51.4 0.0 collective-permute-done.3.zact_ref
  51.4 4.6 %mid_early.1 = bf16[4,8,64,256]{3,2,1,0:T(8,128)(2,1)} custom-call(s32[2]{0:T(128)S(1)} %add_convert_fusion.ok_ref, bf16[4,8,64,256]{3,2,1,0:T(8,128)(2,1)} %get-tuple-element.37.lat_in, bf16[4,4,10,32,256]{4,3,2,1,0:T(8,128)(2,1)S(1)} %get-tuple-element.38.u_ref, ...), custom_call_target="tpu_custom_call", output_to_operand_aliasing={{}: (1, {})} | custom-call | flops 3000000000 | bytes 4194304 | tf_op jit(solution)/shard_map/mid_early/pallas_call | solution.py:337
Async XLA Ops:
  1.0 14.6 %collective-permute-start = (bf16[4,3,128,128]{3,2,1,0:T(8,128)(2,1)S(1)}, bf16[4,3,128,128]{3,2,1,0:T(8,128)(2,1)S(1)}, u32[]{:S(2)}, u32[]{:S(2)}) collective-permute-start(bf16[4,3,128,128]{3,2,1,0:T(8,128)(2,1)S(1)} %slice.3), channel_id=1, source_target_pairs={{1,0},{2,1},{3,2},{4,3},{5,4},{6,5},{7,6},{8,7},{9,8},{10,9},{11,1... | collective-permute-start | bytes 1179656 | tf_op jit(solution)/shard_map/ppermute | solution.py:360
  6.0 0.7 %copy-start.2 = (f32[128]{0:T(128)S(1)}, f32[128]{0:T(128)}, u32[]{:S(2)}) copy-start(f32[128]{0:T(128)} %param.9) | copy-start | bytes 1540
  6.7 8.9 %copy-start = (bf16[3,3,128,256]{3,2,1,0:T(8,128)(2,1)S(1)}, bf16[3,3,128,256]{3,2,1,0:T(8,128)(2,1)}, u32[]{:S(2)}) copy-start(bf16[3,3,128,256]{3,2,1,0:T(8,128)(2,1)} %kd_ref.5) | copy-start | bytes 1769476
  15.6 7.7 %copy-start.1 = (f32[256]{0:T(256)S(1)}, f32[256]{0:T(256)}, u32[]{:S(2)}) copy-start(f32[256]{0:T(256)} %param.11) | copy-start | bytes 3076
  17.7 12.4 %collective-permute-start.1 = (bf16[2,9,64,256]{3,2,1,0:T(8,128)(2,1)S(1)}, bf16[2,9,64,256]{3,2,1,0:T(8,128)(2,1)S(1)}, u32[]{:S(2)}, u32[]{:S(2)}) collective-permute-start(bf16[2,9,64,256]{3,2,1,0:T(8,128)(2,1)S(1)} %get-tuple-element.29), channel_id=1, source_target_pairs={{0,16},{16,32},{32,48},{48,64},{64,80},{80,96},{96,112},{112,128},... | collective-permute-start | bytes 1769480 | tf_op jit(solution)/shard_map/ppermute | solution.py:375
  25.6 25.8 %collective-permute-start.3 = (bf16[2,9,64,256]{3,2,1,0:T(8,128)(2,1)S(1)}, bf16[2,9,64,256]{3,2,1,0:T(8,128)(2,1)S(1)}, u32[]{:S(2)}, u32[]{:S(2)}) collective-permute-start(bf16[2,9,64,256]{3,2,1,0:T(8,128)(2,1)S(1)} %get-tuple-element.39), channel_id=1, source_target_pairs={{0,16},{16,32},{32,48},{48,64},{64,80},{80,96},{96,112},{112,128},... | collective-permute-start | bytes 1769480 | tf_op jit(solution)/shard_map/ppermute | solution.py:381
  33.6 13.5 %collective-permute-start.2 = (bf16[4,2,64,256]{3,2,1,0:T(8,128)(2,1)S(1)}, bf16[4,2,64,256]{3,2,1,0:T(8,128)(2,1)S(1)}, u32[]{:S(2)}, u32[]{:S(2)}) collective-permute-start(bf16[4,2,64,256]{3,2,1,0:T(8,128)(2,1)S(1)} %get-tuple-element.35), channel_id=1, source_target_pairs={{0,1},{1,2},{2,3},{3,4},{4,5},{5,6},{6,7},{7,8},{8,9},{9,10},{10,1... | collective-permute-start | bytes 786440 | tf_op jit(solution)/shard_map/ppermute | solution.py:388
  35.6 15.8 %collective-permute-start.4 = (bf16[2,2,64,256]{3,2,1,0:T(8,128)(2,1)S(1)}, bf16[2,2,64,256]{3,2,1,0:T(8,128)(2,1)S(1)}, u32[]{:S(2)}, u32[]{:S(2)}) collective-permute-start(bf16[2,2,64,256]{3,2,1,0:T(8,128)(2,1)S(1)} %get-tuple-element.40), channel_id=1, source_target_pairs={{0,17},{1,18},{2,19},{3,20},{4,21},{5,22},{6,23},{7,24},{8,25},{9,... | collective-permute-start | bytes 393224 | tf_op jit(solution)/shard_map/ppermute | solution.py:382
  41.8 5.4 %copy-start.3 = (f32[256]{0:T(256)S(1)}, f32[256]{0:T(256)}, u32[]{:S(2)}) copy-start(f32[256]{0:T(256)} %param.13) | copy-start | bytes 3076
where the time goes:
time: 56.5 us; the launch traced here: 56.2 us
  Pallas kernels  28.1 us (50%)
  starting transfers between devices  20.6 us (36%)
  waiting for transfers between devices  5.48 us (10%)
  local copies, waits for them, and re-layouts  1.69 us (3%)
    pallas_call x7, Pallas kernels, call(): pl.pallas_call(body, out_shape=outs, in_specs=in_specs or [V] * len(ins),...  28.1 us
    ppermute x1, starting transfers between devices, on_device(): zedge = lax.ppermute(edge23, ('tm', 'space'), cross)  6.22 us
    ppermute x1, starting transfers between devices, on_device(): zpart = lax.ppermute(part, 'tm', later)  5.6 us
    ppermute x1, starting transfers between devices, on_device(): halo = lax.ppermute(features[:, 0:3], 'space', up)  4.91 us
    ppermute x1, waiting for transfers between devices, on_device(): halo_mid = lax.ppermute(dn, 'space', down)  2.87 us
    ppermute x1, waiting for transfers between devices, on_device(): zpart = lax.ppermute(part, 'tm', later)  2.6 us
    ppermute x1, starting transfers between devices, on_device(): halo_mid = lax.ppermute(dn, 'space', down)  1.92 us
    ppermute x1, starting transfers between devices, on_device(): zact = lax.ppermute(act23, 'tm', later)  1.92 us
  transfers between devices with their start and end apart: 5, of which 2 were waited for; matrix products, arithmetic and copies ran while one was open for 0% of the time, Pallas kernels for 38%

commit v1 on v0

v1 whole, which is shorter than its diff:
```python
import jax
import jax.numpy as jnp
from jax import lax
from jax.experimental import pallas as pl
from jax.experimental.pallas import tpu as pltpu
from jax.sharding import PartitionSpec as P

BF = jnp.bfloat16
F32 = jnp.float32
VMEM = pltpu.VMEM
LIMIT = 24 * 2**20


def silu(v):
    h = 0.5 * v
    return h + h * jnp.tanh(h)


def clear_edges(s_ref):
    for f in range(s_ref.shape[0]):
        for e in range(2):
            s_ref[f, e, 0:8] = jnp.zeros((8, s_ref.shape[-1]), F32)
            s_ref[f, e, s_ref.shape[2] - 8 :] = jnp.zeros((8, s_ref.shape[-1]), F32)


def prep_first(x, f, r, u_ref, x2_ref, s_ref, q_ref, residual=True):
    q_ref[f] = x.astype(F32)
    even = q_ref[f, pl.ds(0, 64, stride=2), :]
    odd = q_ref[f, pl.ds(1, 64, stride=2), :]
    d1 = silu(even)
    d2 = silu(odd)
    s_ref[f, 0, 8:72] = d1
    s_ref[f, 1, 8:72] = d2
    d3 = s_ref[f, 0, 9:73]
    d0 = s_ref[f, 1, 7:71]
    lanes = slice((f % 2) * 128, (f % 2) * 128 + 128)
    for k, v in enumerate((d0 - d2, d1 + d2, d2 - d1, d1 - d3)):
        u_ref[k, f // 2, r + 1, :, lanes] = v.astype(BF)
    if residual:
        x2_ref[f, r, :, 0:128] = even.astype(BF)
        x2_ref[f, r, :, 128:256] = odd.astype(BF)


def transformed(g0, g1, g2):
    half = 0.5 * (g0 + g2)
    return half + 0.5 * g1, half - 0.5 * g1


class Pump:
    def __init__(self, work, slots):
        self.work, self.slots = list(work), slots

    def __call__(self):
        count = -(-len(self.work) // max(self.slots, 1))
        self.slots -= 1
        for _ in range(count):
            self.work.pop(0)()


def idle():
    pass


def first_rows(u_ref, w_ref, f_ref, o_ref, pairs, g0, rows, below, residual, bias, pump=idle):
    ms = []
    for k in range(4):
        lhs = jnp.concatenate(
            [u_ref[k, p, g0 + j : g0 + j + rows].reshape(rows * 64, 256) for j in range(3) for p, _ in pairs], axis=1
        )
        rhs = jnp.concatenate([w_ref[k, j, which] for j in range(3) for _, which in pairs], axis=0)
        ms.append(jnp.dot(lhs, rhs, preferred_element_type=F32))
        pump()
    both = (ms[1] + ms[2] + ms[0], ms[1] - ms[2] - ms[3])
    for q in range(2):
        for e in range(2):
            lanes = slice(e * 128, e * 128 + 128)
            y = both[e][:, q * 128 : q * 128 + 128].reshape(rows, 64, 128)
            if residual is not None:
                y = y + residual[q, g0 : g0 + rows, :, lanes].astype(F32) + bias
            for n in range(rows):
                g = g0 + n
                at = (g % 2, (g + 1) // 2)
                row = y[n] * below if g >= 16 else y[n]
                f_ref[q, at[0], at[1], :, lanes] = row.astype(BF)
                if e == 1:
                    o_ref[q, n, 8:72] = row
                    f_ref[q, at[0], at[1], :, 256:384] = o_ref[q, n, 7:71].astype(BF)


def clear_shift(o_ref):
    for q in range(2):
        for n in range(o_ref.shape[1]):
            o_ref[q, n, 0:8] = jnp.zeros((8, 128), F32)


def down_conv(f_ref, kd_ref):
    rhs = jnp.concatenate([kd_ref[j, c] for j in range(3) for c in (1, 2, 0)], axis=0)
    out = []
    for q in range(2):
        lhs = jnp.concatenate(
            [
                f_ref[q, 1, 0:9].reshape(576, 384),
                f_ref[q, 0, 0:9].reshape(576, 384),
                f_ref[q, 1, 1:10].reshape(576, 384),
            ],
            axis=1,
        )
        out.append(jnp.dot(lhs, rhs, preferred_element_type=F32))
    return out


PAIR01 = ((0, 1),)
PAIR23 = ((0, 0), (1, 1))
PAIR45 = ((1, 0),)


def kernel_own(
    x_hbm, kf_hbm, ks_hbm, kd_hbm, bf_hbm, bd_hbm, bs_hbm,
    u_ref, x2_ref, w_ref, ks_ref, kd_ref, bf_ref, bd_ref, bs_ref, f45_ref, f23_ref,
    x_ref, kf_ref, s_ref, q_ref, o_ref, sem,
):
    xs = [pltpu.make_async_copy(x_hbm.at[:, n * 4 : n * 4 + 4], x_ref.at[:, n * 4 : n * 4 + 4], sem.at[n]) for n in range(4)]
    first = pltpu.make_async_copy(kf_hbm, kf_ref, sem.at[4])
    pairs = ((ks_hbm, ks_ref), (kd_hbm, kd_ref), (bf_hbm, bf_ref), (bd_hbm, bd_ref), (bs_hbm, bs_ref))
    rest = [pltpu.make_async_copy(a, b, sem.at[5 + n]) for n, (a, b) in enumerate(pairs)]
    xs[0].start()
    xs[1].start()
    first.start()
    rest[2].start()
    xs[2].start()
    xs[3].start()
    for n in (0, 1, 3, 4):
        rest[n].start()
    clear_edges(s_ref)
    clear_shift(o_ref)
    for k in range(4):
        for p in range(2):
            u_ref[k, p, 0] = jnp.zeros((64, 256), BF)
    for q in range(2):
        f45_ref[q, 1, 0] = jnp.zeros((64, 384), BF)
        f23_ref[q, 1, 0] = jnp.zeros((64, 384), BF)

    def row(r, carry):
        for f in range(4):
            prep_first(x_ref[f, r], f, r, u_ref, x2_ref, s_ref, q_ref)
        return carry

    for n in range(2):
        xs[n].wait()
        lax.fori_loop(n * 4, n * 4 + 4, row, 0)

    first.wait()

    def wrow(j, carry):
        zero = jnp.zeros((128, 128), BF)
        for i in range(3):
            g0, g1, g2 = (kf_ref[i, j, c] for c in range(3))
            a, b = transformed(g0.astype(F32), g1.astype(F32), g2.astype(F32))
            for k, g in enumerate((g0, a.astype(BF), b.astype(BF), g2)):
                if i == 0:
                    w_ref[k, j, 0, 0:128, 0:128] = g
                    w_ref[k, j, 0, 128:256, 128:256] = g
                    w_ref[k, j, 0, 0:128, 128:256] = zero
                    w_ref[k, j, 1, 128:256, 0:128] = zero
                elif i == 1:
                    w_ref[k, j, 0, 128:256, 0:128] = g
                    w_ref[k, j, 1, 0:128, 128:256] = g
                else:
                    w_ref[k, j, 1, 0:128, 0:128] = g
                    w_ref[k, j, 1, 128:256, 128:256] = g
        return carry

    lax.fori_loop(0, 3, wrow, 0)
    rest[2].wait()
    xs[2].wait()
    xs[3].wait()
    pump = Pump(
        [
            lambda f=f, r=r: prep_first(x_ref[f, r], f, r, u_ref, x2_ref, s_ref, q_ref)
            for r in range(8, 16)
            for f in range(4)
        ],
        8,
    )
    first_rows(u_ref, w_ref, f45_ref, o_ref, PAIR45, 0, 7, None, None, None, pump)
    first_rows(u_ref, w_ref, f23_ref, o_ref, PAIR23, 0, 7, None, x2_ref.at[2:4], bf_ref[...], pump)
    first_rows(u_ref, w_ref, f45_ref, o_ref, PAIR45, 7, 8, None, None, None)
    first_rows(u_ref, w_ref, f23_ref, o_ref, PAIR23, 7, 8, None, x2_ref.at[2:4], bf_ref[...])
    for n in (0, 1, 3, 4):
        rest[n].wait()


def kernel_ahead(ok_ref, u_in, x2_in, f_in, halo_ref, w_ref, kd_ref, u_ref, x2_ref, f_ref, part_ref, s_ref, q_ref, o_ref):
    clear_edges(s_ref)
    clear_shift(o_ref)
    for n in range(3):
        for f in range(4):
            prep_first(halo_ref[f, n], f, 16 + n, u_ref, x2_ref, s_ref, q_ref, n < 2)
    below = ok_ref[1].astype(F32)
    first_rows(u_ref, w_ref, f_ref, o_ref, PAIR45, 15, 3, below, None, None)
    out = down_conv(f_ref, kd_ref)
    for q in range(2):
        part_ref[q] = out[q].reshape(9, 64, 256).astype(BF)


def kernel_late(ok_ref, u_ref, x2_ref, f_in, w_ref, kd_ref, bf_ref, bd_ref, f_ref, red_ref, o_ref):
    clear_shift(o_ref)
    below = ok_ref[1].astype(F32)
    first_rows(u_ref, w_ref, f_ref, o_ref, PAIR23, 15, 3, below, x2_ref.at[2:4], bf_ref[...])
    out = down_conv(f_ref, kd_ref)
    for q in range(2):
        red_ref[q] = (out[q] + bd_ref[...]).astype(BF).reshape(9, 64, 256)


def prep_mid(act, f, to, u_ref, s_ref, q_ref):
    q_ref[f, 0] = act[:, 0:128]
    q_ref[f, 1] = act[:, 128:256]
    d1 = jnp.concatenate([q_ref[f, h, pl.ds(0, 32, stride=2), :] for h in range(2)], axis=1)
    d2 = jnp.concatenate([q_ref[f, h, pl.ds(1, 32, stride=2), :] for h in range(2)], axis=1)
    s_ref[f, 0, 8:40] = d1
    s_ref[f, 1, 8:40] = d2
    d3 = s_ref[f, 0, 9:41]
    d0 = s_ref[f, 1, 7:39]
    for k, v in enumerate((d0 - d2, d1 + d2, d2 - d1, d1 - d3)):
        u_ref[(k, *to)] = v.astype(BF)


def own_row(ok_ref, red_ref, f, r, u_ref, s_ref, q_ref):
    act = silu(red_ref[f % 2, r].astype(F32))
    if r == 8:
        act = act * ok_ref[1].astype(F32)
    prep_mid(act, f, (f, r + 1), u_ref, s_ref, q_ref)


def kernel_early(
    ok_ref, u_ref, x2_ref, w_ref, kd_ref, bf_ref, bd_ref, ks_ref, red_ref, p_ref, u2_ref, g_ref, f_ref, o_ref, s_ref, q_ref
):
    clear_shift(o_ref)
    clear_edges(s_ref)
    below = ok_ref[1].astype(F32)
    for q in range(2):
        f_ref[q, 1, 0] = jnp.zeros((64, 384), BF)

    def weights(i, j):
        a, b = transformed(*(ks_ref[i, j, c].astype(F32) for c in range(3)))
        g_ref[0, i, j] = a.astype(BF)
        g_ref[1, i, j] = b.astype(BF)

    work = [lambda f=f, r=r: own_row(ok_ref, red_ref, f, r, u2_ref, s_ref, q_ref) for r in range(1, 9) for f in (2, 3)]
    work += [lambda i=i, j=j: weights(i, j) for i in range(3) for j in range(3)]
    pump = Pump(work, 8)
    for g0 in (0, 9):
        first_rows(u_ref, w_ref, f_ref, o_ref, PAIR01, g0, 9, below, x2_ref.at[0:2], bf_ref[...], pump)
    out = down_conv(f_ref, kd_ref)
    for q in range(2):
        p_ref[q] = (out[q] + bd_ref[...]).reshape(9, 64, 256)


def kernel_join(p_ref, z_ref, red23_ref, red_ref, dn_ref):
    for q in range(2):
        for r in range(9):
            red_ref[q, r] = (p_ref[q, r] + z_ref[q, r].astype(F32)).astype(BF)
        for n in range(2):
            dn_ref[q, n] = red_ref[q, 7 + n]
            dn_ref[2 + q, n] = red23_ref[q, 7 + n]


def taps(ks_ref, g_ref, k, i):
    if k == 0 or k == 3:
        return jnp.concatenate([ks_ref[i, j, 2 * (k // 3)] for j in range(3)], axis=0)
    return g_ref[k - 1, i].reshape(768, 256)


def columns(t_ref, at, y0, y1):
    for h in range(2):
        lanes = slice(h * 128, h * 128 + 128)
        t_ref[(*at, h, pl.ds(0, 32, stride=2), slice(None))] = y0[:, lanes]
        t_ref[(*at, h, pl.ds(1, 32, stride=2), slice(None))] = y1[:, lanes]


def outer_pairs(u_ref, ks_ref, g_ref, r0, rows, zl_ref, y_ref, t_ref, pump=idle):
    n = rows * 32

    def lhs(k, a, b):
        return jnp.concatenate(
            [
                jnp.concatenate([u_ref[k, f, r0 + j : r0 + j + rows].reshape(n, 256) for f in (a, b)], axis=0)
                for j in range(3)
            ],
            axis=1,
        )

    first, later, own = [], [], []
    for k in range(4):
        first.append(jnp.dot(lhs(k, 2, 3), taps(ks_ref, g_ref, k, 0), preferred_element_type=F32))
        pump()
    for k in range(4):
        d1 = jnp.dot(lhs(k, 3, 0), taps(ks_ref, g_ref, k, 1), preferred_element_type=F32)
        d2 = jnp.dot(lhs(k, 0, 1), taps(ks_ref, g_ref, k, 2), preferred_element_type=F32)
        later.append((first[k][:n] + d1[:n], first[k][n:]))
        own.append((d2[:n], d2[n:] + d1[n:]))
    for f in range(2):
        for ms, to in ((later, t_ref), (own, y_ref)):
            y0 = (ms[1][f] + ms[2][f] + ms[0][f]).reshape(rows, 32, 256)
            y1 = (ms[1][f] - ms[2][f] - ms[3][f]).reshape(rows, 32, 256)
            for r in range(rows):
                columns(to, (f, r0 + r), y0[r], y1[r])
        for r in range(r0, r0 + rows):
            for h in range(2):
                zl_ref[f, r, :, h * 128 : h * 128 + 128] = t_ref[f, r, h].astype(BF)


def kernel_inner(ok_ref, u_in, red01_ref, ks_ref, g_ref, u_ref, zl_ref, y_ref, s_ref, q_ref, t_ref):
    clear_edges(s_ref)
    work = [lambda f=f, r=r: own_row(ok_ref, red01_ref, f, r, u_ref, s_ref, q_ref) for r in range(1, 9) for f in (0, 1)]
    outer_pairs(u_ref, ks_ref, g_ref, 2, 6, zl_ref, y_ref, t_ref, Pump(work, 4))


def kernel_edge(
    ok_ref, u_in, zl_in, y_in, halo_ref, red01_ref, red23_ref, ks_ref, g_ref, u_ref, zl_ref, y_ref, s_ref, q_ref, t_ref
):
    clear_edges(s_ref)
    inner = ok_ref[0] > 0
    for f in range(4):
        own = (red01_ref, red23_ref)[f // 2][f % 2, 0].astype(F32)
        above = jnp.where(inner, halo_ref[f, 1].astype(F32), own)
        prep_mid(silu(halo_ref[f, 0].astype(F32)), f, (f, 0), u_ref, s_ref, q_ref)
        prep_mid(silu(above), f, (f, 1), u_ref, s_ref, q_ref)
    outer_pairs(u_ref, ks_ref, g_ref, 0, 2, zl_ref, y_ref, t_ref)


def kernel_mid_late(ok_ref, u_ref, halo_ref, ks_ref, g_ref, red_ref, bs_ref, out_ref, t_ref):
    inner = ok_ref[0] > 0
    ms = []
    for k in range(4):
        lhs = jnp.concatenate(
            [u_ref[k, i : i + 2, j : j + 8].reshape(512, 256) for i in range(3) for j in range(3)], axis=1
        )
        rhs = jnp.concatenate([taps(ks_ref, g_ref, k, i) for i in range(3)], axis=0)
        ms.append(jnp.dot(lhs, rhs, preferred_element_type=F32))
    y0 = (ms[1] + ms[2] + ms[0]).reshape(2, 8, 32, 256)
    y1 = (ms[1] - ms[2] - ms[3]).reshape(2, 8, 32, 256)
    for f in range(2):
        for r in range(8):
            columns(t_ref, (f, r), y0[f, r], y1[f, r])
            for h in range(2):
                lanes = slice(h * 128, h * 128 + 128)
                v = red_ref[f, r, :, lanes].astype(F32)
                if r == 0:
                    v = jnp.where(inner, halo_ref[2 + f, 1, :, lanes].astype(F32), v)
                out_ref[f, r, :, lanes] = (t_ref[f, r, h] + v + bs_ref[:, lanes]).astype(BF)


def kernel_last(ok_ref, late_ref, y_ref, zl_ref, halo_ref, red_ref, bs_ref, lat_ref, out_ref, sem):
    inner = ok_ref[0] > 0
    copies = [pltpu.make_async_copy(late_ref, lat_ref.at[2:4], sem.at[0])]
    copies[0].start()
    for f in range(2):
        for r in range(8):
            for h in range(2):
                lanes = slice(h * 128, h * 128 + 128)
                v = red_ref[f, r, :, lanes].astype(F32)
                if r == 0:
                    v = jnp.where(inner, halo_ref[f, 1, :, lanes].astype(F32), v)
                v = v + zl_ref[f, r, :, lanes].astype(F32) + bs_ref[:, lanes]
                out_ref[f, r, :, lanes] = (y_ref[f, r, h] + v).astype(BF)
        copies.append(pltpu.make_async_copy(out_ref.at[f], lat_ref.at[f], sem.at[1 + f]))
        copies[-1].start()
    for c in copies:
        c.wait()


V = pl.BlockSpec(memory_space=pltpu.VMEM)
ANY = pl.BlockSpec(memory_space=pl.ANY)
HBM = pl.BlockSpec(memory_space=pltpu.HBM)
SM = pl.BlockSpec(memory_space=pltpu.SMEM)


def sds(*shape):
    return jax.ShapeDtypeStruct(shape, BF)


def res(*shape, dtype=BF):
    return VMEM(shape, dtype)


def keep(*xs):
    return [pltpu.with_memory_space_constraint(x, pltpu.VMEM) for x in xs]


def far(*xs):
    return [pltpu.with_memory_space_constraint(x, pltpu.HBM) for x in xs]


def call(body, name, ins, outs, scratch, flops, in_specs=None, out_specs=None, aliases=None):
    return pl.pallas_call(
        body,
        out_shape=outs,
        in_specs=in_specs or [V] * len(ins),
        out_specs=out_specs or [V] * len(outs),
        scratch_shapes=scratch,
        input_output_aliases=aliases or {},
        compiler_params=pltpu.CompilerParams(vmem_limit_bytes=LIMIT),
        cost_estimate=pl.CostEstimate(flops=flops, bytes_accessed=4 << 20, transcendentals=0),
        name=name,
    )(*ins)


def on_device(features, kf, bf, kd, bd, ks, bs):
    tm, sp = lax.axis_size("tm"), lax.axis_size("space")
    down = [(i, i + 1) for i in range(sp - 1)]
    up = [(i + 1, i) for i in range(sp - 1)]
    later = [(i, i + 1) for i in range(tm - 1)]
    at = lax.axis_index("space")
    ok = jnp.stack([(at > 0).astype(jnp.int32), (at < sp - 1).astype(jnp.int32)])

    halo = lax.ppermute(features[:, 0:3], "space", up)
    wide = [VMEM((4, 2, 80, 128), F32), VMEM((4, 128, 128), F32)]
    half = [VMEM((4, 2, 48, 256), F32), VMEM((4, 2, 64, 128), F32)]
    shift = lambda n: VMEM((2, n, 72, 128), F32)
    fshape, ushape, u2shape = (2, 2, 10, 64, 384), (4, 2, 20, 64, 256), (4, 4, 10, 32, 256)
    yshape = (2, 8, 2, 64, 128)
    u, x2, w, ksv, kdv, bfv, bdv, bsv, f45, f23 = call(
        kernel_own, "own", far(features, kf, ks, kd, bf.reshape(1, 128), bd.reshape(1, 256), bs.reshape(1, 256)),
        [
            res(*ushape), res(4, 18, 64, 256), res(4, 3, 2, 256, 256), res(3, 3, 3, 256, 256), res(3, 3, 128, 256),
            res(1, 128, dtype=F32), res(1, 256, dtype=F32), res(1, 256, dtype=F32), res(*fshape), res(*fshape),
        ],
        [VMEM((4, 16, 128, 128), BF), VMEM((3, 3, 3, 128, 128), BF), *wide, shift(8), pltpu.SemaphoreType.DMA((10,))],
        6_000_000_000, in_specs=[HBM] * 7,
    )
    u, x2, _, part = call(
        kernel_ahead, "ahead", (ok, *keep(u, x2, f45), halo, *keep(w, kdv)),
        [res(*ushape), res(4, 18, 64, 256), res(*fshape), sds(2, 9, 64, 256)],
        [*wide, shift(3)], 2_000_000_000, in_specs=[SM] + [V] * 6, aliases={1: 0, 2: 1, 3: 2},
    )
    zpart = lax.ppermute(part, "tm", later)
    _, red23 = call(
        kernel_late, "late", (ok, *keep(u, x2, f23, w, kdv, bfv, bdv)),
        [res(*fshape), res(2, 9, 64, 256)],
        [shift(3)], 2_500_000_000, in_specs=[SM] + [V] * 7, aliases={3: 0},
    )
    p01, u2, g = call(
        kernel_early, "early", (ok, *keep(u, x2, w, kdv, bfv, bdv, ksv, red23)),
        [res(2, 9, 64, 256, dtype=F32), res(*u2shape), res(2, 3, 3, 256, 256)],
        [VMEM(fshape, BF), shift(9), *half], 3_000_000_000, in_specs=[SM] + [V] * 8,
    )
    red01, dn = call(
        kernel_join, "join", (*keep(p01), zpart, *keep(red23)), [res(2, 9, 64, 256), sds(4, 2, 64, 256)], [], 500_000_000
    )
    halo_mid = lax.ppermute(dn, "space", down)
    u2, zl, y = call(
        kernel_inner, "inner", (ok, *keep(u2, red01, ksv, g)),
        [res(*u2shape), res(2, 8, 64, 256), res(*yshape, dtype=F32)],
        [*half, VMEM(yshape, F32)], 3_000_000_000, in_specs=[SM] + [V] * 4, aliases={1: 0},
    )
    u2, zl, y = call(
        kernel_edge, "edge", (ok, *keep(u2, zl, y), halo_mid, *keep(red01, red23, ksv, g)),
        [res(*u2shape), res(2, 8, 64, 256), res(*yshape, dtype=F32)],
        [*half, VMEM(yshape, F32)], 1_500_000_000, in_specs=[SM] + [V] * 8, aliases={1: 0, 2: 1, 3: 2},
    )
    zlat = lax.ppermute(zl, "tm", later)
    late = call(
        kernel_mid_late, "mid_late", (ok, *keep(u2), halo_mid, *keep(ksv, g, red23, bsv)),
        [res(2, 8, 64, 256)], [VMEM(yshape, F32)], 4_000_000_000, in_specs=[SM] + [V] * 6,
    )
    (lat,) = call(
        kernel_last, "last", (ok, *keep(late[0], y), zlat, halo_mid, *keep(red01, bsv)),
        [sds(4, 8, 64, 256)], [VMEM((2, 8, 64, 256), BF), pltpu.SemaphoreType.DMA((3,))],
        500_000_000, in_specs=[SM] + [V] * 6, out_specs=[HBM],
    )
    return lat


def solution(mesh):
    in_specs = (P("tm", "space", None, None), P(), P(), P(), P(), P(), P())
    out_specs = P("tm", "space", None, None)
    return jax.shard_map(on_device, mesh=mesh, in_specs=in_specs, out_specs=out_specs, check_vma=False)
```

time: 56.5 us -> 55.5 us (0.982)
  waiting for transfers between devices: 5.48 us -> 10.5 us
  starting transfers between devices: 20.6 us -> 16.1 us
  Pallas kernels: 28.1 us -> 26.8 us
  local copies, waits for them, and re-layouts: 1.69 us -> 1.02 us
    ppermute x1, waiting for transfers between devices: 2.87 us -> 7.58 us  [on_device(): halo_mid = lax.ppermute(dn, 'space', down)]
    ppermute x2 -> x1, starting transfers between devices: 8.14 us -> 3.46 us  [on_device(): zlat = lax.ppermute(zl, 'tm', later)]
    ppermute x2 -> x1, waiting for transfers between devices: 0.01 us -> 2.79 us  [on_device(): zlat = lax.ppermute(zl, 'tm', later)]
    ppermute x1, waiting for transfers between devices: 2.6 us -> 0.08 us  [on_device(): zpart = lax.ppermute(part, 'tm', later)]
    pallas_call x7 -> x9, Pallas kernels: 28.1 us -> 26.8 us  [call(): pl.pallas_call(body, out_shape=outs, in_specs=in_specs or [V] * len(ins),...]
    unnamed x8 -> x0, local copies, waits for them, and re-layouts: 0.67 us -> none
  transfers between devices with their start and end apart: 5 -> 4, of which waited for: 2 -> 3; matrix products, arithmetic and copies ran while one was open for 0% -> 0% of each run, Pallas kernels for 38% -> 39%
where the time goes in v1:
time: 55.5 us; the launch traced here: 54.7 us
  Pallas kernels  26.8 us (48%)
  starting transfers between devices  16.1 us (29%)
  waiting for transfers between devices  10.5 us (19%)
  local copies, waits for them, and re-layouts  1.02 us (2%)
    pallas_call x9, Pallas kernels, call(): pl.pallas_call(body, out_shape=outs, in_specs=in_specs or [V] * len(ins),...  26.8 us
    ppermute x1, waiting for transfers between devices, on_device(): halo_mid = lax.ppermute(dn, 'space', down)  7.58 us
    ppermute x1, starting transfers between devices, on_device(): zpart = lax.ppermute(part, 'tm', later)  5.59 us
    ppermute x1, starting transfers between devices, on_device(): halo = lax.ppermute(features[:, 0:3], 'space', up)  4.91 us
    ppermute x1, starting transfers between devices, on_device(): zlat = lax.ppermute(zl, 'tm', later)  3.46 us
    ppermute x1, waiting for transfers between devices, on_device(): zlat = lax.ppermute(zl, 'tm', later)  2.79 us
    ppermute x1, starting transfers between devices, on_device(): halo_mid = lax.ppermute(dn, 'space', down)  2.1 us
  transfers between devices with their start and end apart: 4, of which 3 were waited for; matrix products, arithmetic and copies ran while one was open for 0% of the time, Pallas kernels for 39%

profile of v1, /device:TPU:103, one launch (start us, length us, event | category | flops | bytes accessed | tf_op | source)
XLA Modules:
  0.0 54.7 jit_solution(5238277338080299990)
XLA Ops:
  0.0 1.0 %slice.3 = bf16[4,3,128,128]{3,2,1,0:T(8,128)(2,1)S(1)} slice(bf16[4,16,128,128]{3,2,1,0:T(8,128)(2,1)} %x_hbm.1), slice={[0:4], [0:3], [0:128], [0:128]} | slice | bytes 786432 | tf_op jit(solution)/shard_map/slice | solution.py:417
  1.0 4.9 %collective-permute-start = (bf16[4,3,128,128]{3,2,1,0:T(8,128)(2,1)S(1)}, bf16[4,3,128,128]{3,2,1,0:T(8,128)(2,1)S(1)}, u32[]{:S(2)}, u32[]{:S(2)}) collective-permute-start(bf16[4,3,128,128]{3,2,1,0:T(8,128)(2,1)S(1)} %slice.3), channel_id=1, source_target_pairs={{1,0},{2,1},{3,2},{4,3},{5,4},{6,5},{7,6},{8,7},{9,8},{10,9},{11,1... | collective-permute-start | bytes 1179656 | tf_op jit(solution)/shard_map/ppermute | solution.py:417
  5.9 0.1 add_convert_fusion.ok_ref
  6.0 8.8 %own.1 = (bf16[4,2,20,64,256]{4,3,2,1,0:T(8,128)(2,1)S(1)}, bf16[4,18,64,256]{3,2,1,0:T(8,128)(2,1)S(1)}, bf16[4,3,2,256,256]{4,3,2,1,0:T(8,128)(2,1)S(1)}, bf16...) custom-call(bf16[4,16,128,128]{3,2,1,0:T(8,128)(2,1)} %x_hbm.1, ...), custom_call_target="tpu_custom_call" | custom-call | flops 6000000000 | bytes 4194304 | tf_op jit(solution)/shard_map/own/pallas_call | solution.py:396
  14.8 0.0 collective-permute-done.halo_ref
  14.8 2.1 %ahead.1 = (bf16[4,2,20,64,256]{4,3,2,1,0:T(8,128)(2,1)S(1)}, bf16[4,18,64,256]{3,2,1,0:T(8,128)(2,1)S(1)}, bf16[2,2,10,64,384]{4,3,2,1,0:T(8,128)(2,1)S(1)}, bf16[2,9,64,256]{3,2,1,0:T(8,128)(2,1)S(1)}) custom-call(s32[2]{0:T(128)S(1)} %add_convert_fusion.ok_ref, ...), custom_call_target="tpu_custom_call", output_to_operand_aliasing={{0}: (1, {}), {1}: (2, {}), {2}: (3, {})} | custom-call | flops 2000000000 | bytes 4194304 | tf_op jit(solution)/shard_map/ahead/pallas_call | solution.py:396
  16.9 5.6 %collective-permute-start.1 = (bf16[2,9,64,256]{3,2,1,0:T(8,128)(2,1)S(1)}, bf16[2,9,64,256]{3,2,1,0:T(8,128)(2,1)S(1)}, u32[]{:S(2)}, u32[]{:S(2)}) collective-permute-start(bf16[2,9,64,256]{3,2,1,0:T(8,128)(2,1)S(1)} %get-tuple-element.44), channel_id=1, source_target_pairs={{0,16},{16,32},{32,48},{48,64},{64,80},{80,96},{96,112},{112,128},... | collective-permute-start | bytes 1769480 | tf_op jit(solution)/shard_map/ppermute | solution.py:437
  22.5 2.1 %late.1 = (bf16[2,2,10,64,384]{4,3,2,1,0:T(8,128)(2,1)S(1)}, bf16[2,9,64,256]{3,2,1,0:T(8,128)(2,1)S(1)}) custom-call(s32[2]{0:T(128)S(1)} %add_convert_fusion.ok_ref, bf16[4,2,20,64,256]{4,3,2,1,0:T(8,128)(2,1)S(1)} %get-tuple-element.35.u_ref, bf16[4,18,64,256]{3,2,1,0:T(8,128)(2,1)S(1)} %get-tuple-element.36.x2_ref, ...), custom_call_target="tpu_custom_call", output_to_operand_aliasing={{0}: (3, {})} | custom-call | flops 2500000000 | bytes 4194304 | tf_op jit(solution)/shard_map/late/pallas_call | solution.py:396
  24.6 4.6 %early.1 = (f32[2,9,64,256]{3,2,1,0:T(8,128)S(1)}, bf16[4,4,10,32,256]{4,3,2,1,0:T(8,128)(2,1)S(1)}, bf16[2,3,3,256,256]{4,3,2,1,0:T(8,128)(2,1)S(1)}) custom-call(s32[2]{0:T(128)S(1)} %add_convert_fusion.ok_ref, bf16[4,2,20,64,256]{4,3,2,1,0:T(8,128)(2,1)S(1)} %get-tuple-element.35.u_ref, bf16[4,18,64,256]{3,2,1,0:T(8,128)(2,1)S(1)} %get-tuple-element.36.x2_ref, ...), custom_call_target="tpu_custom_call" | custom-call | flops 3000000000 | bytes 4194304 | tf_op jit(solution)/shard_map/early/pallas_call | solution.py:396
  29.2 0.1 collective-permute-done.1.z_ref
  29.3 0.1 join.1
  29.4 2.1 %collective-permute-start.2 = (bf16[4,2,64,256]{3,2,1,0:T(8,128)(2,1)S(1)}, bf16[4,2,64,256]{3,2,1,0:T(8,128)(2,1)S(1)}, u32[]{:S(2)}, u32[]{:S(2)}) collective-permute-start(bf16[4,2,64,256]{3,2,1,0:T(8,128)(2,1)S(1)} %get-tuple-element.50), channel_id=1, source_target_pairs={{0,1},{1,2},{2,3},{3,4},{4,5},{5,6},{6,7},{7,8},{8,9},{9,10},{10,1... | collective-permute-start | bytes 786440 | tf_op jit(solution)/shard_map/ppermute | solution.py:451
  31.5 2.8 %inner.1 = (bf16[4,4,10,32,256]{4,3,2,1,0:T(8,128)(2,1)S(1)}, bf16[2,8,64,256]{3,2,1,0:T(8,128)(2,1)S(1)}, f32[2,8,2,64,128]{4,3,2,1,0:T(8,128)S(1)}) custom-call(s32[2]{0:T(128)S(1)} %add_convert_fusion.ok_ref, bf16[4,4,10,32,256]{4,3,2,1,0:T(8,128)(2,1)S(1)} %get-tuple-element.42.u_in, ...), custom_call_target="tpu_custom_call", output_to_operand_aliasing={{0}: (1, {})} | custom-call | flops 3000000000 | bytes 4194304 | tf_op jit(solution)/shard_map/inner/pallas_call | solution.py:396
  34.3 7.6 %collective-permute-done.2.halo_ref = bf16[4,2,64,256]{3,2,1,0:T(8,128)(2,1)S(1)} collective-permute-done((bf16[4,2,64,256]{3,2,1,0:T(8,128)(2,1)S(1)}, bf16[4,2,64,256]{3,2,1,0:T(8,128)(2,1)S(1)}, u32[]{:S(2)}, u32[]{:S(2)}) %collective-permute-start.2) | collective-permute-done | bytes 262176 | tf_op jit(solution)/shard_map/ppermute | solution.py:451
  41.9 1.5 %edge.1 = (bf16[4,4,10,32,256]{4,3,2,1,0:T(8,128)(2,1)S(1)}, bf16[2,8,64,256]{3,2,1,0:T(8,128)(2,1)S(1)}, f32[2,8,2,64,128]{4,3,2,1,0:T(8,128)S(1)}) custom-call(s32[2]{0:T(128)S(1)} %add_convert_fusion.ok_ref, bf16[4,4,10,32,256]{4,3,2,1,0:T(8,128)(2,1)S(1)} %get-tuple-element.47.u_in, ...), custom_call_target="tpu_custom_call", output_to_operand_aliasing={{0}: (1, {}), {1}: (2, {}), {2}: (3, {})} | custom-call | flops 1500000000 | bytes 4194304 | tf_op jit(solution)/shard_map/edge/pallas_call | solution.py:396
  43.4 3.5 %collective-permute-start.3 = (bf16[2,8,64,256]{3,2,1,0:T(8,128)(2,1)S(1)}, bf16[2,8,64,256]{3,2,1,0:T(8,128)(2,1)S(1)}, u32[]{:S(2)}, u32[]{:S(2)}) collective-permute-start(bf16[2,8,64,256]{3,2,1,0:T(8,128)(2,1)S(1)} %get-tuple-element.54), channel_id=1, source_target_pairs={{0,16},{16,32},{32,48},{48,64},{64,80},{80,96},{96,112},{112,128},... | collective-permute-start | bytes 1572872 | tf_op jit(solution)/shard_map/ppermute | solution.py:462
  46.9 3.3 %mid_late.1.late_ref = bf16[2,8,64,256]{3,2,1,0:T(8,128)(2,1)S(1)} custom-call(s32[2]{0:T(128)S(1)} %add_convert_fusion.ok_ref, bf16[4,4,10,32,256]{4,3,2,1,0:T(8,128)(2,1)S(1)} %get-tuple-element.51.u_ref, bf16[4,2,64,256]{3,2,1,0:T(8,128)(2,1)S(1)} %collective-permute-done.2.halo_ref, bf16[3,3,3,256,256]{4,3,2,1,0:T(8,128)(2,1)S(1)} %get-tuple-element.39.ks_ref, ...), custom_call_target="tpu_custom_call" | custom-call | flops 4000000000 | bytes 4194304 | tf_op jit(solution)/shard_map/mid_late/pallas_call | solution.py:396
  50.2 2.8 %collective-permute-done.3.zl_ref = bf16[2,8,64,256]{3,2,1,0:T(8,128)(2,1)S(1)} collective-permute-done((bf16[2,8,64,256]{3,2,1,0:T(8,128)(2,1)S(1)}, bf16[2,8,64,256]{3,2,1,0:T(8,128)(2,1)S(1)}, u32[]{:S(2)}, u32[]{:S(2)}) %collective-permute-start.3) | collective-permute-done | bytes 524320 | tf_op jit(solution)/shard_map/ppermute | solution.py:462
  53.0 1.5 %last.1 = bf16[4,8,64,256]{3,2,1,0:T(8,128)(2,1)} custom-call(s32[2]{0:T(128)S(1)} %add_convert_fusion.ok_ref, bf16[2,8,64,256]{3,2,1,0:T(8,128)(2,1)S(1)} %mid_late.1.late_ref, f32[2,8,2,64,128]{4,3,2,1,0:T(8,128)S(1)} %get-tuple-element.53.y_ref, bf16[2,8,64,256]{3,2,1,0:T(8,128)(2,1)S(1)} %collective-permute-done.3.zl_ref, ...), custom_call_target="tpu_custom_call" | custom-call | flops 500000000 | bytes 4194304 | tf_op jit(solution)/shard_map/last/pallas_call | solution.py:396
Async XLA Ops:
  1.0 13.8 %collective-permute-start = (bf16[4,3,128,128]{3,2,1,0:T(8,128)(2,1)S(1)}, bf16[4,3,128,128]{3,2,1,0:T(8,128)(2,1)S(1)}, u32[]{:S(2)}, u32[]{:S(2)}) collective-permute-start(bf16[4,3,128,128]{3,2,1,0:T(8,128)(2,1)S(1)} %slice.3), channel_id=1, source_target_pairs={{1,0},{2,1},{3,2},{4,3},{5,4},{6,5},{7,6},{8,7},{9,8},{10,9},{11,1... | collective-permute-start | bytes 1179656 | tf_op jit(solution)/shard_map/ppermute | solution.py:417
  16.9 12.4 %collective-permute-start.1 = (bf16[2,9,64,256]{3,2,1,0:T(8,128)(2,1)S(1)}, bf16[2,9,64,256]{3,2,1,0:T(8,128)(2,1)S(1)}, u32[]{:S(2)}, u32[]{:S(2)}) collective-permute-start(bf16[2,9,64,256]{3,2,1,0:T(8,128)(2,1)S(1)} %get-tuple-element.44), channel_id=1, source_target_pairs={{0,16},{16,32},{32,48},{48,64},{64,80},{80,96},{96,112},{112,128},... | collective-permute-start | bytes 1769480 | tf_op jit(solution)/shard_map/ppermute | solution.py:437
  29.4 12.5 %collective-permute-start.2 = (bf16[4,2,64,256]{3,2,1,0:T(8,128)(2,1)S(1)}, bf16[4,2,64,256]{3,2,1,0:T(8,128)(2,1)S(1)}, u32[]{:S(2)}, u32[]{:S(2)}) collective-permute-start(bf16[4,2,64,256]{3,2,1,0:T(8,128)(2,1)S(1)} %get-tuple-element.50), channel_id=1, source_target_pairs={{0,1},{1,2},{2,3},{3,4},{4,5},{5,6},{6,7},{7,8},{8,9},{9,10},{10,1... | collective-permute-start | bytes 786440 | tf_op jit(solution)/shard_map/ppermute | solution.py:451
  43.4 9.6 %collective-permute-start.3 = (bf16[2,8,64,256]{3,2,1,0:T(8,128)(2,1)S(1)}, bf16[2,8,64,256]{3,2,1,0:T(8,128)(2,1)S(1)}, u32[]{:S(2)}, u32[]{:S(2)}) collective-permute-start(bf16[2,8,64,256]{3,2,1,0:T(8,128)(2,1)S(1)} %get-tuple-element.54), channel_id=1, source_target_pairs={{0,16},{16,32},{32,48},{48,64},{64,80},{80,96},{96,112},{112,128},... | collective-permute-start | bytes 1572872 | tf_op jit(solution)/shard_map/ppermute | solution.py:462

commit v2 on v1

--- a/solution.py
+++ b/solution.py
@@ -9,6 +9,7 @@
 F32 = jnp.float32
 VMEM = pltpu.VMEM
 LIMIT = 24 * 2**20
+STEP = 4
 
 
 def silu(v):
@@ -93,7 +94,7 @@
             o_ref[q, n, 0:8] = jnp.zeros((8, 128), F32)
 
 
-def down_conv(f_ref, kd_ref):
+def down_conv(f_ref, kd_ref, pump=idle):
     rhs = jnp.concatenate([kd_ref[j, c] for j in range(3) for c in (1, 2, 0)], axis=0)
     out = []
     for q in range(2):
@@ -106,6 +107,7 @@
             axis=1,
         )
         out.append(jnp.dot(lhs, rhs, preferred_element_type=F32))
+        pump()
     return out
 
 
@@ -116,7 +118,7 @@
 
 def kernel_own(
     x_hbm, kf_hbm, ks_hbm, kd_hbm, bf_hbm, bd_hbm, bs_hbm,
-    u_ref, x2_ref, w_ref, ks_ref, kd_ref, bf_ref, bd_ref, bs_ref, f45_ref, f23_ref,
+    u_ref, x2_ref, w_ref, ks_ref, kd_ref, bf_ref, bd_ref, bs_ref, f45_ref, f23_ref, f01_ref,
     x_ref, kf_ref, s_ref, q_ref, o_ref, sem,
 ):
     xs = [pltpu.make_async_copy(x_hbm.at[:, n * 4 : n * 4 + 4], x_ref.at[:, n * 4 : n * 4 + 4], sem.at[n]) for n in range(4)]
@@ -139,6 +141,7 @@
     for q in range(2):
         f45_ref[q, 1, 0] = jnp.zeros((64, 384), BF)
         f23_ref[q, 1, 0] = jnp.zeros((64, 384), BF)
+        f01_ref[q, 1, 0] = jnp.zeros((64, 384), BF)
 
     def row(r, carry):
         for f in range(4):
@@ -180,12 +183,12 @@
             for r in range(8, 16)
             for f in range(4)
         ],
-        8,
-    )
-    first_rows(u_ref, w_ref, f45_ref, o_ref, PAIR45, 0, 7, None, None, None, pump)
-    first_rows(u_ref, w_ref, f23_ref, o_ref, PAIR23, 0, 7, None, x2_ref.at[2:4], bf_ref[...], pump)
-    first_rows(u_ref, w_ref, f45_ref, o_ref, PAIR45, 7, 8, None, None, None)
-    first_rows(u_ref, w_ref, f23_ref, o_ref, PAIR23, 7, 8, None, x2_ref.at[2:4], bf_ref[...])
+        12,
+    )
+    for g0, rows, p in ((0, 7, pump), (7, 8, idle)):
+        first_rows(u_ref, w_ref, f45_ref, o_ref, PAIR45, g0, rows, None, None, None, p)
+        first_rows(u_ref, w_ref, f23_ref, o_ref, PAIR23, g0, rows, None, x2_ref.at[2:4], bf_ref[...], p)
+        first_rows(u_ref, w_ref, f01_ref, o_ref, PAIR01, g0, rows, None, x2_ref.at[0:2], bf_ref[...], p)
     for n in (0, 1, 3, 4):
         rest[n].wait()
 
@@ -203,13 +206,15 @@
         part_ref[q] = out[q].reshape(9, 64, 256).astype(BF)
 
 
-def kernel_late(ok_ref, u_ref, x2_ref, f_in, w_ref, kd_ref, bf_ref, bd_ref, f_ref, red_ref, o_ref):
+def kernel_late(ok_ref, u_ref, x2_ref, f_in, w_ref, kd_ref, bf_ref, bd_ref, f_ref, red_ref, dn_ref, o_ref):
     clear_shift(o_ref)
     below = ok_ref[1].astype(F32)
     first_rows(u_ref, w_ref, f_ref, o_ref, PAIR23, 15, 3, below, x2_ref.at[2:4], bf_ref[...])
     out = down_conv(f_ref, kd_ref)
     for q in range(2):
         red_ref[q] = (out[q] + bd_ref[...]).astype(BF).reshape(9, 64, 256)
+        for n in range(2):
+            dn_ref[q, n] = red_ref[q, 7 + n]
 
 
 def prep_mid(act, f, to, u_ref, s_ref, q_ref):
@@ -233,13 +238,11 @@
 
 
 def kernel_early(
-    ok_ref, u_ref, x2_ref, w_ref, kd_ref, bf_ref, bd_ref, ks_ref, red_ref, p_ref, u2_ref, g_ref, f_ref, o_ref, s_ref, q_ref
+    ok_ref, u_ref, x2_ref, f_in, w_ref, kd_ref, bf_ref, bd_ref, ks_ref, red_ref, f_ref, p_ref, u2_ref, g_ref, o_ref, s_ref, q_ref
 ):
     clear_shift(o_ref)
     clear_edges(s_ref)
     below = ok_ref[1].astype(F32)
-    for q in range(2):
-        f_ref[q, 1, 0] = jnp.zeros((64, 384), BF)
 
     def weights(i, j):
         a, b = transformed(*(ks_ref[i, j, c].astype(F32) for c in range(3)))
@@ -248,21 +251,19 @@
 
     work = [lambda f=f, r=r: own_row(ok_ref, red_ref, f, r, u2_ref, s_ref, q_ref) for r in range(1, 9) for f in (2, 3)]
     work += [lambda i=i, j=j: weights(i, j) for i in range(3) for j in range(3)]
-    pump = Pump(work, 8)
-    for g0 in (0, 9):
-        first_rows(u_ref, w_ref, f_ref, o_ref, PAIR01, g0, 9, below, x2_ref.at[0:2], bf_ref[...], pump)
-    out = down_conv(f_ref, kd_ref)
+    pump = Pump(work, 6)
+    first_rows(u_ref, w_ref, f_ref, o_ref, PAIR01, 15, 3, below, x2_ref.at[0:2], bf_ref[...], pump)
+    out = down_conv(f_ref, kd_ref, pump)
     for q in range(2):
         p_ref[q] = (out[q] + bd_ref[...]).reshape(9, 64, 256)
 
 
-def kernel_join(p_ref, z_ref, red23_ref, red_ref, dn_ref):
+def kernel_join(p_ref, z_ref, red_ref, dn_ref):
     for q in range(2):
         for r in range(9):
             red_ref[q, r] = (p_ref[q, r] + z_ref[q, r].astype(F32)).astype(BF)
         for n in range(2):
             dn_ref[q, n] = red_ref[q, 7 + n]
-            dn_ref[2 + q, n] = red23_ref[q, 7 + n]
 
 
 def taps(ks_ref, g_ref, k, i):
@@ -278,94 +279,96 @@
         t_ref[(*at, h, pl.ds(1, 32, stride=2), slice(None))] = y1[:, lanes]
 
 
-def outer_pairs(u_ref, ks_ref, g_ref, r0, rows, zl_ref, y_ref, t_ref, pump=idle):
-    n = rows * 32
-
-    def lhs(k, a, b):
-        return jnp.concatenate(
-            [
-                jnp.concatenate([u_ref[k, f, r0 + j : r0 + j + rows].reshape(n, 256) for f in (a, b)], axis=0)
-                for j in range(3)
-            ],
-            axis=1,
-        )
-
-    first, later, own = [], [], []
+def frames_lhs(u_ref, k, f, count, r0, rows):
+    return jnp.concatenate(
+        [u_ref[k, f : f + count, r0 + j : r0 + j + rows].reshape(count * rows * 32, 256) for j in range(3)], axis=1
+    )
+
+
+def mixed(ms, rows):
+    y0 = (ms[1] + ms[2] + ms[0]).reshape(rows, 32, 256)
+    y1 = (ms[1] - ms[2] - ms[3]).reshape(rows, 32, 256)
+    return y0, y1
+
+
+def halo_rows(ok_ref, halo_ref, red_ref, frames, u_ref, s_ref, q_ref):
+    for n, f in enumerate(frames):
+        own = red_ref[n, 0].astype(F32)
+        above = jnp.where(ok_ref[0] > 0, halo_ref[n, 1].astype(F32), own)
+        prep_mid(silu(halo_ref[n, 0].astype(F32)), f, (f, 0), u_ref, s_ref, q_ref)
+        prep_mid(silu(above), f, (f, 1), u_ref, s_ref, q_ref)
+
+
+def kernel_next(ok_ref, u_in, halo_ref, red_ref, ks_ref, g_ref, u_ref, zl_ref, s_ref, q_ref, t_ref):
+    clear_edges(s_ref)
+    halo_rows(ok_ref, halo_ref, red_ref, (2, 3), u_ref, s_ref, q_ref)
+    ms = ([], [])
     for k in range(4):
-        first.append(jnp.dot(lhs(k, 2, 3), taps(ks_ref, g_ref, k, 0), preferred_element_type=F32))
-        pump()
-    for k in range(4):
-        d1 = jnp.dot(lhs(k, 3, 0), taps(ks_ref, g_ref, k, 1), preferred_element_type=F32)
-        d2 = jnp.dot(lhs(k, 0, 1), taps(ks_ref, g_ref, k, 2), preferred_element_type=F32)
-        later.append((first[k][:n] + d1[:n], first[k][n:]))
-        own.append((d2[:n], d2[n:] + d1[n:]))
+        d0 = jnp.dot(frames_lhs(u_ref, k, 2, 2, 0, 8), taps(ks_ref, g_ref, k, 0), preferred_element_type=F32)
+        d1 = jnp.dot(frames_lhs(u_ref, k, 3, 1, 0, 8), taps(ks_ref, g_ref, k, 1), preferred_element_type=F32)
+        ms[0].append(d0[:256] + d1)
+        ms[1].append(d0[256:])
     for f in range(2):
-        for ms, to in ((later, t_ref), (own, y_ref)):
-            y0 = (ms[1][f] + ms[2][f] + ms[0][f]).reshape(rows, 32, 256)
-            y1 = (ms[1][f] - ms[2][f] - ms[3][f]).reshape(rows, 32, 256)
-            for r in range(rows):
-                columns(to, (f, r0 + r), y0[r], y1[r])
-        for r in range(r0, r0 + rows):
+        y0, y1 = mixed(ms[f], 8)
+        for r in range(8):
+            columns(t_ref, (f, r), y0[r], y1[r])
             for h in range(2):
                 zl_ref[f, r, :, h * 128 : h * 128 + 128] = t_ref[f, r, h].astype(BF)
 
 
-def kernel_inner(ok_ref, u_in, red01_ref, ks_ref, g_ref, u_ref, zl_ref, y_ref, s_ref, q_ref, t_ref):
-    clear_edges(s_ref)
-    work = [lambda f=f, r=r: own_row(ok_ref, red01_ref, f, r, u_ref, s_ref, q_ref) for r in range(1, 9) for f in (0, 1)]
-    outer_pairs(u_ref, ks_ref, g_ref, 2, 6, zl_ref, y_ref, t_ref, Pump(work, 4))
-
-
-def kernel_edge(
-    ok_ref, u_in, zl_in, y_in, halo_ref, red01_ref, red23_ref, ks_ref, g_ref, u_ref, zl_ref, y_ref, s_ref, q_ref, t_ref
+def kernel_same(ok_ref, u_in, red_ref, ks_ref, g_ref, u_ref, y_ref, s_ref, q_ref):
+    clear_edges(s_ref)
+    work = [lambda f=f, r=r: own_row(ok_ref, red_ref, f, r, u_ref, s_ref, q_ref) for r in range(1, 9) for f in (0, 1)]
+    pump = Pump(work, 4)
+    ms = ([], [])
+    for k in range(4):
+        d2 = jnp.dot(frames_lhs(u_ref, k, 2, 2, 0, 8), taps(ks_ref, g_ref, k, 2), preferred_element_type=F32)
+        d1 = jnp.dot(frames_lhs(u_ref, k, 2, 1, 0, 8), taps(ks_ref, g_ref, k, 1), preferred_element_type=F32)
+        ms[0].append(d2[:256])
+        ms[1].append(d2[256:] + d1)
+        pump()
+    for f in range(2):
+        y0, y1 = mixed(ms[f], 8)
+        for r in range(8):
+            columns(y_ref, (f, r), y0[r], y1[r])
+
+
+def kernel_last(
+    ok_ref, u_in, halo01_ref, halo23_ref, red01_ref, red23_ref, y_ref, zl_ref, ks_ref, g_ref, bs_ref,
+    lat_ref, u_ref, s_ref, q_ref, t_ref, out_ref, sem,
 ):
     clear_edges(s_ref)
+    halo_rows(ok_ref, halo01_ref, red01_ref, (0, 1), u_ref, s_ref, q_ref)
     inner = ok_ref[0] > 0
-    for f in range(4):
-        own = (red01_ref, red23_ref)[f // 2][f % 2, 0].astype(F32)
-        above = jnp.where(inner, halo_ref[f, 1].astype(F32), own)
-        prep_mid(silu(halo_ref[f, 0].astype(F32)), f, (f, 0), u_ref, s_ref, q_ref)
-        prep_mid(silu(above), f, (f, 1), u_ref, s_ref, q_ref)
-    outer_pairs(u_ref, ks_ref, g_ref, 0, 2, zl_ref, y_ref, t_ref)
-
-
-def kernel_mid_late(ok_ref, u_ref, halo_ref, ks_ref, g_ref, red_ref, bs_ref, out_ref, t_ref):
-    inner = ok_ref[0] > 0
-    ms = []
-    for k in range(4):
-        lhs = jnp.concatenate(
-            [u_ref[k, i : i + 2, j : j + 8].reshape(512, 256) for i in range(3) for j in range(3)], axis=1
-        )
-        rhs = jnp.concatenate([taps(ks_ref, g_ref, k, i) for i in range(3)], axis=0)
-        ms.append(jnp.dot(lhs, rhs, preferred_element_type=F32))
-    y0 = (ms[1] + ms[2] + ms[0]).reshape(2, 8, 32, 256)
-    y1 = (ms[1] - ms[2] - ms[3]).reshape(2, 8, 32, 256)
-    for f in range(2):
-        for r in range(8):
-            columns(t_ref, (f, r), y0[f, r], y1[f, r])
-            for h in range(2):
-                lanes = slice(h * 128, h * 128 + 128)
-                v = red_ref[f, r, :, lanes].astype(F32)
-                if r == 0:
-                    v = jnp.where(inner, halo_ref[2 + f, 1, :, lanes].astype(F32), v)
-                out_ref[f, r, :, lanes] = (t_ref[f, r, h] + v + bs_ref[:, lanes]).astype(BF)
-
-
-def kernel_last(ok_ref, late_ref, y_ref, zl_ref, halo_ref, red_ref, bs_ref, lat_ref, out_ref, sem):
-    inner = ok_ref[0] > 0
-    copies = [pltpu.make_async_copy(late_ref, lat_ref.at[2:4], sem.at[0])]
-    copies[0].start()
-    for f in range(2):
-        for r in range(8):
-            for h in range(2):
-                lanes = slice(h * 128, h * 128 + 128)
-                v = red_ref[f, r, :, lanes].astype(F32)
-                if r == 0:
-                    v = jnp.where(inner, halo_ref[f, 1, :, lanes].astype(F32), v)
-                v = v + zl_ref[f, r, :, lanes].astype(F32) + bs_ref[:, lanes]
-                out_ref[f, r, :, lanes] = (y_ref[f, r, h] + v).astype(BF)
-        copies.append(pltpu.make_async_copy(out_ref.at[f], lat_ref.at[f], sem.at[1 + f]))
-        copies[-1].start()
+    copies = []
+    for r0 in range(0, 8, STEP):
+        n = STEP * 32
+        ms = ([], [], [], [])
+        for k in range(4):
+            lhs = frames_lhs(u_ref, k, 0, 2, r0, STEP)
+            e0, e1, e2 = (jnp.dot(lhs, taps(ks_ref, g_ref, k, i), preferred_element_type=F32) for i in range(3))
+            ms[0].append(e2[:n])
+            ms[1].append(e2[n:] + e1[:n])
+            ms[2].append(e1[n:] + e0[:n])
+            ms[3].append(e0[n:])
+        for f in range(4):
+            y0, y1 = mixed(ms[f], STEP)
+            red_ref, halo_ref = ((red01_ref, halo01_ref), (red23_ref, halo23_ref))[f // 2]
+            for r in range(r0, r0 + STEP):
+                columns(t_ref, (f, r), y0[r - r0], y1[r - r0])
+                for h in range(2):
+                    lanes = slice(h * 128, h * 128 + 128)
+                    v = red_ref[f % 2, r, :, lanes].astype(F32)
+                    if r == 0:
+                        v = jnp.where(inner, halo_ref[f % 2, 1, :, lanes].astype(F32), v)
+                    if f < 2:
+                        v = v + zl_ref[f, r, :, lanes].astype(F32)
+                    else:
+                        v = v + y_ref[f - 2, r, h]
+                    out_ref[f, r, :, lanes] = (t_ref[f, r, h] + v + bs_ref[:, lanes]).astype(BF)
+            rows = pl.ds(r0, STEP)
+            copies.append(pltpu.make_async_copy(out_ref.at[f, rows], lat_ref.at[f, rows], sem.at[len(copies)]))
+            copies[-1].start()
     for c in copies:
         c.wait()
 
@@ -420,11 +423,11 @@
     shift = lambda n: VMEM((2, n, 72, 128), F32)
     fshape, ushape, u2shape = (2, 2, 10, 64, 384), (4, 2, 20, 64, 256), (4, 4, 10, 32, 256)
     yshape = (2, 8, 2, 64, 128)
-    u, x2, w, ksv, kdv, bfv, bdv, bsv, f45, f23 = call(
+    u, x2, w, ksv, kdv, bfv, bdv, bsv, f45, f23, f01 = call(
         kernel_own, "own", far(features, kf, ks, kd, bf.reshape(1, 128), bd.reshape(1, 256), bs.reshape(1, 256)),
         [
             res(*ushape), res(4, 18, 64, 256), res(4, 3, 2, 256, 256), res(3, 3, 3, 256, 256), res(3, 3, 128, 256),
-            res(1, 128, dtype=F32), res(1, 256, dtype=F32), res(1, 256, dtype=F32), res(*fshape), res(*fshape),
+            res(1, 128, dtype=F32), res(1, 256, dtype=F32), res(1, 256, dtype=F32), *[res(*fshape)] * 3,
         ],
         [VMEM((4, 16, 128, 128), BF), VMEM((3, 3, 3, 128, 128), BF), *wide, shift(8), pltpu.SemaphoreType.DMA((10,))],
         6_000_000_000, in_specs=[HBM] * 7,
@@ -435,39 +438,37 @@
         [*wide, shift(3)], 2_000_000_000, in_specs=[SM] + [V] * 6, aliases={1: 0, 2: 1, 3: 2},
     )
     zpart = lax.ppermute(part, "tm", later)
-    _, red23 = call(
+    _, red23, dn23 = call(
         kernel_late, "late", (ok, *keep(u, x2, f23, w, kdv, bfv, bdv)),
-        [res(*fshape), res(2, 9, 64, 256)],
+        [res(*fshape), res(2, 9, 64, 256), sds(2, 2, 64, 256)],
         [shift(3)], 2_500_000_000, in_specs=[SM] + [V] * 7, aliases={3: 0},
     )
-    p01, u2, g = call(
-        kernel_early, "early", (ok, *keep(u, x2, w, kdv, bfv, bdv, ksv, red23)),
-        [res(2, 9, 64, 256, dtype=F32), res(*u2shape), res(2, 3, 3, 256, 256)],
-        [VMEM(fshape, BF), shift(9), *half], 3_000_000_000, in_specs=[SM] + [V] * 8,
-    )
-    red01, dn = call(
-        kernel_join, "join", (*keep(p01), zpart, *keep(red23)), [res(2, 9, 64, 256), sds(4, 2, 64, 256)], [], 500_000_000
-    )
-    halo_mid = lax.ppermute(dn, "space", down)
-    u2, zl, y = call(
-        kernel_inner, "inner", (ok, *keep(u2, red01, ksv, g)),
-        [res(*u2shape), res(2, 8, 64, 256), res(*yshape, dtype=F32)],
-        [*half, VMEM(yshape, F32)], 3_000_000_000, in_specs=[SM] + [V] * 4, aliases={1: 0},
-    )
-    u2, zl, y = call(
-        kernel_edge, "edge", (ok, *keep(u2, zl, y), halo_mid, *keep(red01, red23, ksv, g)),
-        [res(*u2shape), res(2, 8, 64, 256), res(*yshape, dtype=F32)],
-        [*half, VMEM(yshape, F32)], 1_500_000_000, in_specs=[SM] + [V] * 8, aliases={1: 0, 2: 1, 3: 2},
+    halo23 = lax.ppermute(dn23, "space", down)
+    _, p01, u2, g = call(
+        kernel_early, "early", (ok, *keep(u, x2, f01, w, kdv, bfv, bdv, ksv, red23)),
+        [res(*fshape), res(2, 9, 64, 256, dtype=F32), res(*u2shape), res(2, 3, 3, 256, 256)],
+        [shift(3), *half], 3_000_000_000, in_specs=[SM] + [V] * 9, aliases={3: 0},
+    )
+    u2, zl = call(
+        kernel_next, "next", (ok, *keep(u2), halo23, *keep(red23, ksv, g)),
+        [res(*u2shape), sds(2, 8, 64, 256)],
+        [*half, VMEM(yshape, F32)], 2_000_000_000, in_specs=[SM] + [V] * 5, aliases={1: 0},
     )
     zlat = lax.ppermute(zl, "tm", later)
-    late = call(
-        kernel_mid_late, "mid_late", (ok, *keep(u2), halo_mid, *keep(ksv, g, red23, bsv)),
-        [res(2, 8, 64, 256)], [VMEM(yshape, F32)], 4_000_000_000, in_specs=[SM] + [V] * 6,
-    )
-    (lat,) = call(
-        kernel_last, "last", (ok, *keep(late[0], y), zlat, halo_mid, *keep(red01, bsv)),
-        [sds(4, 8, 64, 256)], [VMEM((2, 8, 64, 256), BF), pltpu.SemaphoreType.DMA((3,))],
-        500_000_000, in_specs=[SM] + [V] * 6, out_specs=[HBM],
+    red01, dn01 = call(
+        kernel_join, "join", (*keep(p01), zpart), [res(2, 9, 64, 256), sds(2, 2, 64, 256)], [], 500_000_000
+    )
+    halo01 = lax.ppermute(dn01, "space", down)
+    u2, y = call(
+        kernel_same, "same", (ok, *keep(u2, red01, ksv, g)),
+        [res(*u2shape), res(*yshape, dtype=F32)],
+        half, 2_000_000_000, in_specs=[SM] + [V] * 4, aliases={1: 0},
+    )
+    lat, _ = call(
+        kernel_last, "last", (ok, *keep(u2), halo01, halo23, *keep(red01, red23, y), zlat, *keep(ksv, g, bsv)),
+        [sds(4, 8, 64, 256), res(*u2shape)],
+        [*half, VMEM((4, 8, 2, 64, 128), F32), VMEM((4, 8, 64, 256), BF), pltpu.SemaphoreType.DMA((4 * 8 // STEP,))],
+        4_000_000_000, in_specs=[SM] + [V] * 10, out_specs=[HBM, V], aliases={1: 1},
     )
     return lat
 

time: 55.5 us -> 53.5 us (0.964); the launches traced: 54.7 us -> 53.3 us
  waiting for transfers between devices: 10.5 us -> 6.3 us
  starting transfers between devices: 16.1 us -> 18.9 us
    ppermute x1 -> x2, waiting for transfers between devices: 7.58 us -> 4.41 us  [the longest x1 2.56 us: on_device(): halo23 = lax.ppermute(dn23, 'space', down)]
    ppermute x1 -> x2, starting transfers between devices: 2.1 us -> 4.02 us  [the longest x1 2.1 us: on_device(): halo23 = lax.ppermute(dn23, 'space', down)]
    ppermute x1, waiting for transfers between devices: 2.79 us -> 1.89 us  [on_device(): zlat = lax.ppermute(zl, 'tm', later)]
    ppermute x1, starting transfers between devices: 3.46 us -> 4.33 us  [on_device(): zlat = lax.ppermute(zl, 'tm', later)]
    pallas_call x9 -> x8, Pallas kernels: 26.8 us -> 26.8 us  [call(): pl.pallas_call(body, out_shape=outs, in_specs=in_specs or [V] * len(ins),...]
  transfers between devices with their start and end apart: 4 -> 5, of which waited for: 3 -> 3; matrix products, arithmetic and copies ran while one was open for 0% -> 0% of each run, Pallas kernels for 39% -> 38%
where the time goes in v2:
time: 53.5 us; the launch traced here: 53.3 us
  Pallas kernels  26.8 us (50%)
  starting transfers between devices  18.9 us (35%)
  waiting for transfers between devices  6.3 us (12%)
  local copies, waits for them, and re-layouts  1.02 us (2%)
    pallas_call x8, Pallas kernels, call(): pl.pallas_call(body, out_shape=outs, in_specs=in_specs or [V] * len(ins),...  26.8 us
    ppermute x1, starting transfers between devices, on_device(): zpart = lax.ppermute(part, 'tm', later)  5.6 us
    ppermute x1, starting transfers between devices, on_device(): halo = lax.ppermute(features[:, 0:3], 'space', up)  4.91 us
    ppermute x1, starting transfers between devices, on_device(): zlat = lax.ppermute(zl, 'tm', later)  4.33 us
    ppermute x1, waiting for transfers between devices, on_device(): halo23 = lax.ppermute(dn23, 'space', down)  2.56 us
    ppermute x1, starting transfers between devices, on_device(): halo23 = lax.ppermute(dn23, 'space', down)  2.1 us
    ppermute x1, starting transfers between devices, on_device(): halo01 = lax.ppermute(dn01, 'space', down)  1.92 us
    ppermute x1, waiting for transfers between devices, on_device(): zlat = lax.ppermute(zl, 'tm', later)  1.89 us
  transfers between devices with their start and end apart: 5, of which 3 were waited for; matrix products, arithmetic and copies ran while one was open for 0% of the time, Pallas kernels for 38%

profile of v2, /device:TPU:103, one launch (start us, length us, event | category | flops | bytes accessed | tf_op | source)
XLA Modules:
  0.0 53.3 jit_solution(13825830501493761244)
XLA Ops:
  0.0 1.0 %slice.3 = bf16[4,3,128,128]{3,2,1,0:T(8,128)(2,1)S(1)} slice(bf16[4,16,128,128]{3,2,1,0:T(8,128)(2,1)} %x_hbm.1), slice={[0:4], [0:3], [0:128], [0:128]} | slice | bytes 786432 | tf_op jit(solution)/shard_map/slice | solution.py:420
  1.0 4.9 %collective-permute-start = (bf16[4,3,128,128]{3,2,1,0:T(8,128)(2,1)S(1)}, bf16[4,3,128,128]{3,2,1,0:T(8,128)(2,1)S(1)}, u32[]{:S(2)}, u32[]{:S(2)}) collective-permute-start(bf16[4,3,128,128]{3,2,1,0:T(8,128)(2,1)S(1)} %slice.3), channel_id=1, source_target_pairs={{1,0},{2,1},{3,2},{4,3},{5,4},{6,5},{7,6},{8,7},{9,8},{10,9},{11,1... | collective-permute-start | bytes 1179656 | tf_op jit(solution)/shard_map/ppermute | solution.py:420
  5.9 0.1 add_convert_fusion.ok_ref
  6.0 10.7 %own.1 = (bf16[4,2,20,64,256]{4,3,2,1,0:T(8,128)(2,1)S(1)}, bf16[4,18,64,256]{3,2,1,0:T(8,128)(2,1)S(1)}, bf16[4,3,2,256,256]{4,3,2,1,0:T(8,128)(2,1)S(1)}, bf16...) custom-call(bf16[4,16,128,128]{3,2,1,0:T(8,128)(2,1)} %x_hbm.1, ...), custom_call_target="tpu_custom_call" | custom-call | flops 6000000000 | bytes 4194304 | tf_op jit(solution)/shard_map/own/pallas_call | solution.py:399
  16.7 0.0 collective-permute-done.halo_ref
  16.8 2.1 %ahead.1 = (bf16[4,2,20,64,256]{4,3,2,1,0:T(8,128)(2,1)S(1)}, bf16[4,18,64,256]{3,2,1,0:T(8,128)(2,1)S(1)}, bf16[2,2,10,64,384]{4,3,2,1,0:T(8,128)(2,1)S(1)}, bf16[2,9,64,256]{3,2,1,0:T(8,128)(2,1)S(1)}) custom-call(s32[2]{0:T(128)S(1)} %add_convert_fusion.ok_ref, ...), custom_call_target="tpu_custom_call", output_to_operand_aliasing={{0}: (1, {}), {1}: (2, {}), {2}: (3, {})} | custom-call | flops 2000000000 | bytes 4194304 | tf_op jit(solution)/shard_map/ahead/pallas_call | solution.py:399
  18.8 5.6 %collective-permute-start.2 = (bf16[2,9,64,256]{3,2,1,0:T(8,128)(2,1)S(1)}, bf16[2,9,64,256]{3,2,1,0:T(8,128)(2,1)S(1)}, u32[]{:S(2)}, u32[]{:S(2)}) collective-permute-start(bf16[2,9,64,256]{3,2,1,0:T(8,128)(2,1)S(1)} %get-tuple-element.49), channel_id=1, source_target_pairs={{0,16},{16,32},{32,48},{48,64},{64,80},{80,96},{96,112},{112,128},... | collective-permute-start | bytes 1769480 | tf_op jit(solution)/shard_map/ppermute | solution.py:440
  24.4 2.1 %late.1 = (bf16[2,2,10,64,384]{4,3,2,1,0:T(8,128)(2,1)S(1)}, bf16[2,9,64,256]{3,2,1,0:T(8,128)(2,1)S(1)}, bf16[2,2,64,256]{3,2,1,0:T(8,128)(2,1)S(1)}) custom-call(s32[2]{0:T(128)S(1)} %add_convert_fusion.ok_ref, bf16[4,2,20,64,256]{4,3,2,1,0:T(8,128)(2,1)S(1)} %get-tuple-element.36.u_ref, ...), custom_call_target="tpu_custom_call", output_to_operand_aliasing={{0}: (3, {})} | custom-call | flops 2500000000 | bytes 4194304 | tf_op jit(solution)/shard_map/late/pallas_call | solution.py:399
  26.6 2.1 %collective-permute-start.1 = (bf16[2,2,64,256]{3,2,1,0:T(8,128)(2,1)S(1)}, bf16[2,2,64,256]{3,2,1,0:T(8,128)(2,1)S(1)}, u32[]{:S(2)}, u32[]{:S(2)}) collective-permute-start(bf16[2,2,64,256]{3,2,1,0:T(8,128)(2,1)S(1)} %get-tuple-element.45), channel_id=1, source_target_pairs={{0,1},{1,2},{2,3},{3,4},{4,5},{5,6},{6,7},{7,8},{8,9},{9,10},{10,1... | collective-permute-start | bytes 393224 | tf_op jit(solution)/shard_map/ppermute | solution.py:446
  28.7 3.1 %early.1 = (bf16[2,2,10,64,384]{4,3,2,1,0:T(8,128)(2,1)S(1)}, f32[2,9,64,256]{3,2,1,0:T(8,128)S(1)}, bf16[4,4,10,32,256]{4,3,2,1,0:T(8,128)(2,1)S(1)}, bf16[2,3,3,256,256]{4,3,2,1,0:T(8,128)(2,1)S(1)}) custom-call(s32[2]{0:T(128)S(1)} %add_convert_fusion.ok_ref, ...), custom_call_target="tpu_custom_call", output_to_operand_aliasing={{0}: (3, {})} | custom-call | flops 3000000000 | bytes 4194304 | tf_op jit(solution)/shard_map/early/pallas_call | solution.py:399
  31.8 2.6 %collective-permute-done.1.halo_ref.halo23_ref = bf16[2,2,64,256]{3,2,1,0:T(8,128)(2,1)S(1)} collective-permute-done((bf16[2,2,64,256]{3,2,1,0:T(8,128)(2,1)S(1)}, bf16[2,2,64,256]{3,2,1,0:T(8,128)(2,1)S(1)}, u32[]{:S(2)}, u32[]{:S(2)}) %collective-permute-start.1) | collective-permute-done | bytes 131104 | tf_op jit(solution)/shard_map/ppermute | solution.py:446
  34.4 2.1 %next.1 = (bf16[4,4,10,32,256]{4,3,2,1,0:T(8,128)(2,1)S(1)}, bf16[2,8,64,256]{3,2,1,0:T(8,128)(2,1)S(1)}) custom-call(s32[2]{0:T(128)S(1)} %add_convert_fusion.ok_ref, bf16[4,4,10,32,256]{4,3,2,1,0:T(8,128)(2,1)S(1)} %get-tuple-element.44.u_in, ...), custom_call_target="tpu_custom_call", output_to_operand_aliasing={{0}: (1, {})} | custom-call | flops 2000000000 | bytes 4194304 | tf_op jit(solution)/shard_map/next/pallas_call | solution.py:399
  36.5 4.3 %collective-permute-start.4 = (bf16[2,8,64,256]{3,2,1,0:T(8,128)(2,1)S(1)}, bf16[2,8,64,256]{3,2,1,0:T(8,128)(2,1)S(1)}, u32[]{:S(2)}, u32[]{:S(2)}) collective-permute-start(bf16[2,8,64,256]{3,2,1,0:T(8,128)(2,1)S(1)} %get-tuple-element.54), channel_id=1, source_target_pairs={{0,16},{16,32},{32,48},{48,64},{64,80},{80,96},{96,112},{112,128},... | collective-permute-start | bytes 1572872 | tf_op jit(solution)/shard_map/ppermute | solution.py:457
  40.8 0.0 collective-permute-done.2.z_ref
  40.8 0.1 join.1
  40.9 1.9 %collective-permute-start.3 = (bf16[2,2,64,256]{3,2,1,0:T(8,128)(2,1)S(1)}, bf16[2,2,64,256]{3,2,1,0:T(8,128)(2,1)S(1)}, u32[]{:S(2)}, u32[]{:S(2)}) collective-permute-start(bf16[2,2,64,256]{3,2,1,0:T(8,128)(2,1)S(1)} %get-tuple-element.52), channel_id=1, source_target_pairs={{0,1},{1,2},{2,3},{3,4},{4,5},{5,6},{6,7},{7,8},{8,9},{9,10},{10,1... | collective-permute-start | bytes 393224 | tf_op jit(solution)/shard_map/ppermute | solution.py:461
  42.9 2.2 %same.1 = (bf16[4,4,10,32,256]{4,3,2,1,0:T(8,128)(2,1)S(1)}, f32[2,8,2,64,128]{4,3,2,1,0:T(8,128)S(1)}) custom-call(s32[2]{0:T(128)S(1)} %add_convert_fusion.ok_ref, bf16[4,4,10,32,256]{4,3,2,1,0:T(8,128)(2,1)S(1)} %get-tuple-element.47.u_in, bf16[2,9,64,256]{3,2,1,0:T(8,128)(2,1)S(1)} %get-tuple-element.50.red_ref.red01_ref, ...), custom_call_target="tpu_custom_call", output_to_operand_aliasing={{0}: (1, {})} | custom-call | flops 2000000000 | bytes 4194304 | tf_op jit(solution)/shard_map/same/pallas_call | solution.py:399
  45.0 1.9 %collective-permute-done.4.zl_ref = bf16[2,8,64,256]{3,2,1,0:T(8,128)(2,1)S(1)} collective-permute-done((bf16[2,8,64,256]{3,2,1,0:T(8,128)(2,1)S(1)}, bf16[2,8,64,256]{3,2,1,0:T(8,128)(2,1)S(1)}, u32[]{:S(2)}, u32[]{:S(2)}) %collective-permute-start.4) | collective-permute-done | bytes 524320 | tf_op jit(solution)/shard_map/ppermute | solution.py:457
  46.9 1.8 %collective-permute-done.3.halo01_ref = bf16[2,2,64,256]{3,2,1,0:T(8,128)(2,1)S(1)} collective-permute-done((bf16[2,2,64,256]{3,2,1,0:T(8,128)(2,1)S(1)}, bf16[2,2,64,256]{3,2,1,0:T(8,128)(2,1)S(1)}, u32[]{:S(2)}, u32[]{:S(2)}) %collective-permute-start.3) | collective-permute-done | bytes 131104 | tf_op jit(solution)/shard_map/ppermute | solution.py:461
  48.8 4.4 %last.1 = (bf16[4,8,64,256]{3,2,1,0:T(8,128)(2,1)}, bf16[4,4,10,32,256]{4,3,2,1,0:T(8,128)(2,1)S(1)}) custom-call(s32[2]{0:T(128)S(1)} %add_convert_fusion.ok_ref, bf16[4,4,10,32,256]{4,3,2,1,0:T(8,128)(2,1)S(1)} %get-tuple-element.51.u_in, bf16[2,2,64,256]{3,2,1,0:T(8,128)(2,1)S(1)} %collective-permute-done.3.halo01_ref, ...), custom_call_target="tpu_custom_call", output_to_operand_aliasing={{1}: (1, {})} | custom-call | flops 4000000000 | bytes 4194304 | tf_op jit(solution)/shard_map/last/pallas_call | solution.py:399
Async XLA Ops:
  1.0 15.7 %collective-permute-start = (bf16[4,3,128,128]{3,2,1,0:T(8,128)(2,1)S(1)}, bf16[4,3,128,128]{3,2,1,0:T(8,128)(2,1)S(1)}, u32[]{:S(2)}, u32[]{:S(2)}) collective-permute-start(bf16[4,3,128,128]{3,2,1,0:T(8,128)(2,1)S(1)} %slice.3), channel_id=1, source_target_pairs={{1,0},{2,1},{3,2},{4,3},{5,4},{6,5},{7,6},{8,7},{9,8},{10,9},{11,1... | collective-permute-start | bytes 1179656 | tf_op jit(solution)/shard_map/ppermute | solution.py:420
  18.8 22.0 %collective-permute-start.2 = (bf16[2,9,64,256]{3,2,1,0:T(8,128)(2,1)S(1)}, bf16[2,9,64,256]{3,2,1,0:T(8,128)(2,1)S(1)}, u32[]{:S(2)}, u32[]{:S(2)}) collective-permute-start(bf16[2,9,64,256]{3,2,1,0:T(8,128)(2,1)S(1)} %get-tuple-element.49), channel_id=1, source_target_pairs={{0,16},{16,32},{32,48},{48,64},{64,80},{80,96},{96,112},{112,128},... | collective-permute-start | bytes 1769480 | tf_op jit(solution)/shard_map/ppermute | solution.py:440
  26.6 7.8 %collective-permute-start.1 = (bf16[2,2,64,256]{3,2,1,0:T(8,128)(2,1)S(1)}, bf16[2,2,64,256]{3,2,1,0:T(8,128)(2,1)S(1)}, u32[]{:S(2)}, u32[]{:S(2)}) collective-permute-start(bf16[2,2,64,256]{3,2,1,0:T(8,128)(2,1)S(1)} %get-tuple-element.45), channel_id=1, source_target_pairs={{0,1},{1,2},{2,3},{3,4},{4,5},{5,6},{6,7},{7,8},{8,9},{9,10},{10,1... | collective-permute-start | bytes 393224 | tf_op jit(solution)/shard_map/ppermute | solution.py:446
  36.5 10.4 %collective-permute-start.4 = (bf16[2,8,64,256]{3,2,1,0:T(8,128)(2,1)S(1)}, bf16[2,8,64,256]{3,2,1,0:T(8,128)(2,1)S(1)}, u32[]{:S(2)}, u32[]{:S(2)}) collective-permute-start(bf16[2,8,64,256]{3,2,1,0:T(8,128)(2,1)S(1)} %get-tuple-element.54), channel_id=1, source_target_pairs={{0,16},{16,32},{32,48},{48,64},{64,80},{80,96},{96,112},{112,128},... | collective-permute-start | bytes 1572872 | tf_op jit(solution)/shard_map/ppermute | solution.py:457
  40.9 7.8 %collective-permute-start.3 = (bf16[2,2,64,256]{3,2,1,0:T(8,128)(2,1)S(1)}, bf16[2,2,64,256]{3,2,1,0:T(8,128)(2,1)S(1)}, u32[]{:S(2)}, u32[]{:S(2)}) collective-permute-start(bf16[2,2,64,256]{3,2,1,0:T(8,128)(2,1)S(1)} %get-tuple-element.52), channel_id=1, source_target_pairs={{0,1},{1,2},{2,3},{3,4},{4,5},{5,6},{6,7},{7,8},{8,9},{9,10},{10,1... | collective-permute-start | bytes 393224 | tf_op jit(solution)/shard_map/ppermute | solution.py:461

commit v3 on v2

v3 whole, which is shorter than its diff:
```python
import jax
import jax.numpy as jnp
from jax import lax
from jax.experimental import pallas as pl
from jax.experimental.pallas import tpu as pltpu
from jax.sharding import PartitionSpec as P

BF = jnp.bfloat16
F32 = jnp.float32
VMEM = pltpu.VMEM
LIMIT = 20 * 2**20
STEP = 4


def silu(v):
    h = 0.5 * v
    return h + h * jnp.tanh(h)


def clear_edges(s_ref):
    for f in range(s_ref.shape[0]):
        for e in range(2):
            s_ref[f, e, 0:8] = jnp.zeros((8, s_ref.shape[-1]), F32)
            s_ref[f, e, s_ref.shape[2] - 8 :] = jnp.zeros((8, s_ref.shape[-1]), F32)


def prep_first(x, f, r, u_ref, x2_ref, s_ref, q_ref, residual=True):
    q_ref[f] = x.astype(F32)
    even = q_ref[f, pl.ds(0, 64, stride=2), :]
    odd = q_ref[f, pl.ds(1, 64, stride=2), :]
    d1 = silu(even)
    d2 = silu(odd)
    s_ref[f, 0, 8:72] = d1
    s_ref[f, 1, 8:72] = d2
    d3 = s_ref[f, 0, 9:73]
    d0 = s_ref[f, 1, 7:71]
    lanes = slice((f % 2) * 128, (f % 2) * 128 + 128)
    for k, v in enumerate((d0 - d2, d1 + d2, d2 - d1, d1 - d3)):
        u_ref[k, f // 2, r + 4, :, lanes] = v.astype(BF)
    if residual:
        x2_ref[f, r + 3, :, 0:128] = even.astype(BF)
        x2_ref[f, r + 3, :, 128:256] = odd.astype(BF)


def transformed(g0, g1, g2):
    half = 0.5 * (g0 + g2)
    return half + 0.5 * g1, half - 0.5 * g1


class Pump:
    def __init__(self, work, slots):
        self.work, self.slots = list(work), slots

    def __call__(self):
        count = -(-len(self.work) // max(self.slots, 1))
        self.slots -= 1
        for _ in range(count):
            self.work.pop(0)()


def idle():
    pass


def first_rows(u_ref, w_ref, f_ref, o_ref, pairs, parts, masks, residual, bias, pump=idle):
    ms = []
    for k in range(4):
        lhs = jnp.concatenate(
            [
                jnp.concatenate([u_ref[k, p, g + j : g + j + n].reshape(n * 64, 256) for g, n in parts], axis=0)
                for j in range(3)
                for p, _ in pairs
            ],
            axis=1,
        )
        rhs = jnp.concatenate([w_ref[k, j, which] for j in range(3) for _, which in pairs], axis=0)
        ms.append(jnp.dot(lhs, rhs, preferred_element_type=F32))
        pump()
    both = (ms[1] + ms[2] + ms[0], ms[1] - ms[2] - ms[3])
    rows = [g + n for g, count in parts for n in range(count)]
    for q in range(2):
        for e in range(2):
            lanes = slice(e * 128, e * 128 + 128)
            y = both[e][:, q * 128 : q * 128 + 128].reshape(len(rows), 64, 128)
            for n, g in enumerate(rows):
                row = y[n]
                if residual is not None:
                    row = row + residual[q, g, :, lanes].astype(F32) + bias
                if g < 3:
                    row = row * masks[0]
                elif g > 18:
                    row = row * masks[1]
                f_ref[q, g % 2, g // 2, :, lanes] = row.astype(BF)
                if e == 1:
                    o_ref[q, n, 8:72] = row
                    f_ref[q, g % 2, g // 2, :, 256:384] = o_ref[q, n, 7:71].astype(BF)


def clear_shift(o_ref):
    for q in range(2):
        for n in range(o_ref.shape[1]):
            o_ref[q, n, 0:8] = jnp.zeros((8, 128), F32)


def down_conv(f_ref, kd_ref, pump=idle):
    rhs = jnp.concatenate([kd_ref[j, c] for j in range(3) for c in (1, 2, 0)], axis=0)
    out = []
    for q in range(2):
        lhs = jnp.concatenate(
            [
                f_ref[q, 0, 0:10].reshape(640, 384),
                f_ref[q, 1, 0:10].reshape(640, 384),
                f_ref[q, 0, 1:11].reshape(640, 384),
            ],
            axis=1,
        )
        out.append(jnp.dot(lhs, rhs, preferred_element_type=F32))
        pump()
    return out


PAIR01 = ((0, 1),)
PAIR23 = ((0, 0), (1, 1))
PAIR45 = ((1, 0),)


EDGES = ((0, 4), (18, 3))


def edge_masks(ok_ref):
    return ok_ref[0, :, 0:128], ok_ref[1, :, 0:128]


def kernel_load(ok_ref, x_hbm, kf_hbm, x_ref, kf_ref, top_ref, bot_ref, sem):
    copies = [
        pltpu.make_async_copy(x_hbm.at[:, 12:16], top_ref, sem.at[0]),
        pltpu.make_async_copy(x_hbm.at[:, 0:3], bot_ref, sem.at[1]),
        pltpu.make_async_copy(x_hbm, x_ref, sem.at[2]),
        pltpu.make_async_copy(kf_hbm, kf_ref, sem.at[3]),
    ]
    for c in copies:
        c.start()
    for c in copies:
        c.wait()


def kernel_own(
    ok_ref, x_ref, kf_ref, ks_hbm, kd_hbm, bf_hbm, bd_hbm, bs_hbm,
    u_ref, x2_ref, w_ref, ks_ref, g_ref, kd_ref, bf_ref, bd_ref, bs_ref, f45_ref, f23_ref, f01_ref,
    s_ref, q_ref, o_ref, sem,
):
    pairs = ((bf_hbm, bf_ref), (ks_hbm, ks_ref), (kd_hbm, kd_ref), (bd_hbm, bd_ref), (bs_hbm, bs_ref))
    copies = [pltpu.make_async_copy(a, b, sem.at[n]) for n, (a, b) in enumerate(pairs)]
    for c in copies:
        c.start()
    clear_edges(s_ref)
    clear_shift(o_ref)

    def row(r, carry):
        for f in range(4):
            prep_first(x_ref[f, r], f, r, u_ref, x2_ref, s_ref, q_ref)
        return carry

    lax.fori_loop(0, 9, row, 0)

    def wrow(j, carry):
        zero = jnp.zeros((128, 128), BF)
        for i in range(3):
            g0, g1, g2 = (kf_ref[i, j, c] for c in range(3))
            a, b = transformed(g0.astype(F32), g1.astype(F32), g2.astype(F32))
            for k, g in enumerate((g0, a.astype(BF), b.astype(BF), g2)):
                if i == 0:
                    w_ref[k, j, 0, 0:128, 0:128] = g
                    w_ref[k, j, 0, 128:256, 128:256] = g
                    w_ref[k, j, 0, 0:128, 128:256] = zero
                    w_ref[k, j, 1, 128:256, 0:128] = zero
                elif i == 1:
                    w_ref[k, j, 0, 128:256, 0:128] = g
                    w_ref[k, j, 1, 0:128, 128:256] = g
                else:
                    w_ref[k, j, 1, 0:128, 0:128] = g
                    w_ref[k, j, 1, 128:256, 128:256] = g
        return carry

    lax.fori_loop(0, 3, wrow, 0)
    for c in copies:
        c.wait()

    def weights(i, j):
        a, b = transformed(*(ks_ref[i, j, c].astype(F32) for c in range(3)))
        g_ref[0, i, j] = a.astype(BF)
        g_ref[1, i, j] = b.astype(BF)

    rest = Pump(
        [
            lambda f=f, r=r: prep_first(x_ref[f, r], f, r, u_ref, x2_ref, s_ref, q_ref)
            for r in range(9, 16)
            for f in range(4)
        ],
        12,
    )
    late = Pump([lambda i=i, j=j: weights(i, j) for i in range(3) for j in range(3)], 12)
    for g, pump in ((4, rest), (11, late)):
        parts = ((g, 7),)
        first_rows(u_ref, w_ref, f45_ref, o_ref, PAIR45, parts, None, None, None, pump)
        first_rows(u_ref, w_ref, f23_ref, o_ref, PAIR23, parts, None, x2_ref.at[2:4], bf_ref[...], pump)
        first_rows(u_ref, w_ref, f01_ref, o_ref, PAIR01, parts, None, x2_ref.at[0:2], bf_ref[...], pump)


def kernel_ahead(
    ok_ref, u_in, x2_in, f_in, top_ref, bot_ref, w_ref, kd_ref, u_ref, x2_ref, f_ref, part_ref, s_ref, q_ref, o_ref
):
    clear_edges(s_ref)
    clear_shift(o_ref)

    def halo(f, r):
        x = top_ref[f, r + 4] if r < 0 else bot_ref[f, r - 16]
        prep_first(x, f, r, u_ref, x2_ref, s_ref, q_ref, -4 < r < 18)

    rows = (-4, -3, -2, -1, 16, 17, 18)
    for r in rows:
        for f in (2, 3):
            halo(f, r)
    pump = Pump([lambda f=f, r=r: halo(f, r) for r in rows for f in (0, 1)], 6)
    first_rows(u_ref, w_ref, f_ref, o_ref, PAIR45, EDGES, edge_masks(ok_ref), None, None, pump)
    out = down_conv(f_ref, kd_ref, pump)
    for q in range(2):
        part_ref[q] = out[q].reshape(10, 64, 256).astype(BF)


def kernel_late(ok_ref, u_ref, x2_ref, f_in, w_ref, kd_ref, bf_ref, bd_ref, f_ref, red_ref, o_ref):
    clear_shift(o_ref)
    first_rows(u_ref, w_ref, f_ref, o_ref, PAIR23, EDGES, edge_masks(ok_ref), x2_ref.at[2:4], bf_ref[...])
    out = down_conv(f_ref, kd_ref)
    for q in range(2):
        red_ref[q] = (out[q] + bd_ref[...]).astype(BF).reshape(10, 64, 256)


def kernel_early(ok_ref, u_ref, x2_ref, f_in, w_ref, kd_ref, bf_ref, bd_ref, z_ref, f_ref, red_ref, o_ref):
    clear_shift(o_ref)
    first_rows(u_ref, w_ref, f_ref, o_ref, PAIR01, EDGES, edge_masks(ok_ref), x2_ref.at[0:2], bf_ref[...])
    out = down_conv(f_ref, kd_ref)
    for q in range(2):
        red_ref[q] = (out[q] + bd_ref[...] + z_ref[q].reshape(640, 256).astype(F32)).astype(BF).reshape(10, 64, 256)


def prep_mid(act, f, to, u_ref, s_ref, q_ref):
    q_ref[f, 0] = act[:, 0:128]
    q_ref[f, 1] = act[:, 128:256]
    d1 = jnp.concatenate([q_ref[f, h, pl.ds(0, 32, stride=2), :] for h in range(2)], axis=1)
    d2 = jnp.concatenate([q_ref[f, h, pl.ds(1, 32, stride=2), :] for h in range(2)], axis=1)
    s_ref[f, 0, 8:40] = d1
    s_ref[f, 1, 8:40] = d2
    d3 = s_ref[f, 0, 9:41]
    d0 = s_ref[f, 1, 7:39]
    for k, v in enumerate((d0 - d2, d1 + d2, d2 - d1, d1 - d3)):
        u_ref[(k, *to)] = v.astype(BF)


def own_row(ok_ref, red_ref, f, r, u_ref, s_ref, q_ref):
    act = silu(red_ref[f % 2, r].astype(F32))
    if r == 0 or r == 9:
        act = act * ok_ref[r // 9]
    prep_mid(act, f, (f, r), u_ref, s_ref, q_ref)


def taps(ks_ref, g_ref, k, i):
    if k == 0 or k == 3:
        return jnp.concatenate([ks_ref[i, j, 2 * (k // 3)] for j in range(3)], axis=0)
    return g_ref[k - 1, i].reshape(768, 256)


def columns(t_ref, at, y0, y1):
    for h in range(2):
        lanes = slice(h * 128, h * 128 + 128)
        t_ref[(*at, h, pl.ds(0, 32, stride=2), slice(None))] = y0[:, lanes]
        t_ref[(*at, h, pl.ds(1, 32, stride=2), slice(None))] = y1[:, lanes]


def frames_lhs(u_ref, k, f, count, r0, rows):
    return jnp.concatenate(
        [u_ref[k, f : f + count, r0 + j : r0 + j + rows].reshape(count * rows * 32, 256) for j in range(3)], axis=1
    )


def mixed(ms, rows):
    y0 = (ms[1] + ms[2] + ms[0]).reshape(rows, 32, 256)
    y1 = (ms[1] - ms[2] - ms[3]).reshape(rows, 32, 256)
    return y0, y1


def kernel_next(ok_ref, red_ref, ks_ref, g_ref, u_ref, zl_ref, s_ref, q_ref, t_ref):
    clear_edges(s_ref)
    for r in range(10):
        for f in (2, 3):
            own_row(ok_ref, red_ref, f, r, u_ref, s_ref, q_ref)
    ms = ([], [])
    for k in range(4):
        d0 = jnp.dot(frames_lhs(u_ref, k, 2, 2, 0, 8), taps(ks_ref, g_ref, k, 0), preferred_element_type=F32)
        d1 = jnp.dot(frames_lhs(u_ref, k, 3, 1, 0, 8), taps(ks_ref, g_ref, k, 1), preferred_element_type=F32)
        ms[0].append(d0[:256] + d1)
        ms[1].append(d0[256:])
    for f in range(2):
        y0, y1 = mixed(ms[f], 8)
        for r in range(8):
            columns(t_ref, (f, r), y0[r], y1[r])
            for h in range(2):
                zl_ref[f, r, :, h * 128 : h * 128 + 128] = t_ref[f, r, h].astype(BF)


def kernel_same(ok_ref, u_in, red_ref, ks_ref, g_ref, u_ref, y_ref, s_ref, q_ref):
    clear_edges(s_ref)
    work = [lambda f=f, r=r: own_row(ok_ref, red_ref, f, r, u_ref, s_ref, q_ref) for r in range(10) for f in (0, 1)]
    pump = Pump(work, 4)
    ms = ([], [])
    for k in range(4):
        d2 = jnp.dot(frames_lhs(u_ref, k, 2, 2, 0, 8), taps(ks_ref, g_ref, k, 2), preferred_element_type=F32)
        d1 = jnp.dot(frames_lhs(u_ref, k, 2, 1, 0, 8), taps(ks_ref, g_ref, k, 1), preferred_element_type=F32)
        ms[0].append(d2[:256])
        ms[1].append(d2[256:] + d1)
        pump()
    for f in range(2):
        y0, y1 = mixed(ms[f], 8)
        for r in range(8):
            columns(y_ref, (f, r), y0[r], y1[r])


def kernel_last(u_ref, red01_ref, red23_ref, y_ref, zl_ref, ks_ref, g_ref, bs_ref, lat_ref, t_ref, out_ref, sem):
    copies = []
    for r0 in range(0, 8, STEP):
        n = STEP * 32
        ms = ([], [], [], [])
        for k in range(4):
            lhs = frames_lhs(u_ref, k, 0, 2, r0, STEP)
            e0, e1, e2 = (jnp.dot(lhs, taps(ks_ref, g_ref, k, i), preferred_element_type=F32) for i in range(3))
            ms[0].append(e2[:n])
            ms[1].append(e2[n:] + e1[:n])
            ms[2].append(e1[n:] + e0[:n])
            ms[3].append(e0[n:])
        for f in range(4):
            y0, y1 = mixed(ms[f], STEP)
            red_ref = (red01_ref, red23_ref)[f // 2]
            for r in range(r0, r0 + STEP):
                columns(t_ref, (f, r), y0[r - r0], y1[r - r0])
                for h in range(2):
                    lanes = slice(h * 128, h * 128 + 128)
                    v = red_ref[f % 2, r + 1, :, lanes].astype(F32)
                    if f < 2:
                        v = v + zl_ref[f, r, :, lanes].astype(F32)
                    else:
                        v = v + y_ref[f - 2, r, h]
                    out_ref[f, r, :, lanes] = (t_ref[f, r, h] + v + bs_ref[:, lanes]).astype(BF)
            rows = pl.ds(r0, STEP)
            copies.append(pltpu.make_async_copy(out_ref.at[f, rows], lat_ref.at[f, rows], sem.at[len(copies)]))
            copies[-1].start()
    for c in copies:
        c.wait()


V = pl.BlockSpec(memory_space=pltpu.VMEM)
HBM = pl.BlockSpec(memory_space=pltpu.HBM)


def sds(*shape):
    return jax.ShapeDtypeStruct(shape, BF)


def res(*shape, dtype=BF):
    return VMEM(shape, dtype)


def keep(*xs):
    return [pltpu.with_memory_space_constraint(x, pltpu.VMEM) for x in xs]


def far(*xs):
    return [pltpu.with_memory_space_constraint(x, pltpu.HBM) for x in xs]


def call(body, name, ins, outs, scratch, flops, in_specs=None, out_specs=None, aliases=None):
    return pl.pallas_call(
        body,
        out_shape=outs,
        in_specs=in_specs or [V] * len(ins),
        out_specs=out_specs or [V] * len(outs),
        scratch_shapes=scratch,
        input_output_aliases=aliases or {},
        compiler_params=pltpu.CompilerParams(vmem_limit_bytes=LIMIT),
        cost_estimate=pl.CostEstimate(flops=flops, bytes_accessed=4 << 20, transcendentals=0),
        name=name,
    )(*ins)


def on_device(features, kf, bf, kd, bd, ks, bs):
    tm, sp = lax.axis_size("tm"), lax.axis_size("space")
    down = [(i, i + 1) for i in range(sp - 1)]
    up = [(i + 1, i) for i in range(sp - 1)]
    later = [(i, i + 1) for i in range(tm - 1)]
    at = lax.axis_index("space")
    ok = jnp.stack([at > 0, at < sp - 1]).astype(F32).reshape(2, 1, 1) * jnp.ones((1, 1, 256), F32)

    wide = [VMEM((4, 2, 80, 128), F32), VMEM((4, 128, 128), F32)]
    half = [VMEM((4, 2, 48, 256), F32), VMEM((4, 2, 64, 128), F32)]
    shift = VMEM((2, 7, 72, 128), F32)
    fshape, ushape, x2shape, u2shape = (2, 2, 11, 64, 384), (4, 2, 23, 64, 256), (4, 21, 64, 256), (4, 4, 10, 32, 256)
    yshape, rshape = (2, 8, 2, 64, 128), (2, 10, 64, 256)
    xv, kfv, edge_dn, edge_up = call(
        kernel_load, "load", (*keep(ok), *far(features, kf)),
        [res(4, 16, 128, 128), res(3, 3, 3, 128, 128), sds(4, 4, 128, 128), sds(4, 3, 128, 128)],
        [pltpu.SemaphoreType.DMA((4,))], 100_000_000, in_specs=[V] + [HBM] * 2,
    )
    top = lax.ppermute(edge_dn, "space", down)
    bot = lax.ppermute(edge_up, "space", up)
    u, x2, w, ksv, g, kdv, bfv, bdv, bsv, f45, f23, f01 = call(
        kernel_own, "own", (*keep(ok, xv, kfv), *far(ks, kd, bf.reshape(1, 128), bd.reshape(1, 256), bs.reshape(1, 256))),
        [
            res(*ushape), res(*x2shape), res(4, 3, 2, 256, 256), res(3, 3, 3, 256, 256), res(2, 3, 3, 256, 256),
            res(3, 3, 128, 256), res(1, 128, dtype=F32), res(1, 256, dtype=F32), res(1, 256, dtype=F32),
            *[res(*fshape)] * 3,
        ],
        [*wide, shift, pltpu.SemaphoreType.DMA((5,))], 8_000_000_000, in_specs=[V] * 3 + [HBM] * 5,
    )
    u, x2, _, part = call(
        kernel_ahead, "ahead", (*keep(ok, u, x2, f45), top, bot, *keep(w, kdv)),
        [res(*ushape), res(*x2shape), res(*fshape), sds(*rshape)],
        [*wide, shift], 2_000_000_000, in_specs=[V] + [V] * 7, aliases={1: 0, 2: 1, 3: 2},
    )
    zpart = lax.ppermute(part, "tm", later)
    _, red23 = call(
        kernel_late, "late", keep(ok, u, x2, f23, w, kdv, bfv, bdv), [res(*fshape), res(*rshape)],
        [shift], 2_500_000_000, in_specs=[V] + [V] * 7, aliases={3: 0},
    )
    u2, zl = call(
        kernel_next, "next", keep(ok, red23, ksv, g), [res(*u2shape), sds(2, 8, 64, 256)],
        [*half, VMEM(yshape, F32)], 2_000_000_000, in_specs=[V] + [V] * 3,
    )
    zlat = lax.ppermute(zl, "tm", later)
    _, red01 = call(
        kernel_early, "early", (*keep(ok, u, x2, f01, w, kdv, bfv, bdv), zpart), [res(*fshape), res(*rshape)],
        [shift], 2_500_000_000, in_specs=[V] + [V] * 8, aliases={3: 0},
    )
    u2, y = call(
        kernel_same, "same", keep(ok, u2, red01, ksv, g), [res(*u2shape), res(*yshape, dtype=F32)],
        half, 2_000_000_000, in_specs=[V] + [V] * 4, aliases={1: 0},
    )
    (lat,) = call(
        kernel_last, "last", (*keep(u2, red01, red23, y), zlat, *keep(ksv, g, bsv)), [sds(4, 8, 64, 256)],
        [VMEM((4, 8, 2, 64, 128), F32), VMEM((4, 8, 64, 256), BF), pltpu.SemaphoreType.DMA((4 * 8 // STEP,))],
        4_000_000_000, in_specs=[V] * 8, out_specs=[HBM],
    )
    return lat


def solution(mesh):
    in_specs = (P("tm", "space", None, None), P(), P(), P(), P(), P(), P())
    out_specs = P("tm", "space", None, None)
    return jax.shard_map(on_device, mesh=mesh, in_specs=in_specs, out_specs=out_specs, check_vma=False)
```

time: 53.5 us -> 50.2 us (0.938)
  starting transfers between devices: 18.9 us -> 15.4 us
  local copies, waits for them, and re-layouts: 1.02 us -> 0.07 us
  waiting for transfers between devices: 6.3 us -> 7.19 us
    ppermute x1, starting transfers between devices: 4.33 us -> 1.92 us  [on_device(): zlat = lax.ppermute(zl, 'tm', later)]
    ppermute x3 -> x2, starting transfers between devices: 8.93 us -> 6.83 us  [the longest x1 4.91 us: on_device(): bot = lax.ppermute(edge_up, 'space', up)]
    ppermute x1, starting transfers between devices: 5.6 us -> 6.63 us  [on_device(): zpart = lax.ppermute(part, 'tm', later)]
    slice x1 -> x0, local copies, waits for them, and re-layouts: 1.02 us -> none  [on_device(): halo = lax.ppermute(features[:, 0:3], 'space', up)]
    ppermute x1, waiting for transfers between devices: 0.01 us -> 0.94 us  [on_device(): zpart = lax.ppermute(part, 'tm', later)]
    ppermute x3 -> x2, waiting for transfers between devices: 4.41 us -> 4.18 us  [the longest x1 4.18 us: on_device(): top = lax.ppermute(edge_dn, 'space', down)]
  transfers between devices with their start and end apart: 5 -> 4, of which waited for: 3 -> 3; matrix products, arithmetic and copies ran while one was open for 0% -> 0% of each run, Pallas kernels for 38% -> 37%
where the time goes in v3:
time: 50.2 us; the launch traced here: 49.7 us
  Pallas kernels  26.7 us (53%)
  starting transfers between devices  15.4 us (31%)
  waiting for transfers between devices  7.19 us (14%)
    pallas_call x8, Pallas kernels, call(): pl.pallas_call(body, out_shape=outs, in_specs=in_specs or [V] * len(ins),...  26.7 us
    ppermute x1, starting transfers between devices, on_device(): zpart = lax.ppermute(part, 'tm', later)  6.63 us
    ppermute x1, starting transfers between devices, on_device(): bot = lax.ppermute(edge_up, 'space', up)  4.91 us
    ppermute x1, waiting for transfers between devices, on_device(): top = lax.ppermute(edge_dn, 'space', down)  4.18 us
    ppermute x1, waiting for transfers between devices, on_device(): zlat = lax.ppermute(zl, 'tm', later)  2.07 us
    ppermute x1, starting transfers between devices, on_device(): zlat = lax.ppermute(zl, 'tm', later)  1.92 us
    ppermute x1, starting transfers between devices, on_device(): top = lax.ppermute(edge_dn, 'space', down)  1.92 us
  transfers between devices with their start and end apart: 4, of which 3 were waited for; matrix products, arithmetic and copies ran while one was open for 0% of the time, Pallas kernels for 37%

profile of v3, /device:TPU:103, one launch (start us, length us, event | category | flops | bytes accessed | tf_op | source)
XLA Modules:
  0.0 49.7 jit_solution(16816635977151609189)
XLA Ops:
  0.0 0.1 add_convert_fusion
  0.1 0.1 mul.2.ok_ref
  0.2 2.1 %load.1 = (bf16[4,16,128,128]{3,2,1,0:T(8,128)(2,1)S(1)}, bf16[3,3,3,128,128]{4,3,2,1,0:T(8,128)(2,1)S(1)}, bf16[4,4,128,128]{3,2,1,0:T(8,128)(2,1)S(1)}, bf16[4,3,128,128]{3,2,1,0:T(8,128)(2,1)S(1)}) custom-call(f32[2,1,256]{2,1,0:T(1,128)S(1)} %mul.2.ok_ref, bf16[4,16,128,128]{3,2,1,0:T(8,128)(2,1)} %x_hbm.1, bf16[3,3,3,128,128]{4,3,2,1,0:T(8,128)(2,1)} %kf_hbm.1), custom_call_target="tpu_custom_call" | custom-call | flops 100000000 | bytes 4194304 | tf_op jit(solution)/shard_map/load/pallas_call | solution.py:381
  2.3 4.9 %collective-permute-start.1 = (bf16[4,3,128,128]{3,2,1,0:T(8,128)(2,1)S(1)}, bf16[4,3,128,128]{3,2,1,0:T(8,128)(2,1)S(1)}, u32[]{:S(2)}, u32[]{:S(2)}) collective-permute-start(bf16[4,3,128,128]{3,2,1,0:T(8,128)(2,1)S(1)} %get-tuple-element.36), channel_id=1, source_target_pairs={{1,0},{2,1},{3,2},{4,3},{5,4},{6,5},{7,6},{8,7},{9,8},{10,9},{11,1... | collective-permute-start | bytes 1179656 | tf_op jit(solution)/shard_map/ppermute | solution.py:413
  7.2 1.9 %collective-permute-start = (bf16[4,4,128,128]{3,2,1,0:T(8,128)(2,1)S(1)}, bf16[4,4,128,128]{3,2,1,0:T(8,128)(2,1)S(1)}, u32[]{:S(2)}, u32[]{:S(2)}) collective-permute-start(bf16[4,4,128,128]{3,2,1,0:T(8,128)(2,1)S(1)} %get-tuple-element.35), channel_id=1, source_target_pairs={{0,1},{1,2},{2,3},{3,4},{4,5},{5,6},{6,7},{7,8},{8,9},{9,10},{10,1... | collective-permute-start | bytes 1572872 | tf_op jit(solution)/shard_map/ppermute | solution.py:412
  9.1 10.4 %own.1 = (bf16[4,2,23,64,256]{4,3,2,1,0:T(8,128)(2,1)S(1)}, bf16[4,21,64,256]{3,2,1,0:T(8,128)(2,1)S(1)}, bf16[4,3,2,256,256]{4,3,2,1,0:T(8,128)(2,1)S(1)}, bf16...) custom-call(f32[2,1,256]{2,1,0:T(1,128)S(1)} %mul.2.ok_ref, ...), custom_call_target="tpu_custom_call" | custom-call | flops 8000000000 | bytes 4194304 | tf_op jit(solution)/shard_map/own/pallas_call | solution.py:381
  19.5 0.0 collective-permute-done.1.bot_ref
  19.5 4.2 %collective-permute-done.top_ref = bf16[4,4,128,128]{3,2,1,0:T(8,128)(2,1)S(1)} collective-permute-done((bf16[4,4,128,128]{3,2,1,0:T(8,128)(2,1)S(1)}, bf16[4,4,128,128]{3,2,1,0:T(8,128)(2,1)S(1)}, u32[]{:S(2)}, u32[]{:S(2)}) %collective-permute-start) | collective-permute-done | bytes 524320 | tf_op jit(solution)/shard_map/ppermute | solution.py:412
  23.7 2.5 %ahead.1 = (bf16[4,2,23,64,256]{4,3,2,1,0:T(8,128)(2,1)S(1)}, bf16[4,21,64,256]{3,2,1,0:T(8,128)(2,1)S(1)}, bf16[2,2,11,64,384]{4,3,2,1,0:T(8,128)(2,1)S(1)}, bf16[2,10,64,256]{3,2,1,0:T(8,128)(2,1)S(1)}) custom-call(f32[2,1,256]{2,1,0:T(1,128)S(1)} %mul.2.ok_ref, ...), custom_call_target="tpu_custom_call", output_to_operand_aliasing={{0}: (1, {}), {1}: (2, {}), {2}: (3, {})} | custom-call | flops 2000000000 | bytes 4194304 | tf_op jit(solution)/shard_map/ahead/pallas_call | solution.py:381
  26.2 6.6 %collective-permute-start.2 = (bf16[2,10,64,256]{3,2,1,0:T(8,128)(2,1)S(1)}, bf16[2,10,64,256]{3,2,1,0:T(8,128)(2,1)S(1)}, u32[]{:S(2)}, u32[]{:S(2)}) collective-permute-start(bf16[2,10,64,256]{3,2,1,0:T(8,128)(2,1)S(1)} %get-tuple-element.49), channel_id=1, source_target_pairs={{0,16},{16,32},{32,48},{48,64},{64,80},{80,96},{96,112},{112,128},... | collective-permute-start | bytes 1966088 | tf_op jit(solution)/shard_map/ppermute | solution.py:428
  32.8 2.6 %late.1 = (bf16[2,2,11,64,384]{4,3,2,1,0:T(8,128)(2,1)S(1)}, bf16[2,10,64,256]{3,2,1,0:T(8,128)(2,1)S(1)}) custom-call(f32[2,1,256]{2,1,0:T(1,128)S(1)} %mul.2.ok_ref, bf16[4,2,23,64,256]{4,3,2,1,0:T(8,128)(2,1)S(1)} %get-tuple-element.39.u_ref, bf16[4,21,64,256]{3,2,1,0:T(8,128)(2,1)S(1)} %get-tuple-element.40.x2_ref, ...), custom_call_target="tpu_custom_call", output_to_operand_aliasing={{0}: (3, {})} | custom-call | flops 2500000000 | bytes 4194304 | tf_op jit(solution)/shard_map/late/pallas_call | solution.py:381
  35.4 1.9 %next.1 = (bf16[4,4,10,32,256]{4,3,2,1,0:T(8,128)(2,1)S(1)}, bf16[2,8,64,256]{3,2,1,0:T(8,128)(2,1)S(1)}) custom-call(f32[2,1,256]{2,1,0:T(1,128)S(1)} %mul.2.ok_ref, bf16[2,10,64,256]{3,2,1,0:T(8,128)(2,1)S(1)} %get-tuple-element.44.red_ref.red23_ref, bf16[3,3,3,256,256]{4,3,2,1,0:T(8,128)(2,1)S(1)} %get-tuple-element.45.ks_ref, ...), custom_call_target="tpu_custom_call" | custom-call | flops 2000000000 | bytes 4194304 | tf_op jit(solution)/shard_map/next/pallas_call | solution.py:381
  37.3 1.9 %collective-permute-start.3 = (bf16[2,8,64,256]{3,2,1,0:T(8,128)(2,1)S(1)}, bf16[2,8,64,256]{3,2,1,0:T(8,128)(2,1)S(1)}, u32[]{:S(2)}, u32[]{:S(2)}) collective-permute-start(bf16[2,8,64,256]{3,2,1,0:T(8,128)(2,1)S(1)} %get-tuple-element.53), channel_id=1, source_target_pairs={{0,16},{16,32},{32,48},{48,64},{64,80},{80,96},{96,112},{112,128},... | collective-permute-start | bytes 1572872 | tf_op jit(solution)/shard_map/ppermute | solution.py:437
  39.2 0.9 %collective-permute-done.2.z_ref = bf16[2,10,64,256]{3,2,1,0:T(8,128)(2,1)S(1)} collective-permute-done((bf16[2,10,64,256]{3,2,1,0:T(8,128)(2,1)S(1)}, bf16[2,10,64,256]{3,2,1,0:T(8,128)(2,1)S(1)}, u32[]{:S(2)}, u32[]{:S(2)}) %collective-permute-start.2) | collective-permute-done | bytes 655392 | tf_op jit(solution)/shard_map/ppermute | solution.py:428
  40.2 1.9 %early.1 = (bf16[2,2,11,64,384]{4,3,2,1,0:T(8,128)(2,1)S(1)}, bf16[2,10,64,256]{3,2,1,0:T(8,128)(2,1)S(1)}) custom-call(f32[2,1,256]{2,1,0:T(1,128)S(1)} %mul.2.ok_ref, bf16[4,2,23,64,256]{4,3,2,1,0:T(8,128)(2,1)S(1)} %get-tuple-element.39.u_ref, bf16[4,21,64,256]{3,2,1,0:T(8,128)(2,1)S(1)} %get-tuple-element.40.x2_ref, ...), custom_call_target="tpu_custom_call", output_to_operand_aliasing={{0}: (3, {})} | custom-call | flops 2500000000 | bytes 4194304 | tf_op jit(solution)/shard_map/early/pallas_call | solution.py:381
  42.0 1.7 %same.1 = (bf16[4,4,10,32,256]{4,3,2,1,0:T(8,128)(2,1)S(1)}, f32[2,8,2,64,128]{4,3,2,1,0:T(8,128)S(1)}) custom-call(f32[2,1,256]{2,1,0:T(1,128)S(1)} %mul.2.ok_ref, bf16[4,4,10,32,256]{4,3,2,1,0:T(8,128)(2,1)S(1)} %get-tuple-element.47.u_in, bf16[2,10,64,256]{3,2,1,0:T(8,128)(2,1)S(1)} %get-tuple-element.50.red_ref.red01_ref, ...), custom_call_target="tpu_custom_call", output_to_operand_aliasing={{0}: (1, {})} | custom-call | flops 2000000000 | bytes 4194304 | tf_op jit(solution)/shard_map/same/pallas_call | solution.py:381
  43.7 2.1 %collective-permute-done.3.zl_ref = bf16[2,8,64,256]{3,2,1,0:T(8,128)(2,1)S(1)} collective-permute-done((bf16[2,8,64,256]{3,2,1,0:T(8,128)(2,1)S(1)}, bf16[2,8,64,256]{3,2,1,0:T(8,128)(2,1)S(1)}, u32[]{:S(2)}, u32[]{:S(2)}) %collective-permute-start.3) | collective-permute-done | bytes 524320 | tf_op jit(solution)/shard_map/ppermute | solution.py:437
  45.8 3.8 %last.1 = bf16[4,8,64,256]{3,2,1,0:T(8,128)(2,1)} custom-call(bf16[4,4,10,32,256]{4,3,2,1,0:T(8,128)(2,1)S(1)} %get-tuple-element.51.u_ref, bf16[2,10,64,256]{3,2,1,0:T(8,128)(2,1)S(1)} %get-tuple-element.50.red_ref.red01_ref, bf16[2,10,64,256]{3,2,1,0:T(8,128)(2,1)S(1)} %get-tuple-element.44.red_ref.red23_ref, ...), custom_call_target="tpu_custom_call" | custom-call | flops 4000000000 | bytes 4194304 | tf_op jit(solution)/shard_map/last/pallas_call | solution.py:381
Async XLA Ops:
  2.3 17.3 %collective-permute-start.1 = (bf16[4,3,128,128]{3,2,1,0:T(8,128)(2,1)S(1)}, bf16[4,3,128,128]{3,2,1,0:T(8,128)(2,1)S(1)}, u32[]{:S(2)}, u32[]{:S(2)}) collective-permute-start(bf16[4,3,128,128]{3,2,1,0:T(8,128)(2,1)S(1)} %get-tuple-element.36), channel_id=1, source_target_pairs={{1,0},{2,1},{3,2},{4,3},{5,4},{6,5},{7,6},{8,7},{9,8},{10,9},{11,1... | collective-permute-start | bytes 1179656 | tf_op jit(solution)/shard_map/ppermute | solution.py:413
  7.2 16.5 %collective-permute-start = (bf16[4,4,128,128]{3,2,1,0:T(8,128)(2,1)S(1)}, bf16[4,4,128,128]{3,2,1,0:T(8,128)(2,1)S(1)}, u32[]{:S(2)}, u32[]{:S(2)}) collective-permute-start(bf16[4,4,128,128]{3,2,1,0:T(8,128)(2,1)S(1)} %get-tuple-element.35), channel_id=1, source_target_pairs={{0,1},{1,2},{2,3},{3,4},{4,5},{5,6},{6,7},{7,8},{8,9},{9,10},{10,1... | collective-permute-start | bytes 1572872 | tf_op jit(solution)/shard_map/ppermute | solution.py:412
  26.2 14.0 %collective-permute-start.2 = (bf16[2,10,64,256]{3,2,1,0:T(8,128)(2,1)S(1)}, bf16[2,10,64,256]{3,2,1,0:T(8,128)(2,1)S(1)}, u32[]{:S(2)}, u32[]{:S(2)}) collective-permute-start(bf16[2,10,64,256]{3,2,1,0:T(8,128)(2,1)S(1)} %get-tuple-element.49), channel_id=1, source_target_pairs={{0,16},{16,32},{32,48},{48,64},{64,80},{80,96},{96,112},{112,128},... | collective-permute-start | bytes 1966088 | tf_op jit(solution)/shard_map/ppermute | solution.py:428
  37.3 8.5 %collective-permute-start.3 = (bf16[2,8,64,256]{3,2,1,0:T(8,128)(2,1)S(1)}, bf16[2,8,64,256]{3,2,1,0:T(8,128)(2,1)S(1)}, u32[]{:S(2)}, u32[]{:S(2)}) collective-permute-start(bf16[2,8,64,256]{3,2,1,0:T(8,128)(2,1)S(1)} %get-tuple-element.53), channel_id=1, source_target_pairs={{0,16},{16,32},{32,48},{48,64},{64,80},{80,96},{96,112},{112,128},... | collective-permute-start | bytes 1572872 | tf_op jit(solution)/shard_map/ppermute | solution.py:437

commit v4 on v3

--- a/solution.py
+++ b/solution.py
@@ -5,10 +5,11 @@
 from jax.experimental.pallas import tpu as pltpu
 from jax.sharding import PartitionSpec as P
 
+
 BF = jnp.bfloat16
 F32 = jnp.float32
 VMEM = pltpu.VMEM
-LIMIT = 20 * 2**20
+LIMIT = 12 * 2**20
 STEP = 4
 
 
@@ -102,19 +103,20 @@
             o_ref[q, n, 0:8] = jnp.zeros((8, 128), F32)
 
 
-def down_conv(f_ref, kd_ref, pump=idle):
+def down_conv(f_ref, kd_ref, parts, pump=idle):
     rhs = jnp.concatenate([kd_ref[j, c] for j in range(3) for c in (1, 2, 0)], axis=0)
+    rows = [m + n for m, count in parts for n in range(count)]
     out = []
     for q in range(2):
         lhs = jnp.concatenate(
             [
-                f_ref[q, 0, 0:10].reshape(640, 384),
-                f_ref[q, 1, 0:10].reshape(640, 384),
-                f_ref[q, 0, 1:11].reshape(640, 384),
+                jnp.concatenate([f_ref[q, e, m + d : m + d + n].reshape(n * 64, 384) for m, n in parts], axis=0)
+                for e, d in ((0, 0), (1, 0), (0, 1))
             ],
             axis=1,
         )
-        out.append(jnp.dot(lhs, rhs, preferred_element_type=F32))
+        y = jnp.dot(lhs, rhs, preferred_element_type=F32).reshape(len(rows), 64, 256)
+        out += [(q, m, y[n]) for n, m in enumerate(rows)]
         pump()
     return out
 
@@ -125,6 +127,8 @@
 
 
 EDGES = ((0, 4), (18, 3))
+INSIDE = ((2, 6),)
+OUTSIDE = ((0, 2), (8, 2))
 
 
 def edge_masks(ok_ref):
@@ -147,13 +151,14 @@
 def kernel_own(
     ok_ref, x_ref, kf_ref, ks_hbm, kd_hbm, bf_hbm, bd_hbm, bs_hbm,
     u_ref, x2_ref, w_ref, ks_ref, g_ref, kd_ref, bf_ref, bd_ref, bs_ref, f45_ref, f23_ref, f01_ref,
-    s_ref, q_ref, o_ref, sem,
+    part_ref, red_ref, p_ref, u2_ref, s_ref, q_ref, o_ref, s2_ref, q2_ref, sem,
 ):
     pairs = ((bf_hbm, bf_ref), (ks_hbm, ks_ref), (kd_hbm, kd_ref), (bd_hbm, bd_ref), (bs_hbm, bs_ref))
     copies = [pltpu.make_async_copy(a, b, sem.at[n]) for n, (a, b) in enumerate(pairs)]
     for c in copies:
         c.start()
     clear_edges(s_ref)
+    clear_edges(s2_ref)
     clear_shift(o_ref)
 
     def row(r, carry):
@@ -199,16 +204,28 @@
         ],
         12,
     )
-    late = Pump([lambda i=i, j=j: weights(i, j) for i in range(3) for j in range(3)], 12)
-    for g, pump in ((4, rest), (11, late)):
-        parts = ((g, 7),)
-        first_rows(u_ref, w_ref, f45_ref, o_ref, PAIR45, parts, None, None, None, pump)
-        first_rows(u_ref, w_ref, f23_ref, o_ref, PAIR23, parts, None, x2_ref.at[2:4], bf_ref[...], pump)
-        first_rows(u_ref, w_ref, f01_ref, o_ref, PAIR01, parts, None, x2_ref.at[0:2], bf_ref[...], pump)
+    gains = Pump([lambda i=i, j=j: weights(i, j) for i in range(3) for j in range(3)], 6)
+    mids = Pump(
+        [lambda f=f, r=r: own_row(ok_ref, red_ref, f, r, u2_ref, s2_ref, q2_ref) for r in range(2, 8) for f in (2, 3)], 8
+    )
+    bias, parts = bf_ref[...], ((4, 7),)
+    first_rows(u_ref, w_ref, f45_ref, o_ref, PAIR45, parts, None, None, None, rest)
+    first_rows(u_ref, w_ref, f23_ref, o_ref, PAIR23, parts, None, x2_ref.at[2:4], bias, rest)
+    first_rows(u_ref, w_ref, f01_ref, o_ref, PAIR01, parts, None, x2_ref.at[0:2], bias, rest)
+    parts = ((11, 7),)
+    first_rows(u_ref, w_ref, f23_ref, o_ref, PAIR23, parts, None, x2_ref.at[2:4], bias, gains)
+    for q, m, y in down_conv(f23_ref, kd_ref, INSIDE, gains):
+        red_ref[q, m] = (y + bd_ref[...]).astype(BF)
+    first_rows(u_ref, w_ref, f45_ref, o_ref, PAIR45, parts, None, None, None, mids)
+    first_rows(u_ref, w_ref, f01_ref, o_ref, PAIR01, parts, None, x2_ref.at[0:2], bias, mids)
+    for q, m, y in down_conv(f45_ref, kd_ref, INSIDE):
+        part_ref[q, m] = y.astype(BF)
+    for q, m, y in down_conv(f01_ref, kd_ref, INSIDE):
+        p_ref[q, m] = y + bd_ref[...]
 
 
 def kernel_ahead(
-    ok_ref, u_in, x2_in, f_in, top_ref, bot_ref, w_ref, kd_ref, u_ref, x2_ref, f_ref, part_ref, s_ref, q_ref, o_ref
+    ok_ref, u_in, x2_in, f_in, part_in, top_ref, bot_ref, w_ref, kd_ref, u_ref, x2_ref, f_ref, part_ref, s_ref, q_ref, o_ref
 ):
     clear_edges(s_ref)
     clear_shift(o_ref)
@@ -223,25 +240,22 @@
             halo(f, r)
     pump = Pump([lambda f=f, r=r: halo(f, r) for r in rows for f in (0, 1)], 6)
     first_rows(u_ref, w_ref, f_ref, o_ref, PAIR45, EDGES, edge_masks(ok_ref), None, None, pump)
-    out = down_conv(f_ref, kd_ref, pump)
-    for q in range(2):
-        part_ref[q] = out[q].reshape(10, 64, 256).astype(BF)
-
-
-def kernel_late(ok_ref, u_ref, x2_ref, f_in, w_ref, kd_ref, bf_ref, bd_ref, f_ref, red_ref, o_ref):
+    for q, m, y in down_conv(f_ref, kd_ref, OUTSIDE, pump):
+        part_ref[q, m] = y.astype(BF)
+
+
+def kernel_late(ok_ref, u_ref, x2_ref, f_in, red_in, w_ref, kd_ref, bf_ref, bd_ref, f_ref, red_ref, o_ref):
     clear_shift(o_ref)
     first_rows(u_ref, w_ref, f_ref, o_ref, PAIR23, EDGES, edge_masks(ok_ref), x2_ref.at[2:4], bf_ref[...])
-    out = down_conv(f_ref, kd_ref)
-    for q in range(2):
-        red_ref[q] = (out[q] + bd_ref[...]).astype(BF).reshape(10, 64, 256)
-
-
-def kernel_early(ok_ref, u_ref, x2_ref, f_in, w_ref, kd_ref, bf_ref, bd_ref, z_ref, f_ref, red_ref, o_ref):
+    for q, m, y in down_conv(f_ref, kd_ref, OUTSIDE):
+        red_ref[q, m] = (y + bd_ref[...]).astype(BF)
+
+
+def kernel_early(ok_ref, u_ref, x2_ref, f_in, p_in, w_ref, kd_ref, bf_ref, bd_ref, f_ref, p_ref, o_ref):
     clear_shift(o_ref)
     first_rows(u_ref, w_ref, f_ref, o_ref, PAIR01, EDGES, edge_masks(ok_ref), x2_ref.at[0:2], bf_ref[...])
-    out = down_conv(f_ref, kd_ref)
-    for q in range(2):
-        red_ref[q] = (out[q] + bd_ref[...] + z_ref[q].reshape(640, 256).astype(F32)).astype(BF).reshape(10, 64, 256)
+    for q, m, y in down_conv(f_ref, kd_ref, OUTSIDE):
+        p_ref[q, m] = y + bd_ref[...]
 
 
 def prep_mid(act, f, to, u_ref, s_ref, q_ref):
@@ -289,9 +303,9 @@
     return y0, y1
 
 
-def kernel_next(ok_ref, red_ref, ks_ref, g_ref, u_ref, zl_ref, s_ref, q_ref, t_ref):
+def kernel_next(ok_ref, u_in, red_ref, ks_ref, g_ref, u_ref, zl_ref, s_ref, q_ref, t_ref):
     clear_edges(s_ref)
-    for r in range(10):
+    for r in (0, 1, 8, 9):
         for f in (2, 3):
             own_row(ok_ref, red_ref, f, r, u_ref, s_ref, q_ref)
     ms = ([], [])
@@ -308,10 +322,14 @@
                 zl_ref[f, r, :, h * 128 : h * 128 + 128] = t_ref[f, r, h].astype(BF)
 
 
-def kernel_same(ok_ref, u_in, red_ref, ks_ref, g_ref, u_ref, y_ref, s_ref, q_ref):
+def kernel_same(ok_ref, u_in, p_ref, z_ref, ks_ref, g_ref, u_ref, red_ref, y_ref, s_ref, q_ref):
     clear_edges(s_ref)
-    work = [lambda f=f, r=r: own_row(ok_ref, red_ref, f, r, u_ref, s_ref, q_ref) for r in range(10) for f in (0, 1)]
-    pump = Pump(work, 4)
+
+    def joined(f, r):
+        red_ref[f, r] = (p_ref[f, r] + z_ref[f, r].astype(F32)).astype(BF)
+        own_row(ok_ref, red_ref, f, r, u_ref, s_ref, q_ref)
+
+    pump = Pump([lambda f=f, r=r: joined(f, r) for r in range(10) for f in (0, 1)], 4)
     ms = ([], [])
     for k in range(4):
         d2 = jnp.dot(frames_lhs(u_ref, k, 2, 2, 0, 8), taps(ks_ref, g_ref, k, 2), preferred_element_type=F32)
@@ -325,7 +343,7 @@
             columns(y_ref, (f, r), y0[r], y1[r])
 
 
-def kernel_last(u_ref, red01_ref, red23_ref, y_ref, zl_ref, ks_ref, g_ref, bs_ref, lat_ref, t_ref, out_ref, sem):
+def kernel_rest(u_ref, red01_ref, red23_ref, y_ref, ks_ref, g_ref, bs_ref, lat_ref, y01_ref, t_ref, out_ref, sem):
     copies = []
     for r0 in range(0, 8, STEP):
         n = STEP * 32
@@ -337,22 +355,32 @@
             ms[1].append(e2[n:] + e1[:n])
             ms[2].append(e1[n:] + e0[:n])
             ms[3].append(e0[n:])
-        for f in range(4):
+        for f in (2, 3, 0, 1):
             y0, y1 = mixed(ms[f], STEP)
-            red_ref = (red01_ref, red23_ref)[f // 2]
             for r in range(r0, r0 + STEP):
                 columns(t_ref, (f, r), y0[r - r0], y1[r - r0])
                 for h in range(2):
                     lanes = slice(h * 128, h * 128 + 128)
-                    v = red_ref[f % 2, r + 1, :, lanes].astype(F32)
+                    v = t_ref[f, r, h] + (red01_ref, red23_ref)[f // 2][f % 2, r + 1, :, lanes].astype(F32) + bs_ref[:, lanes]
                     if f < 2:
-                        v = v + zl_ref[f, r, :, lanes].astype(F32)
+                        y01_ref[f, r, :, lanes] = v
                     else:
-                        v = v + y_ref[f - 2, r, h]
-                    out_ref[f, r, :, lanes] = (t_ref[f, r, h] + v + bs_ref[:, lanes]).astype(BF)
-            rows = pl.ds(r0, STEP)
-            copies.append(pltpu.make_async_copy(out_ref.at[f, rows], lat_ref.at[f, rows], sem.at[len(copies)]))
-            copies[-1].start()
+                        out_ref[f - 2, r, :, lanes] = (v + y_ref[f - 2, r, h]).astype(BF)
+            if f > 1:
+                rows = pl.ds(r0, STEP)
+                copies.append(pltpu.make_async_copy(out_ref.at[f - 2, rows], lat_ref.at[f, rows], sem.at[len(copies)]))
+                copies[-1].start()
+    for c in copies:
+        c.wait()
+
+
+def kernel_last(lat_in, y_ref, zl_ref, lat_ref, out_ref, sem):
+    copies = []
+    for f in range(2):
+        for r in range(8):
+            out_ref[f, r] = (y_ref[f, r] + zl_ref[f, r].astype(F32)).astype(BF)
+        copies.append(pltpu.make_async_copy(out_ref.at[f], lat_ref.at[f], sem.at[f]))
+        copies[-1].start()
     for c in copies:
         c.wait()
 
@@ -377,7 +405,7 @@
     return [pltpu.with_memory_space_constraint(x, pltpu.HBM) for x in xs]
 
 
-def call(body, name, ins, outs, scratch, flops, in_specs=None, out_specs=None, aliases=None):
+def call(body, ins, outs, scratch, flops, in_specs=None, out_specs=None, aliases=None):
     return pl.pallas_call(
         body,
         out_shape=outs,
@@ -387,7 +415,6 @@
         input_output_aliases=aliases or {},
         compiler_params=pltpu.CompilerParams(vmem_limit_bytes=LIMIT),
         cost_estimate=pl.CostEstimate(flops=flops, bytes_accessed=4 << 20, transcendentals=0),
-        name=name,
     )(*ins)
 
 
@@ -405,48 +432,54 @@
     fshape, ushape, x2shape, u2shape = (2, 2, 11, 64, 384), (4, 2, 23, 64, 256), (4, 21, 64, 256), (4, 4, 10, 32, 256)
     yshape, rshape = (2, 8, 2, 64, 128), (2, 10, 64, 256)
     xv, kfv, edge_dn, edge_up = call(
-        kernel_load, "load", (*keep(ok), *far(features, kf)),
+        kernel_load, (*keep(ok), *far(features, kf)),
         [res(4, 16, 128, 128), res(3, 3, 3, 128, 128), sds(4, 4, 128, 128), sds(4, 3, 128, 128)],
         [pltpu.SemaphoreType.DMA((4,))], 100_000_000, in_specs=[V] + [HBM] * 2,
     )
     top = lax.ppermute(edge_dn, "space", down)
     bot = lax.ppermute(edge_up, "space", up)
-    u, x2, w, ksv, g, kdv, bfv, bdv, bsv, f45, f23, f01 = call(
-        kernel_own, "own", (*keep(ok, xv, kfv), *far(ks, kd, bf.reshape(1, 128), bd.reshape(1, 256), bs.reshape(1, 256))),
+    u, x2, w, ksv, g, kdv, bfv, bdv, bsv, f45, f23, f01, part, red23, p01, u2 = call(
+        kernel_own, (*keep(ok, xv, kfv), *far(ks, kd, bf.reshape(1, 128), bd.reshape(1, 256), bs.reshape(1, 256))),
         [
             res(*ushape), res(*x2shape), res(4, 3, 2, 256, 256), res(3, 3, 3, 256, 256), res(2, 3, 3, 256, 256),
             res(3, 3, 128, 256), res(1, 128, dtype=F32), res(1, 256, dtype=F32), res(1, 256, dtype=F32),
-            *[res(*fshape)] * 3,
+            *[res(*fshape)] * 3, res(*rshape), res(*rshape), res(*rshape, dtype=F32), res(*u2shape),
         ],
-        [*wide, shift, pltpu.SemaphoreType.DMA((5,))], 8_000_000_000, in_specs=[V] * 3 + [HBM] * 5,
+        [*wide, shift, *half, pltpu.SemaphoreType.DMA((5,))], 8_000_000_000, in_specs=[V] * 3 + [HBM] * 5,
     )
     u, x2, _, part = call(
-        kernel_ahead, "ahead", (*keep(ok, u, x2, f45), top, bot, *keep(w, kdv)),
-        [res(*ushape), res(*x2shape), res(*fshape), sds(*rshape)],
-        [*wide, shift], 2_000_000_000, in_specs=[V] + [V] * 7, aliases={1: 0, 2: 1, 3: 2},
+        kernel_ahead, (*keep(ok, u, x2, f45, part), top, bot, *keep(w, kdv)),
+        [res(*ushape), res(*x2shape), res(*fshape), res(*rshape)],
+        [*wide, shift], 2_000_000_000, aliases={1: 0, 2: 1, 3: 2, 4: 3},
     )
     zpart = lax.ppermute(part, "tm", later)
     _, red23 = call(
-        kernel_late, "late", keep(ok, u, x2, f23, w, kdv, bfv, bdv), [res(*fshape), res(*rshape)],
-        [shift], 2_500_000_000, in_specs=[V] + [V] * 7, aliases={3: 0},
+        kernel_late, keep(ok, u, x2, f23, red23, w, kdv, bfv, bdv), [res(*fshape), res(*rshape)],
+        [shift], 2_500_000_000, aliases={3: 0, 4: 1},
     )
     u2, zl = call(
-        kernel_next, "next", keep(ok, red23, ksv, g), [res(*u2shape), sds(2, 8, 64, 256)],
-        [*half, VMEM(yshape, F32)], 2_000_000_000, in_specs=[V] + [V] * 3,
+        kernel_next, keep(ok, u2, red23, ksv, g), [res(*u2shape), sds(2, 8, 64, 256)],
+        [*half, VMEM(yshape, F32)], 2_000_000_000, aliases={1: 0},
     )
     zlat = lax.ppermute(zl, "tm", later)
-    _, red01 = call(
-        kernel_early, "early", (*keep(ok, u, x2, f01, w, kdv, bfv, bdv), zpart), [res(*fshape), res(*rshape)],
-        [shift], 2_500_000_000, in_specs=[V] + [V] * 8, aliases={3: 0},
-    )
-    u2, y = call(
-        kernel_same, "same", keep(ok, u2, red01, ksv, g), [res(*u2shape), res(*yshape, dtype=F32)],
-        half, 2_000_000_000, in_specs=[V] + [V] * 4, aliases={1: 0},
+    _, p01 = call(
+        kernel_early, keep(ok, u, x2, f01, p01, w, kdv, bfv, bdv), [res(*fshape), res(*rshape, dtype=F32)],
+        [shift], 2_500_000_000, aliases={3: 0, 4: 1},
+    )
+    u2, red01, y = call(
+        kernel_same, (*keep(ok, u2, p01), zpart, *keep(ksv, g)),
+        [res(*u2shape), res(*rshape), res(*yshape, dtype=F32)], half, 2_000_000_000, aliases={1: 0},
+    )
+    lat, y01 = call(
+        kernel_rest, keep(u2, red01, red23, y, ksv, g, bsv),
+        [sds(4, 8, 64, 256), res(2, 8, 64, 256, dtype=F32)],
+        [VMEM((4, 8, 2, 64, 128), F32), VMEM((2, 8, 64, 256), BF), pltpu.SemaphoreType.DMA((2 * 8 // STEP,))],
+        4_000_000_000, out_specs=[HBM, V],
     )
     (lat,) = call(
-        kernel_last, "last", (*keep(u2, red01, red23, y), zlat, *keep(ksv, g, bsv)), [sds(4, 8, 64, 256)],
-        [VMEM((4, 8, 2, 64, 128), F32), VMEM((4, 8, 64, 256), BF), pltpu.SemaphoreType.DMA((4 * 8 // STEP,))],
-        4_000_000_000, in_specs=[V] * 8, out_specs=[HBM],
+        kernel_last, (lat, *keep(y01), zlat), [sds(4, 8, 64, 256)],
+        [VMEM((2, 8, 64, 256), BF), pltpu.SemaphoreType.DMA((2,))],
+        100_000_000, in_specs=[HBM, V, V], out_specs=[HBM], aliases={0: 0},
     )
     return lat
 

time: 50.2 us -> 46.6 us (0.928)
  waiting for transfers between devices: 7.19 us -> 3.57 us
    ppermute x1, waiting for transfers between devices: 2.07 us -> 0.54 us  [on_device(): zlat = lax.ppermute(zl, 'tm', later)]
    ppermute x1, waiting for transfers between devices: 4.18 us -> 2.78 us  [on_device(): top = lax.ppermute(edge_dn, 'space', down)]
    ppermute x1, waiting for transfers between devices: 0.94 us -> 0.24 us  [on_device(): zpart = lax.ppermute(part, 'tm', later)]
    pallas_call x8 -> x9, Pallas kernels: 26.7 us -> 26.8 us  [call(): pl.pallas_call(body, out_shape=outs, in_specs=in_specs or [V] * len(ins),...]
  transfers between devices with their start and end apart: 4 -> 4, of which waited for: 3 -> 3; matrix products, arithmetic and copies ran while one was open for 0% -> 0% of each run, Pallas kernels for 37% -> 48%
where the time goes in v4:
time: 46.6 us; the launch traced here: 46.1 us
  Pallas kernels  26.8 us (58%)
  starting transfers between devices  15.4 us (33%)
  waiting for transfers between devices  3.57 us (8%)
    pallas_call x9, Pallas kernels, call(): pl.pallas_call(body, out_shape=outs, in_specs=in_specs or [V] * len(ins),...  26.8 us
    ppermute x1, starting transfers between devices, on_device(): zpart = lax.ppermute(part, 'tm', later)  6.63 us
    ppermute x1, starting transfers between devices, on_device(): bot = lax.ppermute(edge_up, 'space', up)  4.91 us
    ppermute x1, waiting for transfers between devices, on_device(): top = lax.ppermute(edge_dn, 'space', down)  2.78 us
    ppermute x1, starting transfers between devices, on_device(): top = lax.ppermute(edge_dn, 'space', down)  1.92 us
    ppermute x1, starting transfers between devices, on_device(): zlat = lax.ppermute(zl, 'tm', later)  1.92 us
  transfers between devices with their start and end apart: 4, of which 3 were waited for; matrix products, arithmetic and copies ran while one was open for 0% of the time, Pallas kernels for 48%

profile of v4, /device:TPU:103, one launch (start us, length us, event | category | flops | bytes accessed | tf_op | source)
XLA Modules:
  0.0 46.1 jit_solution(15136468405278041786)
XLA Ops:
  0.0 0.1 add_convert_fusion
  0.1 0.1 mul.2.ok_ref
  0.2 2.1 %shard_map.73 = (bf16[4,16,128,128]{3,2,1,0:T(8,128)(2,1)S(1)}, bf16[3,3,3,128,128]{4,3,2,1,0:T(8,128)(2,1)S(1)}, bf16[4,4,128,128]{3,2,1,0:T(8,128)(2,1)S(1)}, bf16[4,3,128,128]{3,2,1,0:T(8,128)(2,1)S(1)}) custom-call(f32[2,1,256]{2,1,0:T(1,128)S(1)} %mul.2.ok_ref, bf16[4,16,128,128]{3,2,1,0:T(8,128)(2,1)} %x_hbm.1, bf16[3,3,3,128,128]{4,3,2,1,0:T(8,128)(2,1)} %kf_hbm.1), custom_call_target="tpu_custom_call" | custom-call | flops 100000000 | bytes 4194304 | tf_op jit(solution)/shard_map/pallas_call | solution.py:409
  2.3 4.9 %collective-permute-start.1 = (bf16[4,3,128,128]{3,2,1,0:T(8,128)(2,1)S(1)}, bf16[4,3,128,128]{3,2,1,0:T(8,128)(2,1)S(1)}, u32[]{:S(2)}, u32[]{:S(2)}) collective-permute-start(bf16[4,3,128,128]{3,2,1,0:T(8,128)(2,1)S(1)} %get-tuple-element.45), channel_id=1, source_target_pairs={{1,0},{2,1},{3,2},{4,3},{5,4},{6,5},{7,6},{8,7},{9,8},{10,9},{11,1... | collective-permute-start | bytes 1179656 | tf_op jit(solution)/shard_map/ppermute | solution.py:440
  7.2 1.9 %collective-permute-start = (bf16[4,4,128,128]{3,2,1,0:T(8,128)(2,1)S(1)}, bf16[4,4,128,128]{3,2,1,0:T(8,128)(2,1)S(1)}, u32[]{:S(2)}, u32[]{:S(2)}) collective-permute-start(bf16[4,4,128,128]{3,2,1,0:T(8,128)(2,1)S(1)} %get-tuple-element.44), channel_id=1, source_target_pairs={{0,1},{1,2},{2,3},{3,4},{4,5},{5,6},{6,7},{7,8},{8,9},{9,10},{10,1... | collective-permute-start | bytes 1572872 | tf_op jit(solution)/shard_map/ppermute | solution.py:439
  9.1 11.8 %shard_map.74 = (bf16[4,2,23,64,256]{4,3,2,1,0:T(8,128)(2,1)S(1)}, bf16[4,21,64,256]{3,2,1,0:T(8,128)(2,1)S(1)}, bf16[4,3,2,256,256]{4,3,2,1,0:T(8,128)(2,1)S(1)...) custom-call(f32[2,1,256]{2,1,0:T(1,128)S(1)} %mul.2.ok_ref, ...), custom_call_target="tpu_custom_call" | custom-call | flops 8000000000 | bytes 4194304 | tf_op jit(solution)/shard_map/pallas_call | solution.py:409
  20.9 0.0 collective-permute-done.1.bot_ref
  20.9 2.8 %collective-permute-done.top_ref = bf16[4,4,128,128]{3,2,1,0:T(8,128)(2,1)S(1)} collective-permute-done((bf16[4,4,128,128]{3,2,1,0:T(8,128)(2,1)S(1)}, bf16[4,4,128,128]{3,2,1,0:T(8,128)(2,1)S(1)}, u32[]{:S(2)}, u32[]{:S(2)}) %collective-permute-start) | collective-permute-done | bytes 524320 | tf_op jit(solution)/shard_map/ppermute | solution.py:439
  23.7 1.8 %shard_map.75 = (bf16[4,2,23,64,256]{4,3,2,1,0:T(8,128)(2,1)S(1)}, bf16[4,21,64,256]{3,2,1,0:T(8,128)(2,1)S(1)}, bf16[2,2,11,64,384]{4,3,2,1,0:T(8,128)(2,1)S(1)}, bf16[2,10,64,256]{3,2,1,0:T(8,128)(2,1)S(1)}) custom-call(f32[2,1,256]{2,1,0:T(1,128)S(1)} %mul.2.ok_ref, ...), custom_call_target="tpu_custom_call", output_to_operand_aliasing={{0}: (1, {}), {1}: (2, {}), {2}: (3, {}), {3}: (4, {})} | custom-call | flops 2000000000 | bytes 4194304 | tf_op jit(solution)/shard_map/pallas_call | solution.py:409
  25.5 6.6 %collective-permute-start.2 = (bf16[2,10,64,256]{3,2,1,0:T(8,128)(2,1)S(1)}, bf16[2,10,64,256]{3,2,1,0:T(8,128)(2,1)S(1)}, u32[]{:S(2)}, u32[]{:S(2)}) collective-permute-start(bf16[2,10,64,256]{3,2,1,0:T(8,128)(2,1)S(1)} %get-tuple-element.61), channel_id=1, source_target_pairs={{0,16},{16,32},{32,48},{48,64},{64,80},{80,96},{96,112},{112,128},... | collective-permute-start | bytes 1966088 | tf_op jit(solution)/shard_map/ppermute | solution.py:455
  32.1 2.1 %shard_map.76 = (bf16[2,2,11,64,384]{4,3,2,1,0:T(8,128)(2,1)S(1)}, bf16[2,10,64,256]{3,2,1,0:T(8,128)(2,1)S(1)}) custom-call(f32[2,1,256]{2,1,0:T(1,128)S(1)} %mul.2.ok_ref, bf16[4,2,23,64,256]{4,3,2,1,0:T(8,128)(2,1)S(1)} %get-tuple-element.48.u_ref, ...), custom_call_target="tpu_custom_call", output_to_operand_aliasing={{0}: (3, {}), {1}: (4, {})} | custom-call | flops 2500000000 | bytes 4194304 | tf_op jit(solution)/shard_map/pallas_call | solution.py:409
  34.3 1.6 %shard_map.77 = (bf16[4,4,10,32,256]{4,3,2,1,0:T(8,128)(2,1)S(1)}, bf16[2,8,64,256]{3,2,1,0:T(8,128)(2,1)S(1)}) custom-call(f32[2,1,256]{2,1,0:T(1,128)S(1)} %mul.2.ok_ref, bf16[4,4,10,32,256]{4,3,2,1,0:T(8,128)(2,1)S(1)} %get-tuple-element.39.u_in, ...), custom_call_target="tpu_custom_call", output_to_operand_aliasing={{0}: (1, {})} | custom-call | flops 2000000000 | bytes 4194304 | tf_op jit(solution)/shard_map/pallas_call | solution.py:409
  35.9 1.9 %collective-permute-start.3 = (bf16[2,8,64,256]{3,2,1,0:T(8,128)(2,1)S(1)}, bf16[2,8,64,256]{3,2,1,0:T(8,128)(2,1)S(1)}, u32[]{:S(2)}, u32[]{:S(2)}) collective-permute-start(bf16[2,8,64,256]{3,2,1,0:T(8,128)(2,1)S(1)} %get-tuple-element.68), channel_id=1, source_target_pairs={{0,16},{16,32},{32,48},{48,64},{64,80},{80,96},{96,112},{112,128},... | collective-permute-start | bytes 1572872 | tf_op jit(solution)/shard_map/ppermute | solution.py:464
  37.8 1.4 %shard_map.78 = (bf16[2,2,11,64,384]{4,3,2,1,0:T(8,128)(2,1)S(1)}, f32[2,10,64,256]{3,2,1,0:T(8,128)S(1)}) custom-call(f32[2,1,256]{2,1,0:T(1,128)S(1)} %mul.2.ok_ref, bf16[4,2,23,64,256]{4,3,2,1,0:T(8,128)(2,1)S(1)} %get-tuple-element.48.u_ref, bf16[4,21,64,256]{3,2,1,0:T(8,128)(2,1)S(1)} %get-tuple-element.49.x2_ref, ...), custom_call_target="tpu_custom_call", output_to_operand_aliasing={{0}: (3, {}), {1}: (4, {})} | custom-call | flops 2500000000 | bytes 4194304 | tf_op jit(solution)/shard_map/pallas_call | solution.py:409
  39.2 0.2 collective-permute-done.2.z_ref
  39.5 1.7 %shard_map.79 = (bf16[4,4,10,32,256]{4,3,2,1,0:T(8,128)(2,1)S(1)}, bf16[2,10,64,256]{3,2,1,0:T(8,128)(2,1)S(1)}, f32[2,8,2,64,128]{4,3,2,1,0:T(8,128)S(1)}) custom-call(f32[2,1,256]{2,1,0:T(1,128)S(1)} %mul.2.ok_ref, bf16[4,4,10,32,256]{4,3,2,1,0:T(8,128)(2,1)S(1)} %get-tuple-element.57.u_in, ...), custom_call_target="tpu_custom_call", output_to_operand_aliasing={{0}: (1, {})} | custom-call | flops 2000000000 | bytes 4194304 | tf_op jit(solution)/shard_map/pallas_call | solution.py:409
  41.2 3.4 %shard_map.80 = (bf16[4,8,64,256]{3,2,1,0:T(8,128)(2,1)}, f32[2,8,64,256]{3,2,1,0:T(8,128)S(1)}) custom-call(bf16[4,4,10,32,256]{4,3,2,1,0:T(8,128)(2,1)S(1)} %get-tuple-element.62.u_ref, bf16[2,10,64,256]{3,2,1,0:T(8,128)(2,1)S(1)} %get-tuple-element.63.red01_ref, bf16[2,10,64,256]{3,2,1,0:T(8,128)(2,1)S(1)} %get-tuple-element.54.red_ref.red23_ref, ...), custom_call_target="tpu_custom_call" | custom-call | flops 4000000000 | bytes 4194304 | tf_op jit(solution)/shard_map/pallas_call | solution.py:409
  44.5 0.5 %collective-permute-done.3.zl_ref = bf16[2,8,64,256]{3,2,1,0:T(8,128)(2,1)S(1)} collective-permute-done((bf16[2,8,64,256]{3,2,1,0:T(8,128)(2,1)S(1)}, bf16[2,8,64,256]{3,2,1,0:T(8,128)(2,1)S(1)}, u32[]{:S(2)}, u32[]{:S(2)}) %collective-permute-start.3) | collective-permute-done | bytes 524320 | tf_op jit(solution)/shard_map/ppermute | solution.py:464
  45.1 0.9 %shard_map.81 = bf16[4,8,64,256]{3,2,1,0:T(8,128)(2,1)} custom-call(bf16[4,8,64,256]{3,2,1,0:T(8,128)(2,1)} %get-tuple-element.66.lat_in, f32[2,8,64,256]{3,2,1,0:T(8,128)S(1)} %get-tuple-element.67.y_ref, bf16[2,8,64,256]{3,2,1,0:T(8,128)(2,1)S(1)} %collective-permute-done.3.zl_ref), custom_call_target="tpu_custom_call", output_to_operand_aliasing={{}: (0, {})} | custom-call | flops 100000000 | bytes 4194304 | tf_op jit(solution)/shard_map/pallas_call | solution.py:409
Async XLA Ops:
  2.3 18.7 %collective-permute-start.1 = (bf16[4,3,128,128]{3,2,1,0:T(8,128)(2,1)S(1)}, bf16[4,3,128,128]{3,2,1,0:T(8,128)(2,1)S(1)}, u32[]{:S(2)}, u32[]{:S(2)}) collective-permute-start(bf16[4,3,128,128]{3,2,1,0:T(8,128)(2,1)S(1)} %get-tuple-element.45), channel_id=1, source_target_pairs={{1,0},{2,1},{3,2},{4,3},{5,4},{6,5},{7,6},{8,7},{9,8},{10,9},{11,1... | collective-permute-start | bytes 1179656 | tf_op jit(solution)/shard_map/ppermute | solution.py:440
  7.2 16.5 %collective-permute-start = (bf16[4,4,128,128]{3,2,1,0:T(8,128)(2,1)S(1)}, bf16[4,4,128,128]{3,2,1,0:T(8,128)(2,1)S(1)}, u32[]{:S(2)}, u32[]{:S(2)}) collective-permute-start(bf16[4,4,128,128]{3,2,1,0:T(8,128)(2,1)S(1)} %get-tuple-element.44), channel_id=1, source_target_pairs={{0,1},{1,2},{2,3},{3,4},{4,5},{5,6},{6,7},{7,8},{8,9},{9,10},{10,1... | collective-permute-start | bytes 1572872 | tf_op jit(solution)/shard_map/ppermute | solution.py:439
  25.5 14.0 %collective-permute-start.2 = (bf16[2,10,64,256]{3,2,1,0:T(8,128)(2,1)S(1)}, bf16[2,10,64,256]{3,2,1,0:T(8,128)(2,1)S(1)}, u32[]{:S(2)}, u32[]{:S(2)}) collective-permute-start(bf16[2,10,64,256]{3,2,1,0:T(8,128)(2,1)S(1)} %get-tuple-element.61), channel_id=1, source_target_pairs={{0,16},{16,32},{32,48},{48,64},{64,80},{80,96},{96,112},{112,128},... | collective-permute-start | bytes 1966088 | tf_op jit(solution)/shard_map/ppermute | solution.py:455
  35.9 9.2 %collective-permute-start.3 = (bf16[2,8,64,256]{3,2,1,0:T(8,128)(2,1)S(1)}, bf16[2,8,64,256]{3,2,1,0:T(8,128)(2,1)S(1)}, u32[]{:S(2)}, u32[]{:S(2)}) collective-permute-start(bf16[2,8,64,256]{3,2,1,0:T(8,128)(2,1)S(1)} %get-tuple-element.68), channel_id=1, source_target_pairs={{0,16},{16,32},{32,48},{48,64},{64,80},{80,96},{96,112},{112,128},... | collective-permute-start | bytes 1572872 | tf_op jit(solution)/shard_map/ppermute | solution.py:464

commit v5 on v4

--- a/solution.py
+++ b/solution.py
@@ -150,8 +150,8 @@
 
 def kernel_own(
     ok_ref, x_ref, kf_ref, ks_hbm, kd_hbm, bf_hbm, bd_hbm, bs_hbm,
-    u_ref, x2_ref, w_ref, ks_ref, g_ref, kd_ref, bf_ref, bd_ref, bs_ref, f45_ref, f23_ref, f01_ref,
-    part_ref, red_ref, p_ref, u2_ref, s_ref, q_ref, o_ref, s2_ref, q2_ref, sem,
+    u_ref, x2_ref, w_ref, ks_ref, g_ref, kd_ref, bf_ref, bd_ref, bs_ref, f45_ref, f23_ref,
+    part_ref, red_ref, u2_ref, s_ref, q_ref, o_ref, s2_ref, q2_ref, sem,
 ):
     pairs = ((bf_hbm, bf_ref), (ks_hbm, ks_ref), (kd_hbm, kd_ref), (bd_hbm, bd_ref), (bs_hbm, bs_ref))
     copies = [pltpu.make_async_copy(a, b, sem.at[n]) for n, (a, b) in enumerate(pairs)]
@@ -202,26 +202,22 @@
             for r in range(9, 16)
             for f in range(4)
         ],
-        12,
+        8,
     )
     gains = Pump([lambda i=i, j=j: weights(i, j) for i in range(3) for j in range(3)], 6)
     mids = Pump(
-        [lambda f=f, r=r: own_row(ok_ref, red_ref, f, r, u2_ref, s2_ref, q2_ref) for r in range(2, 8) for f in (2, 3)], 8
+        [lambda f=f, r=r: own_row(ok_ref, red_ref, f, r, u2_ref, s2_ref, q2_ref) for r in range(2, 8) for f in (2, 3)], 6
     )
     bias, parts = bf_ref[...], ((4, 7),)
     first_rows(u_ref, w_ref, f45_ref, o_ref, PAIR45, parts, None, None, None, rest)
     first_rows(u_ref, w_ref, f23_ref, o_ref, PAIR23, parts, None, x2_ref.at[2:4], bias, rest)
-    first_rows(u_ref, w_ref, f01_ref, o_ref, PAIR01, parts, None, x2_ref.at[0:2], bias, rest)
     parts = ((11, 7),)
     first_rows(u_ref, w_ref, f23_ref, o_ref, PAIR23, parts, None, x2_ref.at[2:4], bias, gains)
     for q, m, y in down_conv(f23_ref, kd_ref, INSIDE, gains):
         red_ref[q, m] = (y + bd_ref[...]).astype(BF)
     first_rows(u_ref, w_ref, f45_ref, o_ref, PAIR45, parts, None, None, None, mids)
-    first_rows(u_ref, w_ref, f01_ref, o_ref, PAIR01, parts, None, x2_ref.at[0:2], bias, mids)
-    for q, m, y in down_conv(f45_ref, kd_ref, INSIDE):
+    for q, m, y in down_conv(f45_ref, kd_ref, INSIDE, mids):
         part_ref[q, m] = y.astype(BF)
-    for q, m, y in down_conv(f01_ref, kd_ref, INSIDE):
-        p_ref[q, m] = y + bd_ref[...]
 
 
 def kernel_ahead(
@@ -251,10 +247,11 @@
         red_ref[q, m] = (y + bd_ref[...]).astype(BF)
 
 
-def kernel_early(ok_ref, u_ref, x2_ref, f_in, p_in, w_ref, kd_ref, bf_ref, bd_ref, f_ref, p_ref, o_ref):
+def kernel_early(ok_ref, u_ref, x2_ref, w_ref, kd_ref, bf_ref, bd_ref, p_ref, f_ref, o_ref):
     clear_shift(o_ref)
-    first_rows(u_ref, w_ref, f_ref, o_ref, PAIR01, EDGES, edge_masks(ok_ref), x2_ref.at[0:2], bf_ref[...])
-    for q, m, y in down_conv(f_ref, kd_ref, OUTSIDE):
+    for parts in (((0, 7),), ((7, 7),), ((14, 7),)):
+        first_rows(u_ref, w_ref, f_ref, o_ref, PAIR01, parts, edge_masks(ok_ref), x2_ref.at[0:2], bf_ref[...])
+    for q, m, y in down_conv(f_ref, kd_ref, ((0, 10),)):
         p_ref[q, m] = y + bd_ref[...]
 
 
@@ -438,12 +435,12 @@
     )
     top = lax.ppermute(edge_dn, "space", down)
     bot = lax.ppermute(edge_up, "space", up)
-    u, x2, w, ksv, g, kdv, bfv, bdv, bsv, f45, f23, f01, part, red23, p01, u2 = call(
+    u, x2, w, ksv, g, kdv, bfv, bdv, bsv, f45, f23, part, red23, u2 = call(
         kernel_own, (*keep(ok, xv, kfv), *far(ks, kd, bf.reshape(1, 128), bd.reshape(1, 256), bs.reshape(1, 256))),
         [
             res(*ushape), res(*x2shape), res(4, 3, 2, 256, 256), res(3, 3, 3, 256, 256), res(2, 3, 3, 256, 256),
             res(3, 3, 128, 256), res(1, 128, dtype=F32), res(1, 256, dtype=F32), res(1, 256, dtype=F32),
-            *[res(*fshape)] * 3, res(*rshape), res(*rshape), res(*rshape, dtype=F32), res(*u2shape),
+            *[res(*fshape)] * 2, res(*rshape), res(*rshape), res(*u2shape),
         ],
         [*wide, shift, *half, pltpu.SemaphoreType.DMA((5,))], 8_000_000_000, in_specs=[V] * 3 + [HBM] * 5,
     )
@@ -462,9 +459,9 @@
         [*half, VMEM(yshape, F32)], 2_000_000_000, aliases={1: 0},
     )
     zlat = lax.ppermute(zl, "tm", later)
-    _, p01 = call(
-        kernel_early, keep(ok, u, x2, f01, p01, w, kdv, bfv, bdv), [res(*fshape), res(*rshape, dtype=F32)],
-        [shift], 2_500_000_000, aliases={3: 0, 4: 1},
+    (p01,) = call(
+        kernel_early, keep(ok, u, x2, w, kdv, bfv, bdv), [res(*rshape, dtype=F32)],
+        [VMEM(fshape, BF), shift], 4_000_000_000,
     )
     u2, red01, y = call(
         kernel_same, (*keep(ok, u2, p01), zpart, *keep(ksv, g)),

time: 46.6 us -> 47.4 us (1.017)
  waiting for transfers between devices: 3.57 us -> 4.84 us
    ppermute x1, waiting for transfers between devices: 2.78 us -> 4.83 us  [on_device(): top = lax.ppermute(edge_dn, 'space', down)]
    ppermute x1, waiting for transfers between devices: 0.54 us -> 0.01 us  [on_device(): zlat = lax.ppermute(zl, 'tm', later)]
  transfers between devices with their start and end apart: 4 -> 4, of which waited for: 3 -> 1; matrix products, arithmetic and copies ran while one was open for 0% -> 0% of each run, Pallas kernels for 48% -> 46%
where the time goes in v5:
time: 47.4 us; the launch traced here: 47.2 us
  Pallas kernels  26.6 us (56%)
  starting transfers between devices  15.4 us (32%)
  waiting for transfers between devices  4.84 us (10%)
    pallas_call x9, Pallas kernels, call(): pl.pallas_call(body, out_shape=outs, in_specs=in_specs or [V] * len(ins),...  26.6 us
    ppermute x1, starting transfers between devices, on_device(): zpart = lax.ppermute(part, 'tm', later)  6.45 us
    ppermute x1, starting transfers between devices, on_device(): bot = lax.ppermute(edge_up, 'space', up)  4.91 us
    ppermute x1, waiting for transfers between devices, on_device(): top = lax.ppermute(edge_dn, 'space', down)  4.83 us
    ppermute x1, starting transfers between devices, on_device(): zlat = lax.ppermute(zl, 'tm', later)  2.1 us
    ppermute x1, starting transfers between devices, on_device(): top = lax.ppermute(edge_dn, 'space', down)  1.92 us
  transfers between devices with their start and end apart: 4, of which 1 were waited for; matrix products, arithmetic and copies ran while one was open for 0% of the time, Pallas kernels for 46%

profile of v5, /device:TPU:103, one launch (start us, length us, event | category | flops | bytes accessed | tf_op | source)
XLA Modules:
  0.0 47.2 jit_solution(16162129727350696963)
XLA Ops:
  0.0 0.1 add_convert_fusion
  0.1 0.1 mul.2.ok_ref
  0.2 2.1 %shard_map.73 = (bf16[4,16,128,128]{3,2,1,0:T(8,128)(2,1)S(1)}, bf16[3,3,3,128,128]{4,3,2,1,0:T(8,128)(2,1)S(1)}, bf16[4,4,128,128]{3,2,1,0:T(8,128)(2,1)S(1)}, bf16[4,3,128,128]{3,2,1,0:T(8,128)(2,1)S(1)}) custom-call(f32[2,1,256]{2,1,0:T(1,128)S(1)} %mul.2.ok_ref, bf16[4,16,128,128]{3,2,1,0:T(8,128)(2,1)} %x_hbm.1, bf16[3,3,3,128,128]{4,3,2,1,0:T(8,128)(2,1)} %kf_hbm.1), custom_call_target="tpu_custom_call" | custom-call | flops 100000000 | bytes 4194304 | tf_op jit(solution)/shard_map/pallas_call | solution.py:406
  2.3 4.9 %collective-permute-start.1 = (bf16[4,3,128,128]{3,2,1,0:T(8,128)(2,1)S(1)}, bf16[4,3,128,128]{3,2,1,0:T(8,128)(2,1)S(1)}, u32[]{:S(2)}, u32[]{:S(2)}) collective-permute-start(bf16[4,3,128,128]{3,2,1,0:T(8,128)(2,1)S(1)} %get-tuple-element.42), channel_id=1, source_target_pairs={{1,0},{2,1},{3,2},{4,3},{5,4},{6,5},{7,6},{8,7},{9,8},{10,9},{11,1... | collective-permute-start | bytes 1179656 | tf_op jit(solution)/shard_map/ppermute | solution.py:437
  7.2 1.9 %collective-permute-start = (bf16[4,4,128,128]{3,2,1,0:T(8,128)(2,1)S(1)}, bf16[4,4,128,128]{3,2,1,0:T(8,128)(2,1)S(1)}, u32[]{:S(2)}, u32[]{:S(2)}) collective-permute-start(bf16[4,4,128,128]{3,2,1,0:T(8,128)(2,1)S(1)} %get-tuple-element.41), channel_id=1, source_target_pairs={{0,1},{1,2},{2,3},{3,4},{4,5},{5,6},{6,7},{7,8},{8,9},{9,10},{10,1... | collective-permute-start | bytes 1572872 | tf_op jit(solution)/shard_map/ppermute | solution.py:436
  9.1 9.8 %shard_map.74 = (bf16[4,2,23,64,256]{4,3,2,1,0:T(8,128)(2,1)S(1)}, bf16[4,21,64,256]{3,2,1,0:T(8,128)(2,1)S(1)}, bf16[4,3,2,256,256]{4,3,2,1,0:T(8,128)(2,1)S(1)...) custom-call(f32[2,1,256]{2,1,0:T(1,128)S(1)} %mul.2.ok_ref, ...), custom_call_target="tpu_custom_call" | custom-call | flops 8000000000 | bytes 4194304 | tf_op jit(solution)/shard_map/pallas_call | solution.py:406
  18.9 0.0 collective-permute-done.1.bot_ref
  18.9 4.8 %collective-permute-done.top_ref = bf16[4,4,128,128]{3,2,1,0:T(8,128)(2,1)S(1)} collective-permute-done((bf16[4,4,128,128]{3,2,1,0:T(8,128)(2,1)S(1)}, bf16[4,4,128,128]{3,2,1,0:T(8,128)(2,1)S(1)}, u32[]{:S(2)}, u32[]{:S(2)}) %collective-permute-start) | collective-permute-done | bytes 524320 | tf_op jit(solution)/shard_map/ppermute | solution.py:436
  23.7 1.8 %shard_map.75 = (bf16[4,2,23,64,256]{4,3,2,1,0:T(8,128)(2,1)S(1)}, bf16[4,21,64,256]{3,2,1,0:T(8,128)(2,1)S(1)}, bf16[2,2,11,64,384]{4,3,2,1,0:T(8,128)(2,1)S(1)}, bf16[2,10,64,256]{3,2,1,0:T(8,128)(2,1)S(1)}) custom-call(f32[2,1,256]{2,1,0:T(1,128)S(1)} %mul.2.ok_ref, ...), custom_call_target="tpu_custom_call", output_to_operand_aliasing={{0}: (1, {}), {1}: (2, {}), {2}: (3, {}), {3}: (4, {})} | custom-call | flops 2000000000 | bytes 4194304 | tf_op jit(solution)/shard_map/pallas_call | solution.py:406
  25.5 6.5 %collective-permute-start.2 = (bf16[2,10,64,256]{3,2,1,0:T(8,128)(2,1)S(1)}, bf16[2,10,64,256]{3,2,1,0:T(8,128)(2,1)S(1)}, u32[]{:S(2)}, u32[]{:S(2)}) collective-permute-start(bf16[2,10,64,256]{3,2,1,0:T(8,128)(2,1)S(1)} %get-tuple-element.55), channel_id=1, source_target_pairs={{0,16},{16,32},{32,48},{48,64},{64,80},{80,96},{96,112},{112,128},... | collective-permute-start | bytes 1966088 | tf_op jit(solution)/shard_map/ppermute | solution.py:452
  32.0 2.1 %shard_map.76 = (bf16[2,2,11,64,384]{4,3,2,1,0:T(8,128)(2,1)S(1)}, bf16[2,10,64,256]{3,2,1,0:T(8,128)(2,1)S(1)}) custom-call(f32[2,1,256]{2,1,0:T(1,128)S(1)} %mul.2.ok_ref, bf16[4,2,23,64,256]{4,3,2,1,0:T(8,128)(2,1)S(1)} %get-tuple-element.45.u_ref, ...), custom_call_target="tpu_custom_call", output_to_operand_aliasing={{0}: (3, {}), {1}: (4, {})} | custom-call | flops 2500000000 | bytes 4194304 | tf_op jit(solution)/shard_map/pallas_call | solution.py:406
  34.1 1.6 %shard_map.77 = (bf16[4,4,10,32,256]{4,3,2,1,0:T(8,128)(2,1)S(1)}, bf16[2,8,64,256]{3,2,1,0:T(8,128)(2,1)S(1)}) custom-call(f32[2,1,256]{2,1,0:T(1,128)S(1)} %mul.2.ok_ref, bf16[4,4,10,32,256]{4,3,2,1,0:T(8,128)(2,1)S(1)} %get-tuple-element.36.u_in, ...), custom_call_target="tpu_custom_call", output_to_operand_aliasing={{0}: (1, {})} | custom-call | flops 2000000000 | bytes 4194304 | tf_op jit(solution)/shard_map/pallas_call | solution.py:406
  35.7 2.1 %collective-permute-start.3 = (bf16[2,8,64,256]{3,2,1,0:T(8,128)(2,1)S(1)}, bf16[2,8,64,256]{3,2,1,0:T(8,128)(2,1)S(1)}, u32[]{:S(2)}, u32[]{:S(2)}) collective-permute-start(bf16[2,8,64,256]{3,2,1,0:T(8,128)(2,1)S(1)} %get-tuple-element.62), channel_id=1, source_target_pairs={{0,16},{16,32},{32,48},{48,64},{64,80},{80,96},{96,112},{112,128},... | collective-permute-start | bytes 1572872 | tf_op jit(solution)/shard_map/ppermute | solution.py:461
  37.8 3.3 %shard_map.78.p_ref = f32[2,10,64,256]{3,2,1,0:T(8,128)S(1)} custom-call(f32[2,1,256]{2,1,0:T(1,128)S(1)} %mul.2.ok_ref, bf16[4,2,23,64,256]{4,3,2,1,0:T(8,128)(2,1)S(1)} %get-tuple-element.45.u_ref, bf16[4,21,64,256]{3,2,1,0:T(8,128)(2,1)S(1)} %get-tuple-element.46.x2_ref, bf16[4,3,2,256,256]{4,3,2,1,0:T(8,128)(2,1)S(1)} %get-tuple-element.43.w_ref, ...), custom_call_target="tpu_custom_call" | custom-call | flops 4000000000 | bytes 4194304 | tf_op jit(solution)/shard_map/pallas_call | solution.py:406
  41.1 0.0 collective-permute-done.2.z_ref
  41.1 1.7 %shard_map.79 = (bf16[4,4,10,32,256]{4,3,2,1,0:T(8,128)(2,1)S(1)}, bf16[2,10,64,256]{3,2,1,0:T(8,128)(2,1)S(1)}, f32[2,8,2,64,128]{4,3,2,1,0:T(8,128)S(1)}) custom-call(f32[2,1,256]{2,1,0:T(1,128)S(1)} %mul.2.ok_ref, bf16[4,4,10,32,256]{4,3,2,1,0:T(8,128)(2,1)S(1)} %get-tuple-element.54.u_in, ...), custom_call_target="tpu_custom_call", output_to_operand_aliasing={{0}: (1, {})} | custom-call | flops 2000000000 | bytes 4194304 | tf_op jit(solution)/shard_map/pallas_call | solution.py:406
  42.8 3.4 %shard_map.80 = (bf16[4,8,64,256]{3,2,1,0:T(8,128)(2,1)}, f32[2,8,64,256]{3,2,1,0:T(8,128)S(1)}) custom-call(bf16[4,4,10,32,256]{4,3,2,1,0:T(8,128)(2,1)S(1)} %get-tuple-element.56.u_ref, bf16[2,10,64,256]{3,2,1,0:T(8,128)(2,1)S(1)} %get-tuple-element.57.red01_ref, bf16[2,10,64,256]{3,2,1,0:T(8,128)(2,1)S(1)} %get-tuple-element.51.red_ref.red23_ref, ...), custom_call_target="tpu_custom_call" | custom-call | flops 4000000000 | bytes 4194304 | tf_op jit(solution)/shard_map/pallas_call | solution.py:406
  46.2 0.0 collective-permute-done.3.zl_ref
  46.2 0.9 %shard_map.81 = bf16[4,8,64,256]{3,2,1,0:T(8,128)(2,1)} custom-call(bf16[4,8,64,256]{3,2,1,0:T(8,128)(2,1)} %get-tuple-element.60.lat_in, f32[2,8,64,256]{3,2,1,0:T(8,128)S(1)} %get-tuple-element.61.y_ref, bf16[2,8,64,256]{3,2,1,0:T(8,128)(2,1)S(1)} %collective-permute-done.3.zl_ref), custom_call_target="tpu_custom_call", output_to_operand_aliasing={{}: (0, {})} | custom-call | flops 100000000 | bytes 4194304 | tf_op jit(solution)/shard_map/pallas_call | solution.py:406
Async XLA Ops:
  2.3 16.6 %collective-permute-start.1 = (bf16[4,3,128,128]{3,2,1,0:T(8,128)(2,1)S(1)}, bf16[4,3,128,128]{3,2,1,0:T(8,128)(2,1)S(1)}, u32[]{:S(2)}, u32[]{:S(2)}) collective-permute-start(bf16[4,3,128,128]{3,2,1,0:T(8,128)(2,1)S(1)} %get-tuple-element.42), channel_id=1, source_target_pairs={{1,0},{2,1},{3,2},{4,3},{5,4},{6,5},{7,6},{8,7},{9,8},{10,9},{11,1... | collective-permute-start | bytes 1179656 | tf_op jit(solution)/shard_map/ppermute | solution.py:437
  7.2 16.5 %collective-permute-start = (bf16[4,4,128,128]{3,2,1,0:T(8,128)(2,1)S(1)}, bf16[4,4,128,128]{3,2,1,0:T(8,128)(2,1)S(1)}, u32[]{:S(2)}, u32[]{:S(2)}) collective-permute-start(bf16[4,4,128,128]{3,2,1,0:T(8,128)(2,1)S(1)} %get-tuple-element.41), channel_id=1, source_target_pairs={{0,1},{1,2},{2,3},{3,4},{4,5},{5,6},{6,7},{7,8},{8,9},{9,10},{10,1... | collective-permute-start | bytes 1572872 | tf_op jit(solution)/shard_map/ppermute | solution.py:436
  25.5 15.6 %collective-permute-start.2 = (bf16[2,10,64,256]{3,2,1,0:T(8,128)(2,1)S(1)}, bf16[2,10,64,256]{3,2,1,0:T(8,128)(2,1)S(1)}, u32[]{:S(2)}, u32[]{:S(2)}) collective-permute-start(bf16[2,10,64,256]{3,2,1,0:T(8,128)(2,1)S(1)} %get-tuple-element.55), channel_id=1, source_target_pairs={{0,16},{16,32},{32,48},{48,64},{64,80},{80,96},{96,112},{112,128},... | collective-permute-start | bytes 1966088 | tf_op jit(solution)/shard_map/ppermute | solution.py:452
  35.7 10.5 %collective-permute-start.3 = (bf16[2,8,64,256]{3,2,1,0:T(8,128)(2,1)S(1)}, bf16[2,8,64,256]{3,2,1,0:T(8,128)(2,1)S(1)}, u32[]{:S(2)}, u32[]{:S(2)}) collective-permute-start(bf16[2,8,64,256]{3,2,1,0:T(8,128)(2,1)S(1)} %get-tuple-element.62), channel_id=1, source_target_pairs={{0,16},{16,32},{32,48},{48,64},{64,80},{80,96},{96,112},{112,128},... | collective-permute-start | bytes 1572872 | tf_op jit(solution)/shard_map/ppermute | solution.py:461

commit v6 on v5

--- a/solution.py
+++ b/solution.py
@@ -10,7 +10,7 @@
 F32 = jnp.float32
 VMEM = pltpu.VMEM
 LIMIT = 12 * 2**20
-STEP = 4
+STEP = 8
 
 
 def silu(v):
@@ -135,12 +135,11 @@
     return ok_ref[0, :, 0:128], ok_ref[1, :, 0:128]
 
 
-def kernel_load(ok_ref, x_hbm, kf_hbm, x_ref, kf_ref, top_ref, bot_ref, sem):
+def kernel_load(ok_ref, x_hbm, kf_hbm, kf_ref, top_ref, bot_ref, sem):
     copies = [
         pltpu.make_async_copy(x_hbm.at[:, 12:16], top_ref, sem.at[0]),
         pltpu.make_async_copy(x_hbm.at[:, 0:3], bot_ref, sem.at[1]),
-        pltpu.make_async_copy(x_hbm, x_ref, sem.at[2]),
-        pltpu.make_async_copy(kf_hbm, kf_ref, sem.at[3]),
+        pltpu.make_async_copy(kf_hbm, kf_ref, sem.at[2]),
     ]
     for c in copies:
         c.start()
@@ -149,13 +148,17 @@
 
 
 def kernel_own(
-    ok_ref, x_ref, kf_ref, ks_hbm, kd_hbm, bf_hbm, bd_hbm, bs_hbm,
+    ok_ref, kf_ref, x_hbm, ks_hbm, kd_hbm, bf_hbm, bd_hbm, bs_hbm,
     u_ref, x2_ref, w_ref, ks_ref, g_ref, kd_ref, bf_ref, bd_ref, bs_ref, f45_ref, f23_ref,
-    part_ref, red_ref, u2_ref, s_ref, q_ref, o_ref, s2_ref, q2_ref, sem,
+    part_ref, red_ref, u2_ref, x_ref, s_ref, q_ref, o_ref, s2_ref, q2_ref, sem,
 ):
     pairs = ((bf_hbm, bf_ref), (ks_hbm, ks_ref), (kd_hbm, kd_ref), (bd_hbm, bd_ref), (bs_hbm, bs_ref))
     copies = [pltpu.make_async_copy(a, b, sem.at[n]) for n, (a, b) in enumerate(pairs)]
-    for c in copies:
+    xs = [
+        pltpu.make_async_copy(x_hbm.at[:, 4 * n : 4 * n + 4], x_ref.at[:, 4 * n : 4 * n + 4], sem.at[5 + n])
+        for n in range(4)
+    ]
+    for c in xs + copies:
         c.start()
     clear_edges(s_ref)
     clear_edges(s2_ref)
@@ -165,8 +168,6 @@
         for f in range(4):
             prep_first(x_ref[f, r], f, r, u_ref, x2_ref, s_ref, q_ref)
         return carry
-
-    lax.fori_loop(0, 9, row, 0)
 
     def wrow(j, carry):
         zero = jnp.zeros((128, 128), BF)
@@ -188,6 +189,11 @@
         return carry
 
     lax.fori_loop(0, 3, wrow, 0)
+    xs[0].wait()
+    lax.fori_loop(0, 4, row, 0)
+    for c in xs[1:]:
+        c.wait()
+    lax.fori_loop(4, 9, row, 0)
     for c in copies:
         c.wait()
 
@@ -428,21 +434,21 @@
     shift = VMEM((2, 7, 72, 128), F32)
     fshape, ushape, x2shape, u2shape = (2, 2, 11, 64, 384), (4, 2, 23, 64, 256), (4, 21, 64, 256), (4, 4, 10, 32, 256)
     yshape, rshape = (2, 8, 2, 64, 128), (2, 10, 64, 256)
-    xv, kfv, edge_dn, edge_up = call(
+    kfv, edge_dn, edge_up = call(
         kernel_load, (*keep(ok), *far(features, kf)),
-        [res(4, 16, 128, 128), res(3, 3, 3, 128, 128), sds(4, 4, 128, 128), sds(4, 3, 128, 128)],
-        [pltpu.SemaphoreType.DMA((4,))], 100_000_000, in_specs=[V] + [HBM] * 2,
+        [res(3, 3, 3, 128, 128), sds(4, 4, 128, 128), sds(4, 3, 128, 128)],
+        [pltpu.SemaphoreType.DMA((3,))], 100_000_000, in_specs=[V] + [HBM] * 2,
     )
     top = lax.ppermute(edge_dn, "space", down)
     bot = lax.ppermute(edge_up, "space", up)
     u, x2, w, ksv, g, kdv, bfv, bdv, bsv, f45, f23, part, red23, u2 = call(
-        kernel_own, (*keep(ok, xv, kfv), *far(ks, kd, bf.reshape(1, 128), bd.reshape(1, 256), bs.reshape(1, 256))),
+        kernel_own, (*keep(ok, kfv), *far(features, ks, kd, bf.reshape(1, 128), bd.reshape(1, 256), bs.reshape(1, 256))),
         [
             res(*ushape), res(*x2shape), res(4, 3, 2, 256, 256), res(3, 3, 3, 256, 256), res(2, 3, 3, 256, 256),
             res(3, 3, 128, 256), res(1, 128, dtype=F32), res(1, 256, dtype=F32), res(1, 256, dtype=F32),
             *[res(*fshape)] * 2, res(*rshape), res(*rshape), res(*u2shape),
         ],
-        [*wide, shift, *half, pltpu.SemaphoreType.DMA((5,))], 8_000_000_000, in_specs=[V] * 3 + [HBM] * 5,
+        [VMEM((4, 16, 128, 128), BF), *wide, shift, *half, pltpu.SemaphoreType.DMA((9,))], 8_000_000_000, in_specs=[V] * 2 + [HBM] * 6,
     )
     u, x2, _, part = call(
         kernel_ahead, (*keep(ok, u, x2, f45, part), top, bot, *keep(w, kdv)),

time: 47.4 us -> 46.6 us (0.983)
  waiting for transfers between devices: 4.84 us -> 4.21 us
    ppermute x1, waiting for transfers between devices: 4.83 us -> 4.2 us  [on_device(): top = lax.ppermute(edge_dn, 'space', down)]
  transfers between devices with their start and end apart: 4 -> 4, of which waited for: 1 -> 1; matrix products, arithmetic and copies ran while one was open for 0% -> 0% of each run, Pallas kernels for 46% -> 48%
where the time goes in v6:
time: 46.6 us; the launch traced here: 46.4 us
  Pallas kernels  26.4 us (57%)
  starting transfers between devices  15.4 us (33%)
  waiting for transfers between devices  4.21 us (9%)
    pallas_call x9, Pallas kernels, call(): pl.pallas_call(body, out_shape=outs, in_specs=in_specs or [V] * len(ins),...  26.4 us
    ppermute x1, starting transfers between devices, on_device(): zpart = lax.ppermute(part, 'tm', later)  6.45 us
    ppermute x1, starting transfers between devices, on_device(): bot = lax.ppermute(edge_up, 'space', up)  4.91 us
    ppermute x1, waiting for transfers between devices, on_device(): top = lax.ppermute(edge_dn, 'space', down)  4.2 us
    ppermute x1, starting transfers between devices, on_device(): zlat = lax.ppermute(zl, 'tm', later)  2.1 us
    ppermute x1, starting transfers between devices, on_device(): top = lax.ppermute(edge_dn, 'space', down)  1.92 us
  transfers between devices with their start and end apart: 4, of which 1 were waited for; matrix products, arithmetic and copies ran while one was open for 0% of the time, Pallas kernels for 48%

profile of v6, /device:TPU:103, one launch (start us, length us, event | category | flops | bytes accessed | tf_op | source)
XLA Modules:
  0.0 46.4 jit_solution(18231395560124058865)
XLA Ops:
  0.0 0.1 add_convert_fusion
  0.1 0.1 mul.2.ok_ref
  0.2 1.5 %shard_map.73 = (bf16[3,3,3,128,128]{4,3,2,1,0:T(8,128)(2,1)S(1)}, bf16[4,4,128,128]{3,2,1,0:T(8,128)(2,1)S(1)}, bf16[4,3,128,128]{3,2,1,0:T(8,128)(2,1)S(1)}) custom-call(f32[2,1,256]{2,1,0:T(1,128)S(1)} %mul.2.ok_ref, bf16[4,16,128,128]{3,2,1,0:T(8,128)(2,1)} %x_hbm.3, bf16[3,3,3,128,128]{4,3,2,1,0:T(8,128)(2,1)} %kf_hbm.1), custom_call_target="tpu_custom_call" | custom-call | flops 100000000 | bytes 4194304 | tf_op jit(solution)/shard_map/pallas_call | solution.py:412
  1.6 4.9 %collective-permute-start.1 = (bf16[4,3,128,128]{3,2,1,0:T(8,128)(2,1)S(1)}, bf16[4,3,128,128]{3,2,1,0:T(8,128)(2,1)S(1)}, u32[]{:S(2)}, u32[]{:S(2)}) collective-permute-start(bf16[4,3,128,128]{3,2,1,0:T(8,128)(2,1)S(1)} %get-tuple-element.40), channel_id=1, source_target_pairs={{1,0},{2,1},{3,2},{4,3},{5,4},{6,5},{7,6},{8,7},{9,8},{10,9},{11,1... | collective-permute-start | bytes 1179656 | tf_op jit(solution)/shard_map/ppermute | solution.py:443
  6.5 1.9 %collective-permute-start = (bf16[4,4,128,128]{3,2,1,0:T(8,128)(2,1)S(1)}, bf16[4,4,128,128]{3,2,1,0:T(8,128)(2,1)S(1)}, u32[]{:S(2)}, u32[]{:S(2)}) collective-permute-start(bf16[4,4,128,128]{3,2,1,0:T(8,128)(2,1)S(1)} %get-tuple-element.39), channel_id=1, source_target_pairs={{0,1},{1,2},{2,3},{3,4},{4,5},{5,6},{6,7},{7,8},{8,9},{9,10},{10,1... | collective-permute-start | bytes 1572872 | tf_op jit(solution)/shard_map/ppermute | solution.py:442
  8.5 10.4 %shard_map.74 = (bf16[4,2,23,64,256]{4,3,2,1,0:T(8,128)(2,1)S(1)}, bf16[4,21,64,256]{3,2,1,0:T(8,128)(2,1)S(1)}, bf16[4,3,2,256,256]{4,3,2,1,0:T(8,128)(2,1)S(1)...) custom-call(f32[2,1,256]{2,1,0:T(1,128)S(1)} %mul.2.ok_ref, ...), custom_call_target="tpu_custom_call" | custom-call | flops 8000000000 | bytes 4194304 | tf_op jit(solution)/shard_map/pallas_call | solution.py:412
  18.9 0.0 collective-permute-done.1.bot_ref
  18.9 4.2 %collective-permute-done.top_ref = bf16[4,4,128,128]{3,2,1,0:T(8,128)(2,1)S(1)} collective-permute-done((bf16[4,4,128,128]{3,2,1,0:T(8,128)(2,1)S(1)}, bf16[4,4,128,128]{3,2,1,0:T(8,128)(2,1)S(1)}, u32[]{:S(2)}, u32[]{:S(2)}) %collective-permute-start) | collective-permute-done | bytes 524320 | tf_op jit(solution)/shard_map/ppermute | solution.py:442
  23.1 1.8 %shard_map.75 = (bf16[4,2,23,64,256]{4,3,2,1,0:T(8,128)(2,1)S(1)}, bf16[4,21,64,256]{3,2,1,0:T(8,128)(2,1)S(1)}, bf16[2,2,11,64,384]{4,3,2,1,0:T(8,128)(2,1)S(1)}, bf16[2,10,64,256]{3,2,1,0:T(8,128)(2,1)S(1)}) custom-call(f32[2,1,256]{2,1,0:T(1,128)S(1)} %mul.2.ok_ref, ...), custom_call_target="tpu_custom_call", output_to_operand_aliasing={{0}: (1, {}), {1}: (2, {}), {2}: (3, {}), {3}: (4, {})} | custom-call | flops 2000000000 | bytes 4194304 | tf_op jit(solution)/shard_map/pallas_call | solution.py:412
  24.9 6.5 %collective-permute-start.2 = (bf16[2,10,64,256]{3,2,1,0:T(8,128)(2,1)S(1)}, bf16[2,10,64,256]{3,2,1,0:T(8,128)(2,1)S(1)}, u32[]{:S(2)}, u32[]{:S(2)}) collective-permute-start(bf16[2,10,64,256]{3,2,1,0:T(8,128)(2,1)S(1)} %get-tuple-element.53), channel_id=1, source_target_pairs={{0,16},{16,32},{32,48},{48,64},{64,80},{80,96},{96,112},{112,128},... | collective-permute-start | bytes 1966088 | tf_op jit(solution)/shard_map/ppermute | solution.py:458
  31.3 2.1 %shard_map.76 = (bf16[2,2,11,64,384]{4,3,2,1,0:T(8,128)(2,1)S(1)}, bf16[2,10,64,256]{3,2,1,0:T(8,128)(2,1)S(1)}) custom-call(f32[2,1,256]{2,1,0:T(1,128)S(1)} %mul.2.ok_ref, bf16[4,2,23,64,256]{4,3,2,1,0:T(8,128)(2,1)S(1)} %get-tuple-element.43.u_ref, ...), custom_call_target="tpu_custom_call", output_to_operand_aliasing={{0}: (3, {}), {1}: (4, {})} | custom-call | flops 2500000000 | bytes 4194304 | tf_op jit(solution)/shard_map/pallas_call | solution.py:412
  33.5 1.6 %shard_map.77 = (bf16[4,4,10,32,256]{4,3,2,1,0:T(8,128)(2,1)S(1)}, bf16[2,8,64,256]{3,2,1,0:T(8,128)(2,1)S(1)}) custom-call(f32[2,1,256]{2,1,0:T(1,128)S(1)} %mul.2.ok_ref, bf16[4,4,10,32,256]{4,3,2,1,0:T(8,128)(2,1)S(1)} %get-tuple-element.34.u_in, ...), custom_call_target="tpu_custom_call", output_to_operand_aliasing={{0}: (1, {})} | custom-call | flops 2000000000 | bytes 4194304 | tf_op jit(solution)/shard_map/pallas_call | solution.py:412
  35.0 2.1 %collective-permute-start.3 = (bf16[2,8,64,256]{3,2,1,0:T(8,128)(2,1)S(1)}, bf16[2,8,64,256]{3,2,1,0:T(8,128)(2,1)S(1)}, u32[]{:S(2)}, u32[]{:S(2)}) collective-permute-start(bf16[2,8,64,256]{3,2,1,0:T(8,128)(2,1)S(1)} %get-tuple-element.60), channel_id=1, source_target_pairs={{0,16},{16,32},{32,48},{48,64},{64,80},{80,96},{96,112},{112,128},... | collective-permute-start | bytes 1572872 | tf_op jit(solution)/shard_map/ppermute | solution.py:467
  37.2 3.3 %shard_map.78.p_ref = f32[2,10,64,256]{3,2,1,0:T(8,128)S(1)} custom-call(f32[2,1,256]{2,1,0:T(1,128)S(1)} %mul.2.ok_ref, bf16[4,2,23,64,256]{4,3,2,1,0:T(8,128)(2,1)S(1)} %get-tuple-element.43.u_ref, bf16[4,21,64,256]{3,2,1,0:T(8,128)(2,1)S(1)} %get-tuple-element.44.x2_ref, bf16[4,3,2,256,256]{4,3,2,1,0:T(8,128)(2,1)S(1)} %get-tuple-element.41.w_ref, ...), custom_call_target="tpu_custom_call" | custom-call | flops 4000000000 | bytes 4194304 | tf_op jit(solution)/shard_map/pallas_call | solution.py:412
  40.5 0.0 collective-permute-done.2.z_ref
  40.5 1.7 %shard_map.79 = (bf16[4,4,10,32,256]{4,3,2,1,0:T(8,128)(2,1)S(1)}, bf16[2,10,64,256]{3,2,1,0:T(8,128)(2,1)S(1)}, f32[2,8,2,64,128]{4,3,2,1,0:T(8,128)S(1)}) custom-call(f32[2,1,256]{2,1,0:T(1,128)S(1)} %mul.2.ok_ref, bf16[4,4,10,32,256]{4,3,2,1,0:T(8,128)(2,1)S(1)} %get-tuple-element.52.u_in, ...), custom_call_target="tpu_custom_call", output_to_operand_aliasing={{0}: (1, {})} | custom-call | flops 2000000000 | bytes 4194304 | tf_op jit(solution)/shard_map/pallas_call | solution.py:412
  42.2 3.2 %shard_map.80 = (bf16[4,8,64,256]{3,2,1,0:T(8,128)(2,1)}, f32[2,8,64,256]{3,2,1,0:T(8,128)S(1)}) custom-call(bf16[4,4,10,32,256]{4,3,2,1,0:T(8,128)(2,1)S(1)} %get-tuple-element.54.u_ref, bf16[2,10,64,256]{3,2,1,0:T(8,128)(2,1)S(1)} %get-tuple-element.55.red01_ref, bf16[2,10,64,256]{3,2,1,0:T(8,128)(2,1)S(1)} %get-tuple-element.49.red_ref.red23_ref, ...), custom_call_target="tpu_custom_call" | custom-call | flops 4000000000 | bytes 4194304 | tf_op jit(solution)/shard_map/pallas_call | solution.py:412
  45.4 0.0 collective-permute-done.3.zl_ref
  45.4 0.9 %shard_map.81 = bf16[4,8,64,256]{3,2,1,0:T(8,128)(2,1)} custom-call(bf16[4,8,64,256]{3,2,1,0:T(8,128)(2,1)} %get-tuple-element.58.lat_in, f32[2,8,64,256]{3,2,1,0:T(8,128)S(1)} %get-tuple-element.59.y_ref, bf16[2,8,64,256]{3,2,1,0:T(8,128)(2,1)S(1)} %collective-permute-done.3.zl_ref), custom_call_target="tpu_custom_call", output_to_operand_aliasing={{}: (0, {})} | custom-call | flops 100000000 | bytes 4194304 | tf_op jit(solution)/shard_map/pallas_call | solution.py:412
Async XLA Ops:
  1.6 17.2 %collective-permute-start.1 = (bf16[4,3,128,128]{3,2,1,0:T(8,128)(2,1)S(1)}, bf16[4,3,128,128]{3,2,1,0:T(8,128)(2,1)S(1)}, u32[]{:S(2)}, u32[]{:S(2)}) collective-permute-start(bf16[4,3,128,128]{3,2,1,0:T(8,128)(2,1)S(1)} %get-tuple-element.40), channel_id=1, source_target_pairs={{1,0},{2,1},{3,2},{4,3},{5,4},{6,5},{7,6},{8,7},{9,8},{10,9},{11,1... | collective-permute-start | bytes 1179656 | tf_op jit(solution)/shard_map/ppermute | solution.py:443
  6.5 16.5 %collective-permute-start = (bf16[4,4,128,128]{3,2,1,0:T(8,128)(2,1)S(1)}, bf16[4,4,128,128]{3,2,1,0:T(8,128)(2,1)S(1)}, u32[]{:S(2)}, u32[]{:S(2)}) collective-permute-start(bf16[4,4,128,128]{3,2,1,0:T(8,128)(2,1)S(1)} %get-tuple-element.39), channel_id=1, source_target_pairs={{0,1},{1,2},{2,3},{3,4},{4,5},{5,6},{6,7},{7,8},{8,9},{9,10},{10,1... | collective-permute-start | bytes 1572872 | tf_op jit(solution)/shard_map/ppermute | solution.py:442
  24.9 15.6 %collective-permute-start.2 = (bf16[2,10,64,256]{3,2,1,0:T(8,128)(2,1)S(1)}, bf16[2,10,64,256]{3,2,1,0:T(8,128)(2,1)S(1)}, u32[]{:S(2)}, u32[]{:S(2)}) collective-permute-start(bf16[2,10,64,256]{3,2,1,0:T(8,128)(2,1)S(1)} %get-tuple-element.53), channel_id=1, source_target_pairs={{0,16},{16,32},{32,48},{48,64},{64,80},{80,96},{96,112},{112,128},... | collective-permute-start | bytes 1966088 | tf_op jit(solution)/shard_map/ppermute | solution.py:458
  35.0 10.3 %collective-permute-start.3 = (bf16[2,8,64,256]{3,2,1,0:T(8,128)(2,1)S(1)}, bf16[2,8,64,256]{3,2,1,0:T(8,128)(2,1)S(1)}, u32[]{:S(2)}, u32[]{:S(2)}) collective-permute-start(bf16[2,8,64,256]{3,2,1,0:T(8,128)(2,1)S(1)} %get-tuple-element.60), channel_id=1, source_target_pairs={{0,16},{16,32},{32,48},{48,64},{64,80},{80,96},{96,112},{112,128},... | collective-permute-start | bytes 1572872 | tf_op jit(solution)/shard_map/ppermute | solution.py:467
